TPU v7x, 32 devices: a whole 2x2x4 slice. The times are simulated.
32 devices in a mesh: ves: 4 (over x, core), shard: 8 (over z, y).
Axes of the slice: x: 2, y: 2, z: 4, core: 2. Of those that a mesh axis runs over, the one named last changes fastest.
Arguments:
- displacement: float32 [3, 8, 256, 128], P(None, 'ves', 'shard'), may hold values from -6 to 6
- tension: float32 [8], P('ves'), may hold values from 2 to 8
- bending: float32 [8], P('ves'), may hold values from 0.2 to 0.8
- offset: float32 [3, 8, 256, 128], P(None, 'ves', 'shard'), may hold values from 0 to 1
- owner: int32 [8, 256, 128], P('ves', 'shard'), may hold values from 0 to 31, as said below
- cell: int32 [8, 256, 128], P('ves', 'shard'), may hold values from 0 to 131071
- populations: float32 [64, 19, 256, 256], P(('ves', 'shard')), may hold values from 0 to 1, as said below
Outputs:
- membrane_force: float32 [3, 8, 256, 128], P(None, 'ves', 'shard')
- force_field: float32 [64, 3, 256, 256], P(('ves', 'shard'))
- new_populations: float32 [64, 19, 256, 256], P(('ves', 'shard'))
Inputs may be any that keep to these rules, and one draw needn't show every extreme that they name: The points of one device name any one owner at most 512 times, and some owner is named exactly 512 times by the points of every device. `populations`: entries are positive.
All inputs are finite; a program needn't handle non-finite values.
Results may differ from a plain program's by a relative error of at most 0.0061.
Values sent between devices are 32-bit elements; how exact they have to be, the bound alone decides.
A program may use at most 128 MiB of HBM per device.

v0:
```python
import math

import jax
import jax.numpy as jnp
from jax import lax
from jax.experimental import pallas as pl
from jax.experimental.pallas import tpu as pltpu
from jax.sharding import PartitionSpec as P


relax_time = 0.8
velocity_x = [0, 1, -1, 0, 0, 0, 1, -1, 0, 0, 0, 1, -1, 0, 0, 1, 1, -1, -1]
velocity_y = [0, 0, 0, 1, -1, 0, 0, 0, 1, -1, 0, 0, 0, 1, -1, 1, -1, 1, -1]
velocity_z = [1, 1, 1, 1, 1, -1, -1, -1, -1, -1, 0, 0, 0, 0, 0, 0, 0, 0, 0]
lattice_weights = [
    1.0 / 18,
    1.0 / 36,
    1.0 / 36,
    1.0 / 36,
    1.0 / 36,
    1.0 / 18,
    1.0 / 36,
    1.0 / 36,
    1.0 / 36,
    1.0 / 36,
    1.0 / 3,
    1.0 / 18,
    1.0 / 18,
    1.0 / 18,
    1.0 / 18,
    1.0 / 36,
    1.0 / 36,
    1.0 / 36,
    1.0 / 36,
]


def passed_along(value, axis, steps):
    count = lax.axis_size(axis)
    pairs = [(source, (source + steps) % count) for source in range(count)]
    return lax.ppermute(value, axis, pairs)


def with_halo(x, axis, dim, width):
    devices, length = (lax.axis_size(axis), x.shape[dim])
    up = [(i, i + 1) for i in range(devices - 1)]
    down = [(j, i) for i, j in up]
    last = lax.slice_in_dim(x, length - width, length, axis=dim)
    initial = lax.slice_in_dim(x, 0, width, axis=dim)
    before = lax.ppermute(last, axis, up)
    after = lax.ppermute(initial, axis, down)
    return jnp.concatenate([before, x, after], axis=dim)


def laplacian(padded):
    center = padded[:, :, 1:-1]
    return (
        padded[:, :, 2:]
        + padded[:, :, :-2]
        + jnp.roll(center, 1, 3)
        + jnp.roll(center, -1, 3)
        - 4.0 * center
    )


def membrane(displacement, tension, bending):
    padded = with_halo(displacement, "shard", 2, 2)
    wide_first = laplacian(padded)
    rows = wide_first.shape[2]
    place = lax.broadcasted_iota(jnp.int32, (1, 1, rows, 1), 2)
    index = lax.axis_index("shard")
    outside = ((place == 0) & (index == 0)) | (
        (place == rows - 1) & (index == lax.axis_size("shard") - 1)
    )
    wide_first = jnp.where(outside, 0.0, wide_first)
    second = laplacian(wide_first)
    first = wide_first[:, :, 1:-1]
    return tension[None, :, None, None] * first - bending[None, :, None, None] * second


WINDOW = 16
ROWS = 24
BLOCK = 256


HALF_PI = 0.5 * math.pi
COSINE = [(-1.0) ** n * HALF_PI ** (2 * n) / math.factorial(2 * n) for n in range(8)]
SINE = [(-1.0) ** n * HALF_PI ** (2 * n + 1) / math.factorial(2 * n + 1) for n in range(8)]


def weights(fraction):
    square = fraction * fraction
    c = jnp.full_like(square, COSINE[-1])
    s = jnp.full_like(square, SINE[-1])
    for n in range(6, -1, -1):
        c = c * square + COSINE[n]
        s = s * square + SINE[n]
    s = s * fraction
    return [0.25 * (1.0 - s), 0.25 * (1.0 + c), 0.25 * (1.0 + s), 0.25 * (1.0 - c)]


def bits(count):
    return (count - 1).bit_length()


def spread_list(starts, list_ref, acc, shift, planes, slab, ranges):
    width = acc.shape[2]
    row_id = lax.broadcasted_iota(jnp.int32, (ROWS, BLOCK), 0)
    y_id = lax.broadcasted_iota(jnp.int32, (width, BLOCK), 0)

    def pick(rel, parts):
        result = jnp.zeros(rel.shape, jnp.float32)
        for k in range(4):
            result = jnp.where(rel == k, parts[k], result)
        return result

    def window(w, offset):
        begin = starts[w] // BLOCK
        end = (starts[w + 1] + (BLOCK - 1)) // BLOCK
        base = w * WINDOW
        at_row = (w + offset) * WINDOW

        @pl.loop(begin, end)
        def _(b):
            at = pl.ds(pl.multiple_of(b * BLOCK, BLOCK), BLOCK)
            phi = weights(list_ref[3:6, at])
            key = list_ref[6:7, at].astype(jnp.int32)
            y = key & ((1 << bits(width)) - 1)
            plane = (key >> bits(width)) & ((1 << bits(slab)) - 1)
            x = (key >> (bits(width) + bits(slab))) - base
            x = jnp.where((x >= 0) & (x < WINDOW), x, 4 * ROWS)
            weight_x = pick(row_id - x, [phi[k][0:1] for k in range(4)])
            right = pick((y_id - (y - 1)) & (width - 1), [phi[k][1:2] for k in range(4)])
            lefts = []
            for q in planes:
                weight_z = pick(q + 1 + shift - plane, [phi[k][2:3] for k in range(4)])
                for c in range(3):
                    lefts.append((list_ref[c : c + 1, at] * weight_z) * weight_x)
            product = lax.dot_general(
                jnp.concatenate(lefts, 0).astype(jnp.bfloat16),
                right.astype(jnp.bfloat16),
                (((1,), (1,)), ((), ())),
                preferred_element_type=jnp.float32,
            )
            rows = pl.ds(pl.multiple_of(at_row, 8), ROWS)
            for n, q in enumerate(planes):
                for c in range(3):
                    i = n * 3 + c
                    acc[q * 3 + c, rows, :] += product[i * ROWS : (i + 1) * ROWS]

    for first, last, offset in ranges:

        @pl.loop(first, last)
        def _(w):
            window(w, offset)


VMEM = pl.BlockSpec(memory_space=pltpu.VMEM)
SMEM = pl.BlockSpec(memory_space=pltpu.SMEM)


def cost(flops):
    return pl.CostEstimate(flops=flops, bytes_accessed=4_000_000, transcendentals=0)


def starts_of(listed, windows):
    return listed[7, : windows + 1].astype(jnp.int32)


def spread_own(listed, slab, width):
    windows = width // WINDOW

    def kernel(starts, list_ref, acc):
        acc[...] = jnp.zeros_like(acc)
        spread_list(starts, list_ref, acc, 0, range(slab), slab, [(0, windows, 0)])

    return pl.pallas_call(
        kernel,
        out_shape=jax.ShapeDtypeStruct((slab * 3, width + ROWS - WINDOW, width), jnp.float32),
        in_specs=[SMEM, VMEM],
        out_specs=VMEM,
        name="spread_own",
        cost_estimate=cost(20_000_000_000),
    )(starts_of(listed, windows), listed)


ANY = pl.BlockSpec(memory_space=pl.ANY)
MIB = 1 << 20
LAG = 7
KEEP = 1.0 - 1.0 / relax_time
FORCING = 1.0 - 0.5 / relax_time


def collided(f, force, items):
    def along(vector, item, start=None):
        total = start
        for e, v in zip((velocity_x[item], velocity_y[item], velocity_z[item]), vector):
            if e == 0:
                continue
            if total is None:
                total = v if e > 0 else -v
            else:
                total = total + v if e > 0 else total - v
        return total

    def tree(values):
        while len(values) > 1:
            values = [
                values[i] + values[i + 1] if i + 1 < len(values) else values[i]
                for i in range(0, len(values), 2)
            ]
        return values[0]

    density = tree(list(f))
    inverse = 1.0 / density
    flow = []
    for axis, table in enumerate((velocity_x, velocity_y, velocity_z)):
        plus = tree([f[i] for i in range(19) if table[i] > 0])
        minus = tree([f[i] for i in range(19) if table[i] < 0])
        flow.append(((plus - minus) + 0.5 * force[axis]) * inverse)
    speed_sq = flow[0] * flow[0] + flow[1] * flow[1] + flow[2] * flow[2]
    work = flow[0] * force[0] + flow[1] * force[1] + flow[2] * force[2]
    scaled = density * (1.0 / relax_time)
    base = scaled - (1.5 * scaled) * speed_sq - (3.0 * FORCING) * work
    linear = 3.0 * scaled
    square = 4.5 * scaled
    pushed = [3.0 * FORCING * v for v in force]
    result = {}
    for item in items:
        cu = along(flow, item)
        if cu is None:
            bracket = base
        else:
            facing = along(pushed, item)
            bracket = base + facing + cu * (linear + square * cu + 3.0 * facing)
        result[item] = KEEP * f[item] + lattice_weights[item] * bracket
    return result


def spread_chunk(lists, total, carry, head, populations, field, first, last):
    below, above = lists
    slab, width = (populations.shape[0], populations.shape[2])
    windows = width // WINDOW
    opening, closing = (first == 0, last == windows)
    begin = 0 if opening else (first - 1) * WINDOW
    end = width if closing else (last - 1) * WINDOW
    n = end - begin
    span = n + ROWS
    planes = (slab - 1, 0)

    def kernel(s0, l0, s1, l1, total_ref, carry_ref, head_ref, pop_ref, field_in, *rest):
        low, high, carry_out, field_out, acc, pop, post, sems = rest
        del field_in
        copies = []

        def fetch(source, target):
            copy = pltpu.make_async_copy(source, target, sems.at[len(copies)])
            copy.start()
            copies.append(copy)

        got = 0
        if not opening:
            fetch(carry_ref, acc.at[:, 0:ROWS, :])
            got = ROWS
        stop = min(span, width + ROWS - WINDOW - begin)
        fetch(total_ref.at[:, begin + got : begin + stop, :], acc.at[:, got:stop, :])
        early = len(copies)
        for n_plane, plane in enumerate(planes):
            for x in range(0, 3):
                source, target, size = (
                    ((begin - 8) % width, 0, 8),
                    (begin, 8, n),
                    (end % width, n + 8, 8),
                )[x]
                fetch(
                    pop_ref.at[plane, :, source : source + size, :],
                    pop.at[n_plane, :, target : target + size, :],
                )
        for copy in copies[:early]:
            copy.wait()
        if closing:
            acc[:, stop:span, :] = jnp.zeros((slab * 3, span - stop, width), jnp.float32)
        moves = (first, last, 0 if opening else 1 - first)
        spread_list(s0, l0, acc, slab, (0, 1), slab, [moves])
        spread_list(s1, l1, acc, -slab, (slab - 1,), slab, [moves])
        if closing:
            acc[:, n : n + 16, :] += head_ref[:, 0:16, :]
        if opening:
            carry_out[:, ROWS : 2 * ROWS, :] = acc[:, 0:ROWS, :]
            carry_out[:, 0:ROWS, :] = acc[:, n : n + ROWS, :]
        elif not closing:
            carry_out[:, 0:ROWS, :] = acc[:, n : n + ROWS, :]
        else:
            carry_out[...] = jnp.zeros_like(carry_out)
        written = [
            pltpu.make_async_copy(
                acc.at[i, 8 : 8 + n, :],
                field_out.at[i // 3, i % 3, begin:end, :],
                sems.at[len(copies) + i],
            )
            for i in range(slab * 3)
        ]
        for copy in written:
            copy.start()
        for copy in copies[early:]:
            copy.wait()

        @pl.loop(0, (n + 16) // 8)
        def _(t):
            rows = pl.ds(pl.multiple_of(t * 8, 8), 8)
            for n_plane, plane in enumerate(planes):
                f = [pop[n_plane, i, rows, :] for i in range(19)]
                force = [acc[plane * 3 + c, rows, :] for c in range(3)]
                items = range(n_plane * 5, n_plane * 5 + 5)
                for i, value in collided(f, force, items).items():
                    post[i, rows, :] = value

        for target, begin_item in ((low, 0), (high, 5)):
            for i in range(5):
                item = begin_item + i
                at = 8 - velocity_x[item]
                value = post[item, at : at + n, :]
                if velocity_y[item]:
                    value = pltpu.roll(value, velocity_y[item] % width, 1)
                target[i] = value
        for copy in written:
            copy.wait()

    shape = jax.ShapeDtypeStruct
    return pl.pallas_call(
        kernel,
        out_shape=(
            shape((5, n, width), jnp.float32),
            shape((5, n, width), jnp.float32),
            shape((slab * 3, 2 * ROWS, width), jnp.float32),
            shape((slab, 3, width, width), jnp.float32),
        ),
        in_specs=[SMEM, VMEM, SMEM, VMEM, ANY, ANY, VMEM, ANY, ANY],
        out_specs=(VMEM, VMEM, VMEM, ANY),
        scratch_shapes=[
            pltpu.VMEM((slab * 3, span, width), jnp.float32),
            pltpu.VMEM((2, 19, n + 16, width), jnp.float32),
            pltpu.VMEM((10, n + 16, width), jnp.float32),
            pltpu.SemaphoreType.DMA((8 + slab * 3,)),
        ],
        input_output_aliases={} if field is None else {8: 3},
        compiler_params=pltpu.CompilerParams(vmem_limit_bytes=20 * MIB),
        cost_estimate=cost(8_000_000_000),
    )(
        starts_of(below, windows),
        below,
        starts_of(above, windows),
        above,
        total,
        jnp.zeros((slab * 3, ROWS, width), jnp.float32) if carry is None else carry[:, :ROWS],
        jnp.zeros((slab * 3, ROWS, width), jnp.float32) if head is None else head,
        populations,
        jnp.zeros((8, 128), jnp.float32) if field is None else field,
    )


def interior(populations, field):
    slab, width = (populations.shape[0], populations.shape[2])
    pieces = 4
    step = width // pieces

    def kernel(pop_ref, field_ref, out_ref, pop, force, post, out, in_sems, out_sems):
        def fetch(k):
            rows = pl.ds(k * step, step)
            return (
                pltpu.make_async_copy(pop_ref.at[:, :, rows, :], pop.at[:, :, rows, :], in_sems.at[0, k]),
                pltpu.make_async_copy(field_ref.at[:, :, rows, :], force.at[:, :, rows, :], in_sems.at[1, k]),
            )

        for k in range(pieces):
            for copy in fetch(k):
                copy.start()

        ranges = []
        for p in range(slab):
            if p > 0:
                ranges.append((p, 0, 5))
            if p < slab - 1:
                ranges.append((p, 5, 19))
            else:
                ranges.append((p, 10, 19))

        def kept(p):
            return [i for i in range(19) if 0 <= p + velocity_z[i] < slab]

        started = []

        def emit(k, low, high):
            @pl.loop(low // 8, high // 8)
            def _(t):
                for p in range(slab):
                    for i in kept(p):
                        x = velocity_x[i]
                        if x == 0:
                            continue
                        q = p + velocity_z[i]
                        near = pl.ds(pl.multiple_of(t * 8 + (0 if x > 0 else 8), 8), 16)
                        value = post[q, i, near, :]
                        value = value[7:15] if x > 0 else value[1:9]
                        out[q, i, pl.ds(pl.multiple_of(t * 8, 8), 8), :] = value

            for r, (p, begin, end) in enumerate(ranges):
                copy = pltpu.make_async_copy(
                    out.at[p, begin:end, low:high, :],
                    out_ref.at[p, begin:end, low:high, :],
                    out_sems.at[r, k],
                )
                copy.start()
                started.append(copy)

        for k in range(pieces):
            for copy in fetch(k):
                copy.wait()

            @pl.loop(k * step // 8, (k + 1) * step // 8)
            def _(t):
                rows = pl.ds(pl.multiple_of(t * 8, 8), 8)
                padded = pl.ds(pl.multiple_of(t * 8 + 8, 8), 8)
                for p in range(slab):
                    f = [pop[p, i, rows, :] for i in range(19)]
                    moved = collided(f, [force[p, c, rows, :] for c in range(3)], kept(p))
                    for i, value in moved.items():
                        if velocity_y[i]:
                            value = pltpu.roll(value, velocity_y[i] % width, 1)
                        q = p + velocity_z[i]
                        if velocity_x[i]:
                            post[q, i, padded, :] = value
                        else:
                            out[q, i, rows, :] = value

            if k < pieces - 1:
                emit(k, 8 if k == 0 else k * step - 8, (k + 1) * step - 8)
        for p in range(slab):
            for i in kept(p):
                q = p + velocity_z[i]
                if velocity_x[i] > 0:
                    post[q, i, 0:8, :] = post[q, i, width : width + 8, :]
                elif velocity_x[i] < 0:
                    post[q, i, width + 8 : width + 16, :] = post[q, i, 8:16, :]
        emit(pieces - 1, (pieces - 1) * step - 8, width)
        emit(pieces, 0, 8)
        for copy in started:
            copy.wait()

    return pl.pallas_call(
        kernel,
        out_shape=jax.ShapeDtypeStruct(populations.shape, jnp.float32),
        in_specs=[ANY, ANY],
        out_specs=ANY,
        scratch_shapes=[
            pltpu.VMEM(populations.shape, jnp.float32),
            pltpu.VMEM(field.shape, jnp.float32),
            pltpu.VMEM((slab, 19, width + 16, width), jnp.float32),
            pltpu.VMEM(populations.shape, jnp.float32),
            pltpu.SemaphoreType.DMA((2, pieces)),
            pltpu.SemaphoreType.DMA((2 * slab, pieces + 1)),
        ],
        compiler_params=pltpu.CompilerParams(vmem_limit_bytes=36 * MIB),
        name="interior",
        cost_estimate=pl.CostEstimate(flops=0, bytes_accessed=25_000_000, transcendentals=0),
    )(populations, field)


def arrivals(new_populations, lows, highs, edges):
    slab = new_populations.shape[0]
    count = len(lows)

    def kernel(*refs):
        parts, out_ref, sems = (refs[1 : 1 + 2 * count], refs[-2], refs[-1])
        copies = []
        for k, (begin, end) in enumerate(edges):
            for s, (part, plane, item) in enumerate(
                ((parts[k], 0, 0), (parts[count + k], slab - 1, 5))
            ):
                copies.append(
                    pltpu.make_async_copy(
                        part, out_ref.at[plane, item : item + 5, begin:end, :], sems.at[s, k]
                    )
                )
        for copy in copies:
            copy.start()
        for copy in copies:
            copy.wait()

    return pl.pallas_call(
        kernel,
        out_shape=jax.ShapeDtypeStruct(new_populations.shape, jnp.float32),
        in_specs=[ANY] + [VMEM] * (2 * count),
        out_specs=ANY,
        scratch_shapes=[pltpu.SemaphoreType.DMA((2, count))],
        input_output_aliases={0: 0},
        compiler_params=pltpu.CompilerParams(vmem_limit_bytes=8 * MIB),
        name="arrivals",
    )(new_populations, *lows, *highs)


def dispatched(membrane_force, offset, owner, cell, device_count, cells):
    point_count = owner.size
    capacity = 2 * point_count // device_count
    slot_total = device_count * capacity
    owner = owner.reshape(point_count)
    cell = cell.reshape(point_count)
    devices = jnp.arange(device_count, dtype=jnp.int32)
    counts = jnp.sum((owner[None, :] == devices[:, None]).astype(jnp.int32), 1)
    filler_ends = jnp.cumsum(capacity - counts)
    filler = jnp.arange(slot_total - point_count, dtype=jnp.int32)
    filler_owner = jnp.sum((filler[None, :] >= filler_ends[:, None]).astype(jnp.int32), 0)
    span = 2 * cells
    key = jnp.concatenate([owner * span + cell, filler_owner * span + cells])
    payload = jnp.concatenate(
        [membrane_force.reshape(3, point_count), offset.reshape(3, point_count)], 0
    )
    payload = jnp.pad(payload, ((0, 0), (0, slot_total - point_count)))
    ordered = lax.sort(
        (key,) + tuple(payload[i] for i in range(6)), num_keys=1, is_stable=False
    )
    tag = (ordered[0] % span).astype(jnp.float32)
    send = jnp.stack(
        [v.reshape(device_count, capacity) for v in list(ordered[1:]) + [tag]], 1
    )
    got = lax.all_to_all(send, ("ves", "shard"), split_axis=0, concat_axis=0, tiled=True)
    return got.transpose(1, 0, 2).reshape(7, slot_total)


CUTS = (0, 4, 8, 12, 16)


def one_step(displacement, tension, bending, offset, owner, cell, populations):
    membrane_force = membrane(displacement, tension, bending)
    device_count = lax.axis_size("ves") * lax.axis_size("shard")
    slab, width = (populations.shape[0], populations.shape[2])
    cells = slab * width * width
    windows = width // WINDOW
    got = dispatched(membrane_force, offset, owner, cell, device_count, cells)
    tag = got[6].astype(jnp.int32)
    plane, x, y = (tag // (width * width), tag // width % width, tag % width)
    x = (x + LAG) & (width - 1)
    x_bit = bits(slab) + bits(width)
    key = jnp.where(tag >= cells, width << x_bit, (x << x_bit) | (plane << bits(width)) | y)
    bounds = jnp.arange(windows + 1, dtype=jnp.int32) * (WINDOW << x_bit)
    starts = jnp.sum((key[None, :] < bounds[:, None]).astype(jnp.float32), 1)
    ordered = lax.sort(
        (key,) + tuple(got[i] for i in range(6)), num_keys=1, is_stable=False
    )
    listed = jnp.stack(
        list(ordered[1:])
        + [ordered[0].astype(jnp.float32), jnp.pad(starts, (0, key.size - windows - 1))],
        0,
    )
    below = passed_along(listed, ("ves", "shard"), 1)
    above = passed_along(listed, ("ves", "shard"), -1)
    total = spread_own(listed, slab, width)

    cuts = [cut * windows // CUTS[-1] for cut in CUTS]
    field = carry = head = None
    lows, highs, edges = ([], [], [])
    begin = 0
    for j, (first, last) in enumerate(zip(cuts[:-1], cuts[1:])):
        low, high, carry, field = spread_chunk(
            (below, above), total, carry, head if last == windows else None,
            populations, field, first, last,
        )
        if j == 0:
            head = carry[:, ROWS:]
        edges.append((begin, begin + low.shape[1]))
        begin += low.shape[1]
        lows.append(passed_along(low, ("ves", "shard"), 1))
        highs.append(passed_along(high, ("ves", "shard"), -1))
    new_populations = interior(populations, field)
    new_populations = arrivals(new_populations, lows, highs, edges)
    return (membrane_force, field, new_populations)


def solution(mesh):
    return jax.shard_map(
        one_step,
        mesh=mesh,
        in_specs=(
            P(None, "ves", "shard", None),
            P("ves"),
            P("ves"),
            P(None, "ves", "shard", None),
            P("ves", "shard", None),
            P("ves", "shard", None),
            P(("ves", "shard"), None, None, None),
        ),
        out_specs=(
            P(None, "ves", "shard", None),
            P(("ves", "shard"), None, None, None),
            P(("ves", "shard"), None, None, None),
        ),
        check_vma=False,
    )
```

profile of v0, /device:TPU:0, one launch (start us, length us, event | category | flops | bytes accessed | tf_op | source)
XLA Modules:
  0.0 180.0 jit_solution(15910921392447479526)
XLA Ops:
  0.6 0.8 fusion.34
  1.5 4.9 %collective-permute-start.1 = (f32[3,2,2,128]{3,2,1,0:T(2,128)S(1)}, f32[3,2,2,128]{3,2,1,0:T(2,128)S(1)}, u32[]{:S(2)}, u32[]{:S(2)}) collective-permute-start(f32[3,2,2,128]{3,2,1,0:T(2,128)S(1)} %get-tuple-element.84), channel_id=1, source_target_pairs={{0,1},{1,2},{2,3},{3,4},{4,5},{5,6},{6,7},{8,9},{9,10},{10,11},{11... | collective-permute-start | bytes 18440 | tf_op jit(solution)/shard_map/ppermute | solution.py:50
  6.3 1.3 collective-permute-start
  7.7 1.0 convert_reduce_fusion.2
  8.8 0.1 reduce
  8.9 0.2 convert_reduce_fusion.1
  9.2 0.8 multiply_add_fusion
  10.0 1.9 %collective-permute-done = f32[3,2,2,128]{3,2,1,0:T(2,128)S(1)} collective-permute-done((f32[3,2,2,128]{3,2,1,0:T(2,128)S(1)}, f32[3,2,2,128]{3,2,1,0:T(2,128)S(1)}, u32[]{:S(2)}, u32[]{:S(2)}) %collective-permute-start) | collective-permute-done | bytes 6176 | tf_op jit(solution)/shard_map/ppermute | solution.py:51
  11.9 0.9 pad_maximum_fusion
  12.8 0.1 fusion.32
  12.9 0.1 fusion.33
  13.0 0.1 fusion.1
  13.2 0.1 fusion.31
  13.3 0.1 fusion.30
  13.4 0.1 fusion.8
  13.5 0.3 copy-done.6
  13.8 0.1 copy_bitcast_fusion
  14.0 0.3 fusion.28
  14.3 13.3 %sort.90 = (s32[16384]{0:T(1024)S(1)}, f32[16384]{0:T(1024)S(1)}, f32[16384]{0:T(1024)S(1)}, f32[16384]{0:T(1024)S(1)}, f32[16384]{0:T(1024)S(1)}, /*index=5*/f32[16384]{0:T(1024)S(1)}, f32[16384]{0:T(1024)S(1)}) sort(s32[16384]{0:T(1024)S(1)} %pad_add_fusion, f32[16384]{0:T(1024)S(1)} %bitcast.63, f32[16384]{0:T(1024)S(1)} %bitcast.62, f32[16384]{0:T(1024)S(1)} %bitcast.61, ...), dimensions={0}, to_apply=%region_3.4 | sort | flops 229376 | bytes 917504 | tf_op jit(solution)/shard_map/sort | solution.py:519
  27.6 1.4 stack.30
  29.0 5.7 %all-to-all-start = ((f32[32,7,512]{2,1,0:T(8,128)}), f32[32,7,512]{2,1,0:T(8,128)S(1)}, u32[]{:S(2)}, u32[]{:S(2)}) async-start(f32[32,7,512]{2,1,0:T(8,128)} %stack.30), calls=%async_computation | async-start | bytes 1048576 | tf_op jit(solution)/shard_map/all_to_all | solution.py:526
  34.8 16.2 %all-to-all-done = f32[32,7,512]{2,1,0:T(8,128)S(1)} async-done(((f32[32,7,512]{2,1,0:T(8,128)}), f32[32,7,512]{2,1,0:T(8,128)S(1)}, u32[]{:S(2)}, u32[]{:S(2)}) %all-to-all-start) | async-done | bytes 458784 | tf_op jit(solution)/shard_map/all_to_all | solution.py:526
  51.0 0.3 fusion.27
  51.3 0.1 fusion.17
  51.4 0.4 convert_reduce_fusion
  51.9 0.5 fusion.24.starts
  52.4 13.3 %sort.91 = (s32[16384]{0:T(1024)S(1)}, f32[16384]{0:T(1024)S(1)}, f32[16384]{0:T(1024)S(1)}, f32[16384]{0:T(1024)S(1)}, f32[16384]{0:T(1024)S(1)}, /*index=5*/f32[16384]{0:T(1024)S(1)}, f32[16384]{0:T(1024)S(1)}) sort(s32[16384]{0:T(1024)S(1)} %fusion.17, f32[16384]{0:T(1024)S(1)} %bitcast.56, f32[16384]{0:T(1024)S(1)} %bitcast.55, f32[16384]{0:T(1024)S(1)} %bitcast.54, ...), dimensions={0}, to_apply=%region_4.5 | sort | flops 229376 | bytes 917504 | tf_op jit(solution)/shard_map/sort | solution.py:547
  65.7 0.8 stack.39.list_ref
  66.6 0.7 collective-permute-start.3
  67.3 1.4 collective-permute-start.2
  68.7 10.0 %spread_own.1.total_ref = f32[6,264,256]{2,1,0:T(8,128)} custom-call(s32[17]{0:T(128)} %fusion.24.starts, f32[8,16384]{1,0:T(8,128)} %copy-done.3), custom_call_target="tpu_custom_call" | custom-call | flops 20000000000 | bytes 4000000 | tf_op jit(solution)/shard_map/spread_own/pallas_call | solution.py:177
  78.6 12.8 %collective-permute-done.3.l1 = f32[8,16384]{1,0:T(8,128)S(1)} collective-permute-done((f32[8,16384]{1,0:T(8,128)S(1)}, f32[8,16384]{1,0:T(8,128)S(1)}, u32[]{:S(2)}, u32[]{:S(2)}) %collective-permute-start.3) | collective-permute-done | bytes 524320 | tf_op jit(solution)/shard_map/ppermute | solution.py:41
  91.5 3.8 %copy-done = f32[2,19,256,256]{3,2,1,0:T(8,128)S(1)} copy-done((f32[2,19,256,256]{3,2,1,0:T(8,128)S(1)}, f32[2,19,256,256]{3,2,1,0:T(8,128)}, u32[]{:S(2)}) %copy-start) | copy-done | bytes 9961496
  95.4 1.4 copy-done.2
  96.8 11.2 %shard_map.94 = (f32[5,48,256]{2,1,0:T(8,128)S(1)}, f32[5,48,256]{2,1,0:T(8,128)S(1)}, f32[6,48,256]{2,1,0:T(8,128)S(1)}, f32[2,3,256,256]{3,2,1,0:T(8,128)}) custom-call(s32[17]{0:T(128)S(1)} %fusion.26.s0, f32[8,16384]{1,0:T(8,128)S(1)} %collective-permute-done.2.l0, s32[17]{0:T(128)S(1)} %fusion.25.s1, f32[8,16384]{1,0:T(8,128)S(1)} %collective-permute-done.3.l1, ...), custom_call_target="tpu_custom_call" | custom-call | flops 8000000000 | bytes 4000000 | tf_op jit(solution)/shard_map/pallas_call | solution.py:330
  108.1 5.3 %collective-permute-start.8 = (f32[5,48,256]{2,1,0:T(8,128)S(1)}, f32[5,48,256]{2,1,0:T(8,128)S(1)}, u32[]{:S(2)}, u32[]{:S(2)}) collective-permute-start(f32[5,48,256]{2,1,0:T(8,128)S(1)} %get-tuple-element.57), channel_id=1, source_target_pairs={{0,31},{1,0},{2,1},{3,2},{4,3},{5,4},{6,5},{7,6},{8,7},{9,8},{10,9... | collective-permute-start | bytes 737288 | tf_op jit(solution)/shard_map/ppermute | solution.py:41
  113.4 12.2 %shard_map.95 = (f32[5,64,256]{2,1,0:T(8,128)S(1)}, f32[5,64,256]{2,1,0:T(8,128)S(1)}, f32[6,48,256]{2,1,0:T(8,128)S(1)}, f32[2,3,256,256]{3,2,1,0:T(8,128)}) custom-call(s32[17]{0:T(128)S(1)} %fusion.26.s0, f32[8,16384]{1,0:T(8,128)S(1)} %collective-permute-done.2.l0, s32[17]{0:T(128)S(1)} %fusion.25.s1, ...), custom_call_target="tpu_custom_call", output_to_operand_aliasing={{3}: (8, {})} | custom-call | flops 8000000000 | bytes 4000000 | tf_op jit(solution)/shard_map/pallas_call | solution.py:330
  125.7 11.7 %shard_map.96 = (f32[5,64,256]{2,1,0:T(8,128)S(1)}, f32[5,64,256]{2,1,0:T(8,128)S(1)}, f32[6,48,256]{2,1,0:T(8,128)S(1)}, f32[2,3,256,256]{3,2,1,0:T(8,128)}) custom-call(s32[17]{0:T(128)S(1)} %fusion.26.s0, f32[8,16384]{1,0:T(8,128)S(1)} %collective-permute-done.2.l0, s32[17]{0:T(128)S(1)} %fusion.25.s1, ...), custom_call_target="tpu_custom_call", output_to_operand_aliasing={{3}: (8, {})} | custom-call | flops 8000000000 | bytes 4000000 | tf_op jit(solution)/shard_map/pallas_call | solution.py:330
  137.5 12.9 %shard_map.97 = (f32[5,80,256]{2,1,0:T(8,128)S(1)}, f32[5,80,256]{2,1,0:T(8,128)S(1)}, f32[6,48,256]{2,1,0:T(8,128)}, f32[2,3,256,256]{3,2,1,0:T(8,128)}) custom-call(s32[17]{0:T(128)S(1)} %fusion.26.s0, f32[8,16384]{1,0:T(8,128)S(1)} %collective-permute-done.2.l0, s32[17]{0:T(128)S(1)} %fusion.25.s1, ...), custom_call_target="tpu_custom_call", output_to_operand_aliasing={{3}: (8, {})} | custom-call | flops 8000000000 | bytes 4000000 | tf_op jit(solution)/shard_map/pallas_call | solution.py:330
  150.4 5.3 %collective-permute-start.11 = (f32[5,80,256]{2,1,0:T(8,128)S(1)}, f32[5,80,256]{2,1,0:T(8,128)S(1)}, u32[]{:S(2)}, u32[]{:S(2)}) collective-permute-start(f32[5,80,256]{2,1,0:T(8,128)S(1)} %get-tuple-element.60), channel_id=1, source_target_pairs={{0,31},{1,0},{2,1},{3,2},{4,3},{5,4},{6,5},{7,6},{8,7},{9,8},{10,9... | collective-permute-start | bytes 1228808 | tf_op jit(solution)/shard_map/ppermute | solution.py:41
  155.8 2.0 %collective-permute-start.6 = (f32[5,64,256]{2,1,0:T(8,128)S(1)}, f32[5,64,256]{2,1,0:T(8,128)S(1)}, u32[]{:S(2)}, u32[]{:S(2)}) collective-permute-start(f32[5,64,256]{2,1,0:T(8,128)S(1)} %get-tuple-element.55), channel_id=1, source_target_pairs={{0,1},{1,2},{2,3},{3,4},{4,5},{5,6},{6,7},{7,8},{8,9},{9,10},{10,1... | collective-permute-start | bytes 983048 | tf_op jit(solution)/shard_map/ppermute | solution.py:41
  157.8 3.4 %collective-permute-start.10 = (f32[5,64,256]{2,1,0:T(8,128)S(1)}, f32[5,64,256]{2,1,0:T(8,128)S(1)}, u32[]{:S(2)}, u32[]{:S(2)}) collective-permute-start(f32[5,64,256]{2,1,0:T(8,128)S(1)} %get-tuple-element.59), channel_id=1, source_target_pairs={{0,31},{1,0},{2,1},{3,2},{4,3},{5,4},{6,5},{7,6},{8,7},{9,8},{10,9... | collective-permute-start | bytes 983048 | tf_op jit(solution)/shard_map/ppermute | solution.py:41
  161.2 1.4 copy-done.1
  162.6 10.2 %interior.1.refs_0_ = f32[2,19,256,256]{3,2,1,0:T(8,128)} custom-call(f32[2,19,256,256]{3,2,1,0:T(8,128)S(1)} %bitcast.48, f32[2,3,256,256]{3,2,1,0:T(8,128)S(1)} %copy-done.1), custom_call_target="tpu_custom_call" | custom-call | bytes 25000000 | tf_op jit(solution)/shard_map/interior/pallas_call | solution.py:450
  172.8 1.9 %collective-permute-done.9.refs_6_ = f32[5,64,256]{2,1,0:T(8,128)S(1)} collective-permute-done((f32[5,64,256]{2,1,0:T(8,128)S(1)}, f32[5,64,256]{2,1,0:T(8,128)S(1)}, u32[]{:S(2)}, u32[]{:S(2)}) %collective-permute-start.9) | collective-permute-done | bytes 327712 | tf_op jit(solution)/shard_map/ppermute | solution.py:41
  174.7 1.2 collective-permute-done.6.refs_3_
  175.9 2.3 %collective-permute-done.10.refs_7_ = f32[5,64,256]{2,1,0:T(8,128)S(1)} collective-permute-done((f32[5,64,256]{2,1,0:T(8,128)S(1)}, f32[5,64,256]{2,1,0:T(8,128)S(1)}, u32[]{:S(2)}, u32[]{:S(2)}) %collective-permute-start.10) | collective-permute-done | bytes 327712 | tf_op jit(solution)/shard_map/ppermute | solution.py:41
  178.2 1.5 arrivals.1
  (49 shorter events, 0.7 us)
Async XLA Ops:
  0.6 12.4 %copy-start.4 = (f32[3,2,32,128]{3,2,1,0:T(8,128)S(1)}, f32[3,2,32,128]{3,2,1,0:T(8,128)}, u32[]{:S(2)}) copy-start(f32[3,2,32,128]{3,2,1,0:T(8,128)} %param.7) | copy-start | bytes 294916
  1.5 8.5 %collective-permute-start.1 = (f32[3,2,2,128]{3,2,1,0:T(2,128)S(1)}, f32[3,2,2,128]{3,2,1,0:T(2,128)S(1)}, u32[]{:S(2)}, u32[]{:S(2)}) collective-permute-start(f32[3,2,2,128]{3,2,1,0:T(2,128)S(1)} %get-tuple-element.84), channel_id=1, source_target_pairs={{0,1},{1,2},{2,3},{3,4},{4,5},{5,6},{6,7},{8,9},{9,10},{10,11},{11... | collective-permute-start | bytes 18440 | tf_op jit(solution)/shard_map/ppermute | solution.py:50
  6.3 5.5 %collective-permute-start = (f32[3,2,2,128]{3,2,1,0:T(2,128)S(1)}, f32[3,2,2,128]{3,2,1,0:T(2,128)S(1)}, u32[]{:S(2)}, u32[]{:S(2)}) collective-permute-start(f32[3,2,2,128]{3,2,1,0:T(2,128)S(1)} %get-tuple-element.85), channel_id=1, source_target_pairs={{1,0},{2,1},{3,2},{4,3},{5,4},{6,5},{7,6},{9,8},{10,9},{11,10},{12... | collective-permute-start | bytes 18440 | tf_op jit(solution)/shard_map/ppermute | solution.py:51
  9.1 4.2 %copy-start.7 = (f32[2]{0:T(128)S(1)}, f32[2]{0:T(128)}, u32[]{:S(2)}) copy-start(f32[2]{0:T(128)} %param.9) | copy-start | bytes 28
  9.2 4.2 %copy-start.8 = (f32[2]{0:T(128)S(1)}, f32[2]{0:T(128)}, u32[]{:S(2)}) copy-start(f32[2]{0:T(128)} %param.8) | copy-start | bytes 28
  12.9 0.9 copy-start.6
  13.5 15.5 %copy-start.5 = (f32[3,2,32,128]{3,2,1,0:T(8,128)}, f32[3,2,32,128]{3,2,1,0:T(8,128)S(1)}, u32[]{:S(2)}) copy-start(f32[3,2,32,128]{3,2,1,0:T(8,128)S(1)} %fusion.8) | copy-start | bytes 294916
  29.0 22.0 %all-to-all-start = ((f32[32,7,512]{2,1,0:T(8,128)}), f32[32,7,512]{2,1,0:T(8,128)S(1)}, u32[]{:S(2)}, u32[]{:S(2)}) async-start(f32[32,7,512]{2,1,0:T(8,128)} %stack.30), calls=%async_computation | async-start | bytes 1048576 | tf_op jit(solution)/shard_map/all_to_all | solution.py:526
  66.6 2.1 %copy-start.3 = (f32[8,16384]{1,0:T(8,128)}, f32[8,16384]{1,0:T(8,128)S(1)}, u32[]{:S(2)}) copy-start(f32[8,16384]{1,0:T(8,128)S(1)} %stack.39.list_ref) | copy-start | bytes 1572868
  66.6 24.9 %collective-permute-start.3 = (f32[8,16384]{1,0:T(8,128)S(1)}, f32[8,16384]{1,0:T(8,128)S(1)}, u32[]{:S(2)}, u32[]{:S(2)}) collective-permute-start(f32[8,16384]{1,0:T(8,128)S(1)} %stack.39.list_ref), channel_id=1, source_target_pairs={{0,31},{1,0},{2,1},{3,2},{4,3},{5,4},{6,5},{7,6},{8,7},{9,8},{10,9... | collective-permute-start | bytes 1572872 | tf_op jit(solution)/shard_map/ppermute | solution.py:41
  67.3 24.2 %collective-permute-start.2 = (f32[8,16384]{1,0:T(8,128)S(1)}, f32[8,16384]{1,0:T(8,128)S(1)}, u32[]{:S(2)}, u32[]{:S(2)}) collective-permute-start(f32[8,16384]{1,0:T(8,128)S(1)} %stack.39.list_ref), channel_id=1, source_target_pairs={{0,1},{1,2},{2,3},{3,4},{4,5},{5,6},{6,7},{7,8},{8,9},{9,10},{10,1... | collective-permute-start | bytes 1572872 | tf_op jit(solution)/shard_map/ppermute | solution.py:41
  91.5 3.8 %copy-start = (f32[2,19,256,256]{3,2,1,0:T(8,128)S(1)}, f32[2,19,256,256]{3,2,1,0:T(8,128)}, u32[]{:S(2)}) copy-start(f32[2,19,256,256]{3,2,1,0:T(8,128)} %pop_ref.9) | copy-start | bytes 29884420
  95.4 1.4 copy-start.2
  108.0 47.8 %collective-permute-start.4 = (f32[5,48,256]{2,1,0:T(8,128)S(1)}, f32[5,48,256]{2,1,0:T(8,128)S(1)}, u32[]{:S(2)}, u32[]{:S(2)}) collective-permute-start(f32[5,48,256]{2,1,0:T(8,128)S(1)} %get-tuple-element.53), channel_id=1, source_target_pairs={{0,1},{1,2},{2,3},{3,4},{4,5},{5,6},{6,7},{7,8},{8,9},{9,10},{10,1... | collective-permute-start | bytes 737288 | tf_op jit(solution)/shard_map/ppermute | solution.py:41
  108.1 47.8 %collective-permute-start.8 = (f32[5,48,256]{2,1,0:T(8,128)S(1)}, f32[5,48,256]{2,1,0:T(8,128)S(1)}, u32[]{:S(2)}, u32[]{:S(2)}) collective-permute-start(f32[5,48,256]{2,1,0:T(8,128)S(1)} %get-tuple-element.57), channel_id=1, source_target_pairs={{0,31},{1,0},{2,1},{3,2},{4,3},{5,4},{6,5},{7,6},{8,7},{9,8},{10,9... | collective-permute-start | bytes 737288 | tf_op jit(solution)/shard_map/ppermute | solution.py:41
  113.4 24.0 %slice-start = ((s8[9961472]{0:T(1024)(128)(4,1)}), s8[4194304]{0:T(1024)(128)(4,1)S(1)}, s32[]{:S(2)}) async-start(s8[9961472]{0:T(1024)(128)(4,1)} %bitcast.47), calls=%async_computation.1 | async-start | bytes 8388608
  113.4 24.1 %slice-start.1 = ((s8[9961472]{0:T(1024)(128)(4,1)}), s8[4194304]{0:T(1024)(128)(4,1)S(1)}, s32[]{:S(2)}) async-start(s8[9961472]{0:T(1024)(128)(4,1)} %bitcast.47), calls=%async_computation.2 | async-start | bytes 8388608
  125.6 32.2 %collective-permute-start.5 = (f32[5,64,256]{2,1,0:T(8,128)S(1)}, f32[5,64,256]{2,1,0:T(8,128)S(1)}, u32[]{:S(2)}, u32[]{:S(2)}) collective-permute-start(f32[5,64,256]{2,1,0:T(8,128)S(1)} %get-tuple-element.54), channel_id=1, source_target_pairs={{0,1},{1,2},{2,3},{3,4},{4,5},{5,6},{6,7},{7,8},{8,9},{9,10},{10,1... | collective-permute-start | bytes 983048 | tf_op jit(solution)/shard_map/ppermute | solution.py:41
  125.7 11.8 %slice-start.2 = ((s8[9961472]{0:T(1024)(128)(4,1)}), s8[1572864]{0:T(1024)(128)(4,1)S(1)}, s32[]{:S(2)}) async-start(s8[9961472]{0:T(1024)(128)(4,1)} %bitcast.47), calls=%async_computation.3 | async-start | bytes 3145728
  150.4 27.8 %collective-permute-start.7 = (f32[5,80,256]{2,1,0:T(8,128)S(1)}, f32[5,80,256]{2,1,0:T(8,128)S(1)}, u32[]{:S(2)}, u32[]{:S(2)}) collective-permute-start(f32[5,80,256]{2,1,0:T(8,128)S(1)} %get-tuple-element.56), channel_id=1, source_target_pairs={{0,1},{1,2},{2,3},{3,4},{4,5},{5,6},{6,7},{7,8},{8,9},{9,10},{10,1... | collective-permute-start | bytes 1228808 | tf_op jit(solution)/shard_map/ppermute | solution.py:41
  150.4 27.8 %collective-permute-start.11 = (f32[5,80,256]{2,1,0:T(8,128)S(1)}, f32[5,80,256]{2,1,0:T(8,128)S(1)}, u32[]{:S(2)}, u32[]{:S(2)}) collective-permute-start(f32[5,80,256]{2,1,0:T(8,128)S(1)} %get-tuple-element.60), channel_id=1, source_target_pairs={{0,31},{1,0},{2,1},{3,2},{4,3},{5,4},{6,5},{7,6},{8,7},{9,8},{10,9... | collective-permute-start | bytes 1228808 | tf_op jit(solution)/shard_map/ppermute | solution.py:41
  155.8 18.9 %collective-permute-start.9 = (f32[5,64,256]{2,1,0:T(8,128)S(1)}, f32[5,64,256]{2,1,0:T(8,128)S(1)}, u32[]{:S(2)}, u32[]{:S(2)}) collective-permute-start(f32[5,64,256]{2,1,0:T(8,128)S(1)} %get-tuple-element.58), channel_id=1, source_target_pairs={{0,31},{1,0},{2,1},{3,2},{4,3},{5,4},{6,5},{7,6},{8,7},{9,8},{10,9... | collective-permute-start | bytes 983048 | tf_op jit(solution)/shard_map/ppermute | solution.py:41
  155.8 20.1 %collective-permute-start.6 = (f32[5,64,256]{2,1,0:T(8,128)S(1)}, f32[5,64,256]{2,1,0:T(8,128)S(1)}, u32[]{:S(2)}, u32[]{:S(2)}) collective-permute-start(f32[5,64,256]{2,1,0:T(8,128)S(1)} %get-tuple-element.55), channel_id=1, source_target_pairs={{0,1},{1,2},{2,3},{3,4},{4,5},{5,6},{6,7},{7,8},{8,9},{9,10},{10,1... | collective-permute-start | bytes 983048 | tf_op jit(solution)/shard_map/ppermute | solution.py:41
  157.8 20.4 %collective-permute-start.10 = (f32[5,64,256]{2,1,0:T(8,128)S(1)}, f32[5,64,256]{2,1,0:T(8,128)S(1)}, u32[]{:S(2)}, u32[]{:S(2)}) collective-permute-start(f32[5,64,256]{2,1,0:T(8,128)S(1)} %get-tuple-element.59), channel_id=1, source_target_pairs={{0,31},{1,0},{2,1},{3,2},{4,3},{5,4},{6,5},{7,6},{8,7},{9,8},{10,9... | collective-permute-start | bytes 983048 | tf_op jit(solution)/shard_map/ppermute | solution.py:41
  161.2 1.4 copy-start.1
where the time goes:
time: 181 us; the launch traced here: 180 us
  Pallas kernels  69.7 us (39%)
  waiting for transfers between devices  36.4 us (20%)
  other arithmetic  31.5 us (17%)
  starting transfers between devices  30.3 us (17%)
  local copies, waits for them, and re-layouts  10.9 us (6%)
    pallas_call x4, Pallas kernels, spread_chunk(): pl.pallas_call(kernel, out_shape=(shape((5, n, width), jnp.float32), shap...  48 us
    ppermute x10, starting transfers between devices, passed_along(): return lax.ppermute(value, axis, pairs)  18.3 us
    ppermute x10, waiting for transfers between devices, passed_along(): return lax.ppermute(value, axis, pairs)  18.3 us
    all_to_all x1, waiting for transfers between devices, dispatched(): lax.all_to_all(send, ('ves', 'shard'), split_axis=0, concat_axis=0, tiled...  16.2 us
    sort x1, other arithmetic, one_step(): lax.sort((key,) + tuple((got[i] for i in range(6))), num_keys=1, is_stabl...  13.3 us
    sort x1, other arithmetic, dispatched(): lax.sort((key,) + tuple((payload[i] for i in range(6))), num_keys=1, is_s...  13.3 us
    pallas_call x1, Pallas kernels, interior(): pl.pallas_call(kernel, out_shape=jax.ShapeDtypeStruct(populations.shape,...  10.2 us
    pallas_call x1, Pallas kernels, spread_own(): pl.pallas_call(kernel, out_shape=jax.ShapeDtypeStruct((slab * 3, width +...  9.98 us
  transfers between devices with their start and end apart: 13, of which 6 were waited for; matrix products, arithmetic and copies ran while one was open for 1% of the time, Pallas kernels for 32%

commit v1 on v0

--- a/solution.py
+++ b/solution.py
@@ -103,42 +103,71 @@
     return (count - 1).bit_length()
 
 
-def spread_list(starts, list_ref, acc, shift, planes, slab, ranges):
+LANES = 128
+MIB = 1 << 20
+
+
+def rows_of(planes):
+    return 13 + 3 * len(planes)
+
+
+def spread_list(starts, list_ref, acc, table, shift, planes, slab, ranges):
     width = acc.shape[2]
-    row_id = lax.broadcasted_iota(jnp.int32, (ROWS, BLOCK), 0)
-    y_id = lax.broadcasted_iota(jnp.int32, (width, BLOCK), 0)
-
-    def pick(rel, parts):
-        result = jnp.zeros(rel.shape, jnp.float32)
+    count = table.shape[1]
+    row_id = lax.broadcasted_iota(jnp.int32, (ROWS, LANES), 0).astype(jnp.float32)
+    y_id = lax.broadcasted_iota(jnp.int32, (width, LANES), 0).astype(jnp.bfloat16)
+
+    def prepare(t):
+        at = pl.ds(pl.multiple_of(t * 8, 8), 8)
+        part = [list_ref[pl.ds(pl.multiple_of(c * count + t * 8, 8), 8), :] for c in range(7)]
+        key = part[6].astype(jnp.int32)
+        y = key & (width - 1)
+        plane = (key >> bits(width)) & (slab - 1)
+        table[0, at, :] = (key >> (bits(width) + bits(slab))).astype(jnp.float32)
+        phi_x, phi_y, phi_z = (weights(part[c]) for c in (3, 4, 5))
         for k in range(4):
-            result = jnp.where(rel == k, parts[k], result)
-        return result
+            table[1 + k, at, :] = phi_x[k]
+            table[5 + k, at, :] = phi_y[k]
+            table[9 + k, at, :] = ((y + (k - 1)) & (width - 1)).astype(jnp.float32)
+        for n, q in enumerate(planes):
+            rel = q + 1 + shift - plane
+            weight = jnp.zeros_like(part[0])
+            for k in range(4):
+                weight = jnp.where(rel == k, phi_z[k], weight)
+            for c in range(3):
+                table[13 + n * 3 + c, at, :] = part[c] * weight
+
+    def half(r, base):
+        def row(i, like):
+            return jnp.broadcast_to(table[i, pl.ds(r, 1), :], like.shape)
+
+        def narrow(i):
+            return jnp.broadcast_to(table[i, pl.ds(r, 1), :].astype(jnp.bfloat16), y_id.shape)
+
+        right = jnp.zeros(y_id.shape, jnp.bfloat16)
+        for k in range(4):
+            right = jnp.where(y_id == narrow(9 + k), narrow(5 + k), right)
+        x = table[0, pl.ds(r, 1), :] - base
+        x = jnp.where((x >= 0.0) & (x < WINDOW), x, 4.0 * ROWS)
+        rel = row_id - x
+        weight_x = jnp.zeros(row_id.shape, jnp.float32)
+        for k in range(4):
+            weight_x = jnp.where(rel == k, row(1 + k, row_id), weight_x)
+        lefts = [row(13 + i, row_id) * weight_x for i in range(3 * len(planes))]
+        return jnp.concatenate(lefts, 0).astype(jnp.bfloat16), right
 
     def window(w, offset):
         begin = starts[w] // BLOCK
         end = (starts[w + 1] + (BLOCK - 1)) // BLOCK
-        base = w * WINDOW
+        base = (w * WINDOW).astype(jnp.float32)
         at_row = (w + offset) * WINDOW
 
         @pl.loop(begin, end)
         def _(b):
-            at = pl.ds(pl.multiple_of(b * BLOCK, BLOCK), BLOCK)
-            phi = weights(list_ref[3:6, at])
-            key = list_ref[6:7, at].astype(jnp.int32)
-            y = key & ((1 << bits(width)) - 1)
-            plane = (key >> bits(width)) & ((1 << bits(slab)) - 1)
-            x = (key >> (bits(width) + bits(slab))) - base
-            x = jnp.where((x >= 0) & (x < WINDOW), x, 4 * ROWS)
-            weight_x = pick(row_id - x, [phi[k][0:1] for k in range(4)])
-            right = pick((y_id - (y - 1)) & (width - 1), [phi[k][1:2] for k in range(4)])
-            lefts = []
-            for q in planes:
-                weight_z = pick(q + 1 + shift - plane, [phi[k][2:3] for k in range(4)])
-                for c in range(3):
-                    lefts.append((list_ref[c : c + 1, at] * weight_z) * weight_x)
+            parts = [half(b * (BLOCK // LANES) + h, base) for h in range(BLOCK // LANES)]
             product = lax.dot_general(
-                jnp.concatenate(lefts, 0).astype(jnp.bfloat16),
-                right.astype(jnp.bfloat16),
+                jnp.concatenate([p[0] for p in parts], 1),
+                jnp.concatenate([p[1] for p in parts], 1),
                 (((1,), (1,)), ((), ())),
                 preferred_element_type=jnp.float32,
             )
@@ -149,6 +178,13 @@
                     acc[q * 3 + c, rows, :] += product[i * ROWS : (i + 1) * ROWS]
 
     for first, last, offset in ranges:
+        unit = 8 * LANES
+        low = starts[first] // BLOCK * BLOCK // unit
+        high = (starts[last] + (BLOCK - 1)) // BLOCK * BLOCK
+
+        @pl.loop(low, (high + (unit - 1)) // unit)
+        def _(t):
+            prepare(t)
 
         @pl.loop(first, last)
         def _(w):
@@ -164,28 +200,33 @@
 
 
 def starts_of(listed, windows):
-    return listed[7, : windows + 1].astype(jnp.int32)
+    return listed[-8, : windows + 1].astype(jnp.int32)
 
 
 def spread_own(listed, slab, width):
     windows = width // WINDOW
 
-    def kernel(starts, list_ref, acc):
+    count = (listed.shape[0] - 8) // 7
+    assert count % 8 == 0
+
+    def kernel(starts, list_ref, acc, table):
         acc[...] = jnp.zeros_like(acc)
-        spread_list(starts, list_ref, acc, 0, range(slab), slab, [(0, windows, 0)])
+        spread_list(starts, list_ref, acc, table, 0, range(slab), slab, [(0, windows, 0)])
 
     return pl.pallas_call(
         kernel,
         out_shape=jax.ShapeDtypeStruct((slab * 3, width + ROWS - WINDOW, width), jnp.float32),
         in_specs=[SMEM, VMEM],
         out_specs=VMEM,
+        scratch_shapes=[pltpu.VMEM((rows_of(range(slab)), count, LANES), jnp.float32)],
+        compiler_params=pltpu.CompilerParams(vmem_limit_bytes=12 * MIB),
         name="spread_own",
         cost_estimate=cost(20_000_000_000),
     )(starts_of(listed, windows), listed)
 
 
 ANY = pl.BlockSpec(memory_space=pl.ANY)
-MIB = 1 << 20
+HBM = pl.BlockSpec(memory_space=pltpu.HBM)
 LAG = 7
 KEEP = 1.0 - 1.0 / relax_time
 FORCING = 1.0 - 0.5 / relax_time
@@ -249,7 +290,7 @@
     planes = (slab - 1, 0)
 
     def kernel(s0, l0, s1, l1, total_ref, carry_ref, head_ref, pop_ref, field_in, *rest):
-        low, high, carry_out, field_out, acc, pop, post, sems = rest
+        low, high, carry_out, field_out, acc, pop, post, table, sems = rest
         del field_in
         copies = []
 
@@ -281,8 +322,8 @@
         if closing:
             acc[:, stop:span, :] = jnp.zeros((slab * 3, span - stop, width), jnp.float32)
         moves = (first, last, 0 if opening else 1 - first)
-        spread_list(s0, l0, acc, slab, (0, 1), slab, [moves])
-        spread_list(s1, l1, acc, -slab, (slab - 1,), slab, [moves])
+        spread_list(s0, l0, acc, table, slab, (0, 1), slab, [moves])
+        spread_list(s1, l1, acc, table, -slab, (slab - 1,), slab, [moves])
         if closing:
             acc[:, n : n + 16, :] += head_ref[:, 0:16, :]
         if opening:
@@ -335,12 +376,13 @@
             shape((slab * 3, 2 * ROWS, width), jnp.float32),
             shape((slab, 3, width, width), jnp.float32),
         ),
-        in_specs=[SMEM, VMEM, SMEM, VMEM, ANY, ANY, VMEM, ANY, ANY],
-        out_specs=(VMEM, VMEM, VMEM, ANY),
+        in_specs=[SMEM, VMEM, SMEM, VMEM, HBM, ANY, VMEM, HBM, HBM],
+        out_specs=(VMEM, VMEM, VMEM, HBM),
         scratch_shapes=[
             pltpu.VMEM((slab * 3, span, width), jnp.float32),
             pltpu.VMEM((2, 19, n + 16, width), jnp.float32),
             pltpu.VMEM((10, n + 16, width), jnp.float32),
+            pltpu.VMEM((rows_of((0, 1)), (below.shape[0] - 8) // 7, LANES), jnp.float32),
             pltpu.SemaphoreType.DMA((8 + slab * 3,)),
         ],
         input_output_aliases={} if field is None else {8: 3},
@@ -450,8 +492,8 @@
     return pl.pallas_call(
         kernel,
         out_shape=jax.ShapeDtypeStruct(populations.shape, jnp.float32),
-        in_specs=[ANY, ANY],
-        out_specs=ANY,
+        in_specs=[HBM, HBM],
+        out_specs=HBM,
         scratch_shapes=[
             pltpu.VMEM(populations.shape, jnp.float32),
             pltpu.VMEM(field.shape, jnp.float32),
@@ -490,8 +532,8 @@
     return pl.pallas_call(
         kernel,
         out_shape=jax.ShapeDtypeStruct(new_populations.shape, jnp.float32),
-        in_specs=[ANY] + [VMEM] * (2 * count),
-        out_specs=ANY,
+        in_specs=[HBM] + [VMEM] * (2 * count),
+        out_specs=HBM,
         scratch_shapes=[pltpu.SemaphoreType.DMA((2, count))],
         input_output_aliases={0: 0},
         compiler_params=pltpu.CompilerParams(vmem_limit_bytes=8 * MIB),
@@ -547,9 +589,11 @@
     ordered = lax.sort(
         (key,) + tuple(got[i] for i in range(6)), num_keys=1, is_stable=False
     )
-    listed = jnp.stack(
-        list(ordered[1:])
-        + [ordered[0].astype(jnp.float32), jnp.pad(starts, (0, key.size - windows - 1))],
+    columns = list(ordered[1:]) + [ordered[0].astype(jnp.float32)]
+    starts = jnp.pad(starts, (0, LANES - windows - 1))
+    listed = jnp.concatenate(
+        [v.reshape(-1, LANES) for v in columns]
+        + [jnp.broadcast_to(starts[None, :], (8, LANES))],
         0,
     )
     below = passed_along(listed, ("ves", "shard"), 1)

time: 181 us -> 167 us (0.923)
  Pallas kernels: 69.7 us -> 60.8 us
  local copies, waits for them, and re-layouts: 10.9 us -> 4.88 us
  waiting for transfers between devices: 36.4 us -> 38.7 us
    pallas_call x4, Pallas kernels: 48 us -> 42.1 us  [spread_chunk(): pl.pallas_call(kernel, out_shape=(shape((5, n, width), jnp.float32), shap...]
    unnamed x24, local copies, waits for them, and re-layouts: 6.96 us -> 1.75 us
    pallas_call x1, Pallas kernels: 9.98 us -> 7.05 us  [spread_own(): pl.pallas_call(kernel, out_shape=jax.ShapeDtypeStruct((slab * 3, width +...]
    ppermute x10, waiting for transfers between devices: 18.3 us -> 20.6 us  [passed_along(): return lax.ppermute(value, axis, pairs)]
  transfers between devices with their start and end apart: 13 -> 13, of which waited for: 6 -> 6; matrix products, arithmetic and copies ran while one was open for 1% -> 1% of each run, Pallas kernels for 32% -> 30%
where the time goes in v1:
time: 167 us
  Pallas kernels  60.8 us (36%)
  waiting for transfers between devices  38.7 us (23%)
  other arithmetic  31 us (19%)
  starting transfers between devices  30.3 us (18%)
  local copies, waits for them, and re-layouts  4.88 us (3%)
    pallas_call x4, Pallas kernels, spread_chunk(): pl.pallas_call(kernel, out_shape=(shape((5, n, width), jnp.float32), shap...  42.1 us
    ppermute x10, waiting for transfers between devices, passed_along(): return lax.ppermute(value, axis, pairs)  20.6 us
    ppermute x10, starting transfers between devices, passed_along(): return lax.ppermute(value, axis, pairs)  18.3 us
    all_to_all x1, waiting for transfers between devices, dispatched(): lax.all_to_all(send, ('ves', 'shard'), split_axis=0, concat_axis=0, tiled...  16.2 us
    sort x1, other arithmetic, one_step(): lax.sort((key,) + tuple((got[i] for i in range(6))), num_keys=1, is_stabl...  13.3 us
    sort x1, other arithmetic, dispatched(): lax.sort((key,) + tuple((payload[i] for i in range(6))), num_keys=1, is_s...  13.3 us
    pallas_call x1, Pallas kernels, interior(): pl.pallas_call(kernel, out_shape=jax.ShapeDtypeStruct(populations.shape,...  10.2 us
    pallas_call x1, Pallas kernels, spread_own(): pl.pallas_call(kernel, out_shape=jax.ShapeDtypeStruct((slab * 3, width +...  7.05 us
  transfers between devices with their start and end apart: 13, of which 6 were waited for; matrix products, arithmetic and copies ran while one was open for 1% of the time, Pallas kernels for 30%

profile of v1, /device:TPU:0, one launch (start us, length us, event | category | flops | bytes accessed | tf_op | source)
XLA Modules:
  0.0 166.9 jit_solution(9709631368813057453)
XLA Ops:
  0.6 0.8 fusion.33
  1.5 4.9 %collective-permute-start.1 = (f32[3,2,2,128]{3,2,1,0:T(2,128)S(1)}, f32[3,2,2,128]{3,2,1,0:T(2,128)S(1)}, u32[]{:S(2)}, u32[]{:S(2)}) collective-permute-start(f32[3,2,2,128]{3,2,1,0:T(2,128)S(1)} %get-tuple-element.84), channel_id=1, source_target_pairs={{0,1},{1,2},{2,3},{3,4},{4,5},{5,6},{6,7},{8,9},{9,10},{10,11},{11... | collective-permute-start | bytes 18440 | tf_op jit(solution)/shard_map/ppermute | solution.py:50
  6.3 1.3 collective-permute-start
  7.7 1.0 convert_reduce_fusion.2
  8.6 0.1 copy.16
  8.8 0.1 reduce
  8.9 0.2 convert_reduce_fusion.1
  9.2 0.8 multiply_add_fusion
  10.0 1.9 %collective-permute-done = f32[3,2,2,128]{3,2,1,0:T(2,128)S(1)} collective-permute-done((f32[3,2,2,128]{3,2,1,0:T(2,128)S(1)}, f32[3,2,2,128]{3,2,1,0:T(2,128)S(1)}, u32[]{:S(2)}, u32[]{:S(2)}) %collective-permute-start) | collective-permute-done | bytes 6176 | tf_op jit(solution)/shard_map/ppermute | solution.py:51
  11.9 0.9 pad_maximum_fusion
  12.8 0.1 fusion.31
  12.9 0.1 fusion.32
  13.0 0.1 fusion.1
  13.2 0.1 fusion.30
  13.3 0.1 fusion.29
  13.4 0.1 fusion.8
  13.5 0.2 copy-done.3
  13.8 0.1 copy_bitcast_fusion
  14.0 0.3 fusion.27
  14.3 13.3 %sort.90 = (s32[16384]{0:T(1024)S(1)}, f32[16384]{0:T(1024)S(1)}, f32[16384]{0:T(1024)S(1)}, f32[16384]{0:T(1024)S(1)}, f32[16384]{0:T(1024)S(1)}, /*index=5*/f32[16384]{0:T(1024)S(1)}, f32[16384]{0:T(1024)S(1)}) sort(s32[16384]{0:T(1024)S(1)} %pad_add_fusion, f32[16384]{0:T(1024)S(1)} %bitcast.67, f32[16384]{0:T(1024)S(1)} %bitcast.66, f32[16384]{0:T(1024)S(1)} %bitcast.65, ...), dimensions={0}, to_apply=%region_3.4 | sort | flops 229376 | bytes 917504 | tf_op jit(solution)/shard_map/sort | solution.py:561
  27.6 1.4 stack.3
  29.0 5.7 %all-to-all-start = ((f32[32,7,512]{2,1,0:T(8,128)}), f32[32,7,512]{2,1,0:T(8,128)S(1)}, u32[]{:S(2)}, u32[]{:S(2)}) async-start(f32[32,7,512]{2,1,0:T(8,128)} %stack.3), calls=%async_computation | async-start | bytes 1048576 | tf_op jit(solution)/shard_map/all_to_all | solution.py:568
  34.8 16.2 %all-to-all-done = f32[32,7,512]{2,1,0:T(8,128)S(1)} async-done(((f32[32,7,512]{2,1,0:T(8,128)}), f32[32,7,512]{2,1,0:T(8,128)S(1)}, u32[]{:S(2)}, u32[]{:S(2)}) %all-to-all-start) | async-done | bytes 458784 | tf_op jit(solution)/shard_map/all_to_all | solution.py:568
  51.0 0.3 fusion.26
  51.3 0.1 fusion.17
  51.4 0.4 convert_reduce_fusion
  51.9 13.3 %sort.91 = (s32[16384]{0:T(1024)S(1)}, f32[16384]{0:T(1024)S(1)}, f32[16384]{0:T(1024)S(1)}, f32[16384]{0:T(1024)S(1)}, f32[16384]{0:T(1024)S(1)}, /*index=5*/f32[16384]{0:T(1024)S(1)}, f32[16384]{0:T(1024)S(1)}) sort(s32[16384]{0:T(1024)S(1)} %fusion.17, f32[16384]{0:T(1024)S(1)} %bitcast.60, f32[16384]{0:T(1024)S(1)} %bitcast.59, f32[16384]{0:T(1024)S(1)} %bitcast.58, ...), dimensions={0}, to_apply=%region_4.5 | sort | flops 229376 | bytes 917504 | tf_op jit(solution)/shard_map/sort | solution.py:589
  65.4 0.7 collective-permute-start.3
  66.0 1.4 collective-permute-start.2
  67.5 7.0 %spread_own.1.total_ref = f32[6,264,256]{2,1,0:T(8,128)S(1)} custom-call(s32[17]{0:T(128)S(1)} %convert_element_type.59.starts, f32[904,128]{1,0:T(8,128)S(1)} %constant_dynamic-update-slice_fusion.list_ref), custom_call_target="tpu_custom_call" | custom-call | flops 20000000000 | bytes 4000000 | tf_op jit(solution)/shard_map/spread_own/pallas_call | solution.py:216
  74.5 13.1 %collective-permute-done.3.l1 = f32[904,128]{1,0:T(8,128)S(1)} collective-permute-done((f32[904,128]{1,0:T(8,128)S(1)}, f32[904,128]{1,0:T(8,128)S(1)}, u32[]{:S(2)}, u32[]{:S(2)}) %collective-permute-start.3) | collective-permute-done | bytes 462880 | tf_op jit(solution)/shard_map/ppermute | solution.py:41
  87.7 9.7 %shard_map.94 = (f32[5,48,256]{2,1,0:T(8,128)S(1)}, f32[5,48,256]{2,1,0:T(8,128)S(1)}, f32[6,48,256]{2,1,0:T(8,128)S(1)}, f32[2,3,256,256]{3,2,1,0:T(8,128)}) custom-call(s32[17]{0:T(128)S(1)} %fusion.25.s0, f32[904,128]{1,0:T(8,128)S(1)} %collective-permute-done.2.l0, s32[17]{0:T(128)S(1)} %fusion.24.s1, f32[904,128]{1,0:T(8,128)S(1)} %collective-permute-done.3.l1, ...), custom_call_target="tpu_custom_call" | custom-call | flops 8000000000 | bytes 4000000 | tf_op jit(solution)/shard_map/pallas_call | solution.py:371
  97.5 0.1 collective-permute-start.4
  97.6 5.3 %collective-permute-start.8 = (f32[5,48,256]{2,1,0:T(8,128)S(1)}, f32[5,48,256]{2,1,0:T(8,128)S(1)}, u32[]{:S(2)}, u32[]{:S(2)}) collective-permute-start(f32[5,48,256]{2,1,0:T(8,128)S(1)} %get-tuple-element.57), channel_id=1, source_target_pairs={{0,31},{1,0},{2,1},{3,2},{4,3},{5,4},{6,5},{7,6},{8,7},{9,8},{10,9... | collective-permute-start | bytes 737288 | tf_op jit(solution)/shard_map/ppermute | solution.py:41
  102.9 10.7 %shard_map.95 = (f32[5,64,256]{2,1,0:T(8,128)S(1)}, f32[5,64,256]{2,1,0:T(8,128)S(1)}, f32[6,48,256]{2,1,0:T(8,128)S(1)}, f32[2,3,256,256]{3,2,1,0:T(8,128)}) custom-call(s32[17]{0:T(128)S(1)} %fusion.25.s0, f32[904,128]{1,0:T(8,128)S(1)} %collective-permute-done.2.l0, s32[17]{0:T(128)S(1)} %fusion.24.s1, ...), custom_call_target="tpu_custom_call", output_to_operand_aliasing={{3}: (8, {})} | custom-call | flops 8000000000 | bytes 4000000 | tf_op jit(solution)/shard_map/pallas_call | solution.py:371
  113.6 0.1 collective-permute-start.5
  113.7 10.3 %shard_map.96 = (f32[5,64,256]{2,1,0:T(8,128)S(1)}, f32[5,64,256]{2,1,0:T(8,128)S(1)}, f32[6,48,256]{2,1,0:T(8,128)S(1)}, f32[2,3,256,256]{3,2,1,0:T(8,128)}) custom-call(s32[17]{0:T(128)S(1)} %fusion.25.s0, f32[904,128]{1,0:T(8,128)S(1)} %collective-permute-done.2.l0, s32[17]{0:T(128)S(1)} %fusion.24.s1, ...), custom_call_target="tpu_custom_call", output_to_operand_aliasing={{3}: (8, {})} | custom-call | flops 8000000000 | bytes 4000000 | tf_op jit(solution)/shard_map/pallas_call | solution.py:371
  124.0 11.4 %shard_map.97 = (f32[5,80,256]{2,1,0:T(8,128)S(1)}, f32[5,80,256]{2,1,0:T(8,128)S(1)}, f32[6,48,256]{2,1,0:T(8,128)}, f32[2,3,256,256]{3,2,1,0:T(8,128)}) custom-call(s32[17]{0:T(128)S(1)} %fusion.25.s0, f32[904,128]{1,0:T(8,128)S(1)} %collective-permute-done.2.l0, s32[17]{0:T(128)S(1)} %fusion.24.s1, ...), custom_call_target="tpu_custom_call", output_to_operand_aliasing={{3}: (8, {})} | custom-call | flops 8000000000 | bytes 4000000 | tf_op jit(solution)/shard_map/pallas_call | solution.py:371
  135.3 0.1 collective-permute-start.7
  135.4 5.3 %collective-permute-start.11 = (f32[5,80,256]{2,1,0:T(8,128)S(1)}, f32[5,80,256]{2,1,0:T(8,128)S(1)}, u32[]{:S(2)}, u32[]{:S(2)}) collective-permute-start(f32[5,80,256]{2,1,0:T(8,128)S(1)} %get-tuple-element.60), channel_id=1, source_target_pairs={{0,31},{1,0},{2,1},{3,2},{4,3},{5,4},{6,5},{7,6},{8,7},{9,8},{10,9... | collective-permute-start | bytes 1228808 | tf_op jit(solution)/shard_map/ppermute | solution.py:41
  140.8 2.0 %collective-permute-start.6 = (f32[5,64,256]{2,1,0:T(8,128)S(1)}, f32[5,64,256]{2,1,0:T(8,128)S(1)}, u32[]{:S(2)}, u32[]{:S(2)}) collective-permute-start(f32[5,64,256]{2,1,0:T(8,128)S(1)} %get-tuple-element.55), channel_id=1, source_target_pairs={{0,1},{1,2},{2,3},{3,4},{4,5},{5,6},{6,7},{7,8},{8,9},{9,10},{10,1... | collective-permute-start | bytes 983048 | tf_op jit(solution)/shard_map/ppermute | solution.py:41
  142.8 3.4 %collective-permute-start.10 = (f32[5,64,256]{2,1,0:T(8,128)S(1)}, f32[5,64,256]{2,1,0:T(8,128)S(1)}, u32[]{:S(2)}, u32[]{:S(2)}) collective-permute-start(f32[5,64,256]{2,1,0:T(8,128)S(1)} %get-tuple-element.59), channel_id=1, source_target_pairs={{0,31},{1,0},{2,1},{3,2},{4,3},{5,4},{6,5},{7,6},{8,7},{9,8},{10,9... | collective-permute-start | bytes 983048 | tf_op jit(solution)/shard_map/ppermute | solution.py:41
  146.2 1.4 copy-done
  147.6 10.2 %interior.1.refs_0_ = f32[2,19,256,256]{3,2,1,0:T(8,128)} custom-call(f32[2,19,256,256]{3,2,1,0:T(8,128)S(1)} %bitcast.52, f32[2,3,256,256]{3,2,1,0:T(8,128)S(1)} %copy-done), custom_call_target="tpu_custom_call" | custom-call | bytes 25000000 | tf_op jit(solution)/shard_map/interior/pallas_call | solution.py:492
  157.7 3.9 %collective-permute-done.9.refs_6_ = f32[5,64,256]{2,1,0:T(8,128)S(1)} collective-permute-done((f32[5,64,256]{2,1,0:T(8,128)S(1)}, f32[5,64,256]{2,1,0:T(8,128)S(1)}, u32[]{:S(2)}, u32[]{:S(2)}) %collective-permute-start.9) | collective-permute-done | bytes 327712 | tf_op jit(solution)/shard_map/ppermute | solution.py:41
  161.7 1.2 collective-permute-done.6.refs_3_
  162.9 2.3 %collective-permute-done.10.refs_7_ = f32[5,64,256]{2,1,0:T(8,128)S(1)} collective-permute-done((f32[5,64,256]{2,1,0:T(8,128)S(1)}, f32[5,64,256]{2,1,0:T(8,128)S(1)}, u32[]{:S(2)}, u32[]{:S(2)}) %collective-permute-start.10) | collective-permute-done | bytes 327712 | tf_op jit(solution)/shard_map/ppermute | solution.py:41
  165.2 1.5 arrivals.1
  (49 shorter events, 0.4 us)
Async XLA Ops:
  0.6 12.4 %copy-start.1 = (f32[3,2,32,128]{3,2,1,0:T(8,128)S(1)}, f32[3,2,32,128]{3,2,1,0:T(8,128)}, u32[]{:S(2)}) copy-start(f32[3,2,32,128]{3,2,1,0:T(8,128)} %param.7) | copy-start | bytes 294916
  1.5 8.5 %collective-permute-start.1 = (f32[3,2,2,128]{3,2,1,0:T(2,128)S(1)}, f32[3,2,2,128]{3,2,1,0:T(2,128)S(1)}, u32[]{:S(2)}, u32[]{:S(2)}) collective-permute-start(f32[3,2,2,128]{3,2,1,0:T(2,128)S(1)} %get-tuple-element.84), channel_id=1, source_target_pairs={{0,1},{1,2},{2,3},{3,4},{4,5},{5,6},{6,7},{8,9},{9,10},{10,11},{11... | collective-permute-start | bytes 18440 | tf_op jit(solution)/shard_map/ppermute | solution.py:50
  6.3 5.5 %collective-permute-start = (f32[3,2,2,128]{3,2,1,0:T(2,128)S(1)}, f32[3,2,2,128]{3,2,1,0:T(2,128)S(1)}, u32[]{:S(2)}, u32[]{:S(2)}) collective-permute-start(f32[3,2,2,128]{3,2,1,0:T(2,128)S(1)} %get-tuple-element.85), channel_id=1, source_target_pairs={{1,0},{2,1},{3,2},{4,3},{5,4},{6,5},{7,6},{9,8},{10,9},{11,10},{12... | collective-permute-start | bytes 18440 | tf_op jit(solution)/shard_map/ppermute | solution.py:51
  9.1 4.2 %copy-start.4 = (f32[2]{0:T(128)S(1)}, f32[2]{0:T(128)}, u32[]{:S(2)}) copy-start(f32[2]{0:T(128)} %param.9) | copy-start | bytes 28
  9.2 4.2 %copy-start.5 = (f32[2]{0:T(128)S(1)}, f32[2]{0:T(128)}, u32[]{:S(2)}) copy-start(f32[2]{0:T(128)} %param.8) | copy-start | bytes 28
  12.9 0.9 copy-start.3
  13.5 15.5 %copy-start.2 = (f32[3,2,32,128]{3,2,1,0:T(8,128)}, f32[3,2,32,128]{3,2,1,0:T(8,128)S(1)}, u32[]{:S(2)}) copy-start(f32[3,2,32,128]{3,2,1,0:T(8,128)S(1)} %fusion.8) | copy-start | bytes 294916
  29.0 22.0 %all-to-all-start = ((f32[32,7,512]{2,1,0:T(8,128)}), f32[32,7,512]{2,1,0:T(8,128)S(1)}, u32[]{:S(2)}, u32[]{:S(2)}) async-start(f32[32,7,512]{2,1,0:T(8,128)} %stack.3), calls=%async_computation | async-start | bytes 1048576 | tf_op jit(solution)/shard_map/all_to_all | solution.py:568
  65.3 22.4 %slice-start = ((s8[9961472]{0:T(1024)(128)(4,1)}), s8[4194304]{0:T(1024)(128)(4,1)S(1)}, s32[]{:S(2)}) async-start(s8[9961472]{0:T(1024)(128)(4,1)} %bitcast.51), calls=%async_computation.1 | async-start | bytes 8388608
  65.3 22.3 %slice-start.1 = ((s8[9961472]{0:T(1024)(128)(4,1)}), s8[4194304]{0:T(1024)(128)(4,1)S(1)}, s32[]{:S(2)}) async-start(s8[9961472]{0:T(1024)(128)(4,1)} %bitcast.51), calls=%async_computation.2 | async-start | bytes 8388608
  65.4 22.3 %slice-start.2 = ((s8[9961472]{0:T(1024)(128)(4,1)}), s8[1572864]{0:T(1024)(128)(4,1)S(1)}, s32[]{:S(2)}) async-start(s8[9961472]{0:T(1024)(128)(4,1)} %bitcast.51), calls=%async_computation.3 | async-start | bytes 3145728
  65.4 22.3 %collective-permute-start.3 = (f32[904,128]{1,0:T(8,128)S(1)}, f32[904,128]{1,0:T(8,128)S(1)}, u32[]{:S(2)}, u32[]{:S(2)}) collective-permute-start(f32[904,128]{1,0:T(8,128)S(1)} %constant_dynamic-update-slice_fusion.list_ref), channel_id=1, source_target_pairs={{0,31},{1,0},{2,1},{3,2},{4,3},{5,4},{6,5},{7,6},{8,7},{9,8},{10,9... | collective-permute-start | bytes 1388552 | tf_op jit(solution)/shard_map/ppermute | solution.py:41
  66.0 21.6 %collective-permute-start.2 = (f32[904,128]{1,0:T(8,128)S(1)}, f32[904,128]{1,0:T(8,128)S(1)}, u32[]{:S(2)}, u32[]{:S(2)}) collective-permute-start(f32[904,128]{1,0:T(8,128)S(1)} %constant_dynamic-update-slice_fusion.list_ref), channel_id=1, source_target_pairs={{0,1},{1,2},{2,3},{3,4},{4,5},{5,6},{6,7},{7,8},{8,9},{9,10},{10,1... | collective-permute-start | bytes 1388552 | tf_op jit(solution)/shard_map/ppermute | solution.py:41
  97.5 43.2 %collective-permute-start.4 = (f32[5,48,256]{2,1,0:T(8,128)S(1)}, f32[5,48,256]{2,1,0:T(8,128)S(1)}, u32[]{:S(2)}, u32[]{:S(2)}) collective-permute-start(f32[5,48,256]{2,1,0:T(8,128)S(1)} %get-tuple-element.53), channel_id=1, source_target_pairs={{0,1},{1,2},{2,3},{3,4},{4,5},{5,6},{6,7},{7,8},{8,9},{9,10},{10,1... | collective-permute-start | bytes 737288 | tf_op jit(solution)/shard_map/ppermute | solution.py:41
  97.6 43.2 %collective-permute-start.8 = (f32[5,48,256]{2,1,0:T(8,128)S(1)}, f32[5,48,256]{2,1,0:T(8,128)S(1)}, u32[]{:S(2)}, u32[]{:S(2)}) collective-permute-start(f32[5,48,256]{2,1,0:T(8,128)S(1)} %get-tuple-element.57), channel_id=1, source_target_pairs={{0,31},{1,0},{2,1},{3,2},{4,3},{5,4},{6,5},{7,6},{8,7},{9,8},{10,9... | collective-permute-start | bytes 737288 | tf_op jit(solution)/shard_map/ppermute | solution.py:41
  113.6 29.2 %collective-permute-start.5 = (f32[5,64,256]{2,1,0:T(8,128)S(1)}, f32[5,64,256]{2,1,0:T(8,128)S(1)}, u32[]{:S(2)}, u32[]{:S(2)}) collective-permute-start(f32[5,64,256]{2,1,0:T(8,128)S(1)} %get-tuple-element.54), channel_id=1, source_target_pairs={{0,1},{1,2},{2,3},{3,4},{4,5},{5,6},{6,7},{7,8},{8,9},{9,10},{10,1... | collective-permute-start | bytes 983048 | tf_op jit(solution)/shard_map/ppermute | solution.py:41
  135.3 29.8 %collective-permute-start.7 = (f32[5,80,256]{2,1,0:T(8,128)S(1)}, f32[5,80,256]{2,1,0:T(8,128)S(1)}, u32[]{:S(2)}, u32[]{:S(2)}) collective-permute-start(f32[5,80,256]{2,1,0:T(8,128)S(1)} %get-tuple-element.56), channel_id=1, source_target_pairs={{0,1},{1,2},{2,3},{3,4},{4,5},{5,6},{6,7},{7,8},{8,9},{9,10},{10,1... | collective-permute-start | bytes 1228808 | tf_op jit(solution)/shard_map/ppermute | solution.py:41
  135.4 29.8 %collective-permute-start.11 = (f32[5,80,256]{2,1,0:T(8,128)S(1)}, f32[5,80,256]{2,1,0:T(8,128)S(1)}, u32[]{:S(2)}, u32[]{:S(2)}) collective-permute-start(f32[5,80,256]{2,1,0:T(8,128)S(1)} %get-tuple-element.60), channel_id=1, source_target_pairs={{0,31},{1,0},{2,1},{3,2},{4,3},{5,4},{6,5},{7,6},{8,7},{9,8},{10,9... | collective-permute-start | bytes 1228808 | tf_op jit(solution)/shard_map/ppermute | solution.py:41
  140.7 20.9 %collective-permute-start.9 = (f32[5,64,256]{2,1,0:T(8,128)S(1)}, f32[5,64,256]{2,1,0:T(8,128)S(1)}, u32[]{:S(2)}, u32[]{:S(2)}) collective-permute-start(f32[5,64,256]{2,1,0:T(8,128)S(1)} %get-tuple-element.58), channel_id=1, source_target_pairs={{0,31},{1,0},{2,1},{3,2},{4,3},{5,4},{6,5},{7,6},{8,7},{9,8},{10,9... | collective-permute-start | bytes 983048 | tf_op jit(solution)/shard_map/ppermute | solution.py:41
  140.8 22.1 %collective-permute-start.6 = (f32[5,64,256]{2,1,0:T(8,128)S(1)}, f32[5,64,256]{2,1,0:T(8,128)S(1)}, u32[]{:S(2)}, u32[]{:S(2)}) collective-permute-start(f32[5,64,256]{2,1,0:T(8,128)S(1)} %get-tuple-element.55), channel_id=1, source_target_pairs={{0,1},{1,2},{2,3},{3,4},{4,5},{5,6},{6,7},{7,8},{8,9},{9,10},{10,1... | collective-permute-start | bytes 983048 | tf_op jit(solution)/shard_map/ppermute | solution.py:41
  142.8 22.4 %collective-permute-start.10 = (f32[5,64,256]{2,1,0:T(8,128)S(1)}, f32[5,64,256]{2,1,0:T(8,128)S(1)}, u32[]{:S(2)}, u32[]{:S(2)}) collective-permute-start(f32[5,64,256]{2,1,0:T(8,128)S(1)} %get-tuple-element.59), channel_id=1, source_target_pairs={{0,31},{1,0},{2,1},{3,2},{4,3},{5,4},{6,5},{7,6},{8,7},{9,8},{10,9... | collective-permute-start | bytes 983048 | tf_op jit(solution)/shard_map/ppermute | solution.py:41
  146.2 1.4 copy-start

commit v2 on v1

--- a/solution.py
+++ b/solution.py
@@ -41,41 +41,13 @@
     return lax.ppermute(value, axis, pairs)
 
 
-def with_halo(x, axis, dim, width):
+def halos(x, axis, dim, width):
     devices, length = (lax.axis_size(axis), x.shape[dim])
     up = [(i, i + 1) for i in range(devices - 1)]
     down = [(j, i) for i, j in up]
     last = lax.slice_in_dim(x, length - width, length, axis=dim)
     initial = lax.slice_in_dim(x, 0, width, axis=dim)
-    before = lax.ppermute(last, axis, up)
-    after = lax.ppermute(initial, axis, down)
-    return jnp.concatenate([before, x, after], axis=dim)
-
-
-def laplacian(padded):
-    center = padded[:, :, 1:-1]
-    return (
-        padded[:, :, 2:]
-        + padded[:, :, :-2]
-        + jnp.roll(center, 1, 3)
-        + jnp.roll(center, -1, 3)
-        - 4.0 * center
-    )
-
-
-def membrane(displacement, tension, bending):
-    padded = with_halo(displacement, "shard", 2, 2)
-    wide_first = laplacian(padded)
-    rows = wide_first.shape[2]
-    place = lax.broadcasted_iota(jnp.int32, (1, 1, rows, 1), 2)
-    index = lax.axis_index("shard")
-    outside = ((place == 0) & (index == 0)) | (
-        (place == rows - 1) & (index == lax.axis_size("shard") - 1)
-    )
-    wide_first = jnp.where(outside, 0.0, wide_first)
-    second = laplacian(wide_first)
-    first = wide_first[:, :, 1:-1]
-    return tension[None, :, None, None] * first - bending[None, :, None, None] * second
+    return lax.ppermute(last, axis, up), lax.ppermute(initial, axis, down)
 
 
 WINDOW = 16
@@ -541,53 +513,143 @@
     )(new_populations, *lows, *highs)
 
 
-def dispatched(membrane_force, offset, owner, cell, device_count, cells):
-    point_count = owner.size
-    capacity = 2 * point_count // device_count
-    slot_total = device_count * capacity
-    owner = owner.reshape(point_count)
-    cell = cell.reshape(point_count)
+def prepared(displacement, tension, bending, offset, owner, cell, cells, width):
+    before, after = halos(displacement, "shard", 2, 2)
+    _, vesicles, rows, lanes = displacement.shape
+    assert lanes == LANES
+    index = lax.axis_index("shard")
+    outside = jnp.stack(
+        [
+            jnp.where(index == 0, 0, -1),
+            jnp.where(index == lax.axis_size("shard") - 1, rows + 1, -1),
+        ]
+    ).astype(jnp.int32)
+    slab_bits = bits(cells // (width * width))
+
+    def kernel(edge, t_ref, b_ref, x_ref, before_ref, after_ref, o_ref, own_ref, cell_ref, *rest):
+        force_ref, key_ref = rest[:2]
+        values, (padded, wide_ref) = (rest[2:8], rest[8:])
+        place = lax.broadcasted_iota(jnp.int32, (rows + 2, lanes), 0)
+
+        def laplacian(ref, begin, count):
+            center = ref[begin : begin + count, :]
+            return (
+                ref[begin + 1 : begin + count + 1, :]
+                + ref[begin - 1 : begin + count - 1, :]
+                + pltpu.roll(center, 1, 1)
+                + pltpu.roll(center, lanes - 1, 1)
+                - 4.0 * center
+            )
+
+        for v in range(vesicles):
+            at = slice(v * rows, (v + 1) * rows)
+            code = cell_ref[v]
+            plane, x, y = (
+                code >> (2 * bits(width)),
+                (code >> bits(width)) & (width - 1),
+                code & (width - 1),
+            )
+            x = (x + LAG) & (width - 1)
+            key_ref[at, :] = own_ref[v] * cells + (
+                (x << (bits(width) + slab_bits)) | (plane << bits(width)) | y
+            )
+            for c in range(3):
+                values[3 + c][at, :] = o_ref[c, v]
+                padded[6:8, :] = before_ref[c, v]
+                padded[8 : 8 + rows, :] = x_ref[c, v]
+                padded[8 + rows : 10 + rows, :] = after_ref[c, v]
+                wide = laplacian(padded, 7, rows + 2)
+                hidden = (place == edge[0]) | (place == edge[1])
+                wide_ref[7 : 9 + rows, :] = jnp.where(hidden, 0.0, wide)
+                second = laplacian(wide_ref, 8, rows)
+                force = t_ref[v] * wide_ref[8 : 8 + rows, :] - b_ref[v] * second
+                force_ref[c, v] = force
+                values[c][at, :] = force
+
+    shape = jax.ShapeDtypeStruct
+    flat = (vesicles * rows, lanes)
+    out = pl.pallas_call(
+        kernel,
+        out_shape=(shape(displacement.shape, jnp.float32), shape(flat, jnp.int32))
+        + (shape(flat, jnp.float32),) * 6,
+        in_specs=[SMEM] * 3 + [VMEM] * 6,
+        out_specs=(VMEM,) * 8,
+        scratch_shapes=[pltpu.VMEM((rows + 16, lanes), jnp.float32)] * 2,
+        compiler_params=pltpu.CompilerParams(vmem_limit_bytes=8 * MIB),
+        name="prepared",
+    )(outside, tension, bending, displacement, before, after, offset, owner, cell)
+    return out[0], out[1], out[2:]
+
+
+def packed(starts, columns, device_count, capacity, cells):
+    count = columns[0].shape[0]
+    lanes = min(capacity, LANES)
+    tiles = capacity // lanes
+
+    def kernel(start_ref, *refs):
+        columns, out, table = (refs[:7], refs[7], refs[8])
+        for i in range(7):
+            table[0:count, i, :] = columns[i][...].astype(jnp.float32)
+        field = lax.broadcasted_iota(jnp.int32, (7, LANES), 0)
+        lane = lax.broadcasted_iota(jnp.int32, (7, LANES), 1)
+        for r in range(tiles + 1):
+            table[count + r] = jnp.where(field == 0, float(device_count * cells), 0.0)
+
+        @pl.loop(0, device_count)
+        def _(d):
+            row, shift = (start_ref[d] // LANES, start_ref[d] % LANES)
+            turned = [
+                pltpu.roll(table[row + j], (LANES - shift) % LANES, 1) for j in range(tiles + 1)
+            ]
+            before = (d * cells).astype(jnp.float32)
+            for j in range(tiles):
+                value = jnp.where(lane < LANES - shift, turned[j], turned[j + 1])
+                tag = jnp.minimum(value - before, float(cells))
+                out[d, j] = jnp.where(field == 0, tag, value)[:, :lanes]
+
+    return pl.pallas_call(
+        kernel,
+        out_shape=jax.ShapeDtypeStruct((device_count, tiles, 7, lanes), jnp.float32),
+        in_specs=[SMEM] + [VMEM] * 7,
+        out_specs=VMEM,
+        scratch_shapes=[pltpu.VMEM((count + tiles + 1, 7, LANES), jnp.float32)],
+        compiler_params=pltpu.CompilerParams(vmem_limit_bytes=8 * MIB),
+        name="packed",
+    )(starts, *columns)
+
+
+def dispatched(key, values, owner, device_count, cells):
+    capacity = 2 * owner.size // device_count
     devices = jnp.arange(device_count, dtype=jnp.int32)
-    counts = jnp.sum((owner[None, :] == devices[:, None]).astype(jnp.int32), 1)
-    filler_ends = jnp.cumsum(capacity - counts)
-    filler = jnp.arange(slot_total - point_count, dtype=jnp.int32)
-    filler_owner = jnp.sum((filler[None, :] >= filler_ends[:, None]).astype(jnp.int32), 0)
-    span = 2 * cells
-    key = jnp.concatenate([owner * span + cell, filler_owner * span + cells])
-    payload = jnp.concatenate(
-        [membrane_force.reshape(3, point_count), offset.reshape(3, point_count)], 0
+    starts = jnp.sum((owner.reshape(-1)[None, :] < devices[:, None]).astype(jnp.int32), 1)
+    ordered = lax.sort(
+        (key.reshape(-1),) + tuple(v.reshape(-1) for v in values), num_keys=1, is_stable=False
     )
-    payload = jnp.pad(payload, ((0, 0), (0, slot_total - point_count)))
-    ordered = lax.sort(
-        (key,) + tuple(payload[i] for i in range(6)), num_keys=1, is_stable=False
+    send = packed(
+        starts, [v.reshape(-1, LANES) for v in ordered], device_count, capacity, cells
     )
-    tag = (ordered[0] % span).astype(jnp.float32)
-    send = jnp.stack(
-        [v.reshape(device_count, capacity) for v in list(ordered[1:]) + [tag]], 1
-    )
-    got = lax.all_to_all(send, ("ves", "shard"), split_axis=0, concat_axis=0, tiled=True)
-    return got.transpose(1, 0, 2).reshape(7, slot_total)
+    return lax.all_to_all(send, ("ves", "shard"), split_axis=0, concat_axis=0, tiled=True)
 
 
 CUTS = (0, 4, 8, 12, 16)
 
 
 def one_step(displacement, tension, bending, offset, owner, cell, populations):
-    membrane_force = membrane(displacement, tension, bending)
     device_count = lax.axis_size("ves") * lax.axis_size("shard")
     slab, width = (populations.shape[0], populations.shape[2])
     cells = slab * width * width
     windows = width // WINDOW
-    got = dispatched(membrane_force, offset, owner, cell, device_count, cells)
-    tag = got[6].astype(jnp.int32)
-    plane, x, y = (tag // (width * width), tag // width % width, tag % width)
-    x = (x + LAG) & (width - 1)
     x_bit = bits(slab) + bits(width)
-    key = jnp.where(tag >= cells, width << x_bit, (x << x_bit) | (plane << bits(width)) | y)
+    membrane_force, key, values = prepared(
+        displacement, tension, bending, offset, owner, cell, cells, width
+    )
+    got = dispatched(key, values, owner, device_count, cells)
+    got = [got[:, :, i, :].reshape(-1) for i in range(7)]
+    key = got[0].astype(jnp.int32)
     bounds = jnp.arange(windows + 1, dtype=jnp.int32) * (WINDOW << x_bit)
     starts = jnp.sum((key[None, :] < bounds[:, None]).astype(jnp.float32), 1)
     ordered = lax.sort(
-        (key,) + tuple(got[i] for i in range(6)), num_keys=1, is_stable=False
+        (key,) + tuple(got[1:]), num_keys=1, is_stable=False
     )
     columns = list(ordered[1:]) + [ordered[0].astype(jnp.float32)]
     starts = jnp.pad(starts, (0, LANES - windows - 1))

time: 167 us -> 165 us (0.988)
  other arithmetic: 31 us -> 20.7 us
  Pallas kernels: 60.8 us -> 65.4 us
  waiting for transfers between devices: 38.7 us -> 35.5 us
  starting transfers between devices: 30.3 us -> 33.5 us
  local copies, waits for them, and re-layouts: 4.88 us -> 7.8 us
    sort x2, other arithmetic: 26.6 us -> 19.2 us  [the longest x1 13.1 us: one_step(): ordered = lax.sort((key,) + tuple(got[1:]), num_keys=1, is_stable=False)]
    pallas_call x0 -> x2, Pallas kernels: none -> 4.62 us  [the longest x1 3.18 us: packed(): pl.pallas_call(kernel, out_shape=jax.ShapeDtypeStruct((device_count, tile...]
    unnamed x24 -> x26, local copies, waits for them, and re-layouts: 1.75 us -> 6.08 us
    all_to_all x1, starting transfers between devices: 5.74 us -> 8.13 us  [dispatched(): lax.all_to_all(send, ('ves', 'shard'), split_axis=0, concat_axis=0, tiled...]
where the time goes in v2:
time: 165 us; the launch traced here: 164 us
  Pallas kernels  65.4 us (40%)
  waiting for transfers between devices  35.5 us (22%)
  starting transfers between devices  33.5 us (20%)
  other arithmetic  20.7 us (13%)
  local copies, waits for them, and re-layouts  7.8 us (5%)
    pallas_call x4, Pallas kernels, spread_chunk(): pl.pallas_call(kernel, out_shape=(shape((5, n, width), jnp.float32), shap...  42.1 us
    ppermute x10, waiting for transfers between devices, passed_along(): return lax.ppermute(value, axis, pairs)  20.6 us
    ppermute x10, starting transfers between devices, passed_along(): return lax.ppermute(value, axis, pairs)  18.6 us
    all_to_all x1, waiting for transfers between devices, dispatched(): lax.all_to_all(send, ('ves', 'shard'), split_axis=0, concat_axis=0, tiled...  14.6 us
    sort x1, other arithmetic, one_step(): ordered = lax.sort((key,) + tuple(got[1:]), num_keys=1, is_stable=False)  13.1 us
    pallas_call x1, Pallas kernels, interior(): pl.pallas_call(kernel, out_shape=jax.ShapeDtypeStruct(populations.shape,...  10.2 us
    all_to_all x1, starting transfers between devices, dispatched(): lax.all_to_all(send, ('ves', 'shard'), split_axis=0, concat_axis=0, tiled...  8.13 us
    pallas_call x1, Pallas kernels, spread_own(): pl.pallas_call(kernel, out_shape=jax.ShapeDtypeStruct((slab * 3, width +...  7.04 us
  transfers between devices with their start and end apart: 13, of which 6 were waited for; matrix products, arithmetic and copies ran while one was open for 1% of the time, Pallas kernels for 30%

profile of v2, /device:TPU:0, one launch (start us, length us, event | category | flops | bytes accessed | tf_op | source)
XLA Modules:
  0.0 164.1 jit_solution(14138959917489484512)
XLA Ops:
  0.6 0.8 fusion.4
  1.4 1.3 collective-permute-start.1
  2.7 5.5 %collective-permute-start = (f32[3,2,2,128]{3,2,1,0:T(2,128)S(1)}, f32[3,2,2,128]{3,2,1,0:T(2,128)S(1)}, u32[]{:S(2)}, u32[]{:S(2)}) collective-permute-start(f32[3,2,2,128]{3,2,1,0:T(2,128)S(1)} %get-tuple-element.87), channel_id=1, source_target_pairs={{0,1},{1,2},{2,3},{3,4},{4,5},{5,6},{6,7},{8,9},{9,10},{10,11},{11... | collective-permute-start | bytes 18440 | tf_op jit(solution)/shard_map/ppermute | solution.py:50
  8.2 1.0 convert_reduce_fusion.1.start_ref
  9.2 0.1 pad_add_fusion.edge
  9.3 0.0 collective-permute-done.1.after_ref
  9.3 0.3 collective-permute-done.before_ref
  9.5 0.8 copy-done.1
  10.3 0.9 copy-done.2
  11.2 0.9 copy-done.3
  12.1 0.8 copy-done.4
  12.9 0.7 copy-done.5
  13.5 0.7 copy-done.6
  14.2 1.4 prepared.1
  15.6 6.0 %sort.90 = (s32[8192]{0:T(1024)S(1)}, f32[8192]{0:T(1024)S(1)}, f32[8192]{0:T(1024)S(1)}, f32[8192]{0:T(1024)S(1)}, f32[8192]{0:T(1024)S(1)}, /*index=5*/f32[8192]{0:T(1024)S(1)}, f32[8192]{0:T(1024)S(1)}) sort(s32[8192]{0:T(1024)S(1)} %bitcast.45, f32[8192]{0:T(1024)S(1)} %bitcast.46, f32[8192]{0:T(1024)S(1)} %bitcast.47, f32[8192]{0:T(1024)S(1)} %bitcast.48, ...), dimensions={0}, to_apply=%region_1.2 | sort | flops 106496 | bytes 458752 | tf_op jit(solution)/shard_map/sort | solution.py:625
  21.6 3.2 %packed.1 = f32[32,4,7,128]{3,2,1,0:T(8,128)S(1)} custom-call(s32[32]{0:T(128)S(1)} %convert_reduce_fusion.1.start_ref, s32[64,128]{1,0:T(8,128)S(1)} %bitcast.52, f32[64,128]{1,0:T(8,128)S(1)} %bitcast.53, f32[64,128]{1,0:T(8,128)S(1)} %bitcast.54, f32[64,128]{1,0:T(8,128)S(1)} %bitcast.55, f32[64,128]{1,0:T(8,128)S(1)} %bitcast.56, ...), custom_call_target="tpu_custom_call" | custom-call | tf_op jit(solution)/shard_map/packed/pallas_call | solution.py:610
  24.8 0.9 copy.15
  25.7 8.1 %all-to-all-start = ((f32[32,4,7,128]{3,1,2,0:T(4,128)}), f32[32,4,7,128]{3,1,2,0:T(4,128)S(1)}, u32[]{:S(2)}, u32[]{:S(2)}) async-start(f32[32,4,7,128]{3,1,2,0:T(4,128)} %copy.15), calls=%async_computation | async-start | bytes 917504 | tf_op jit(solution)/shard_map/all_to_all | solution.py:631
  33.9 14.6 %all-to-all-done = f32[32,4,7,128]{3,1,2,0:T(4,128)S(1)} async-done(((f32[32,4,7,128]{3,1,2,0:T(4,128)}), f32[32,4,7,128]{3,1,2,0:T(4,128)S(1)}, u32[]{:S(2)}, u32[]{:S(2)}) %all-to-all-start) | async-done | bytes 458784 | tf_op jit(solution)/shard_map/all_to_all | solution.py:631
  48.5 0.1 fusion.2
  48.6 0.4 convert_reduce_fusion
  49.0 13.1 %sort.91 = (s32[16384]{0:T(1024)S(1)}, f32[16384]{0:T(1024)S(1)}, f32[16384]{0:T(1024)S(1)}, f32[16384]{0:T(1024)S(1)}, f32[16384]{0:T(1024)S(1)}, /*index=5*/f32[16384]{0:T(1024)S(1)}, f32[16384]{0:T(1024)S(1)}) sort(s32[16384]{0:T(1024)S(1)} %bitcast.60, f32[16384]{0:T(1024)S(1)} %bitcast.66, f32[16384]{0:T(1024)S(1)} %bitcast.65, f32[16384]{0:T(1024)S(1)} %bitcast.64, ...), dimensions={0}, to_apply=%region_2.3 | sort | flops 229376 | bytes 917504 | tf_op jit(solution)/shard_map/sort | solution.py:651
  62.3 0.0 slice-start
  62.3 0.0 slice-start.1
  62.3 0.0 slice-start.2
  62.3 1.3 collective-permute-start.3
  63.6 1.0 collective-permute-start.2
  64.6 7.0 %spread_own.1.total_ref = f32[6,264,256]{2,1,0:T(8,128)S(1)} custom-call(s32[17]{0:T(128)S(1)} %convert_element_type.49.starts, f32[904,128]{1,0:T(8,128)S(1)} %constant_dynamic-update-slice_fusion.list_ref), custom_call_target="tpu_custom_call" | custom-call | flops 20000000000 | bytes 4000000 | tf_op jit(solution)/shard_map/spread_own/pallas_call | solution.py:188
  71.6 13.1 %collective-permute-done.3.l1 = f32[904,128]{1,0:T(8,128)S(1)} collective-permute-done((f32[904,128]{1,0:T(8,128)S(1)}, f32[904,128]{1,0:T(8,128)S(1)}, u32[]{:S(2)}, u32[]{:S(2)}) %collective-permute-start.3) | collective-permute-done | bytes 462880 | tf_op jit(solution)/shard_map/ppermute | solution.py:41
  84.8 0.0 collective-permute-done.2.l0
  84.9 9.7 %shard_map.94 = (f32[5,48,256]{2,1,0:T(8,128)S(1)}, f32[5,48,256]{2,1,0:T(8,128)S(1)}, f32[6,48,256]{2,1,0:T(8,128)S(1)}, f32[2,3,256,256]{3,2,1,0:T(8,128)}) custom-call(s32[17]{0:T(128)S(1)} %fusion.1.s0, f32[904,128]{1,0:T(8,128)S(1)} %collective-permute-done.2.l0, s32[17]{0:T(128)S(1)} %fusion.s1, f32[904,128]{1,0:T(8,128)S(1)} %collective-permute-done.3.l1, ...), custom_call_target="tpu_custom_call" | custom-call | flops 8000000000 | bytes 4000000 | tf_op jit(solution)/shard_map/pallas_call | solution.py:343
  94.6 0.1 collective-permute-start.4
  94.7 5.3 %collective-permute-start.8 = (f32[5,48,256]{2,1,0:T(8,128)S(1)}, f32[5,48,256]{2,1,0:T(8,128)S(1)}, u32[]{:S(2)}, u32[]{:S(2)}) collective-permute-start(f32[5,48,256]{2,1,0:T(8,128)S(1)} %get-tuple-element.73), channel_id=1, source_target_pairs={{0,31},{1,0},{2,1},{3,2},{4,3},{5,4},{6,5},{7,6},{8,7},{9,8},{10,9... | collective-permute-start | bytes 737288 | tf_op jit(solution)/shard_map/ppermute | solution.py:41
  100.0 10.7 %shard_map.95 = (f32[5,64,256]{2,1,0:T(8,128)S(1)}, f32[5,64,256]{2,1,0:T(8,128)S(1)}, f32[6,48,256]{2,1,0:T(8,128)S(1)}, f32[2,3,256,256]{3,2,1,0:T(8,128)}) custom-call(s32[17]{0:T(128)S(1)} %fusion.1.s0, f32[904,128]{1,0:T(8,128)S(1)} %collective-permute-done.2.l0, s32[17]{0:T(128)S(1)} %fusion.s1, ...), custom_call_target="tpu_custom_call", output_to_operand_aliasing={{3}: (8, {})} | custom-call | flops 8000000000 | bytes 4000000 | tf_op jit(solution)/shard_map/pallas_call | solution.py:343
  110.7 0.1 collective-permute-start.5
  110.8 10.3 %shard_map.96 = (f32[5,64,256]{2,1,0:T(8,128)S(1)}, f32[5,64,256]{2,1,0:T(8,128)S(1)}, f32[6,48,256]{2,1,0:T(8,128)S(1)}, f32[2,3,256,256]{3,2,1,0:T(8,128)}) custom-call(s32[17]{0:T(128)S(1)} %fusion.1.s0, f32[904,128]{1,0:T(8,128)S(1)} %collective-permute-done.2.l0, s32[17]{0:T(128)S(1)} %fusion.s1, ...), custom_call_target="tpu_custom_call", output_to_operand_aliasing={{3}: (8, {})} | custom-call | flops 8000000000 | bytes 4000000 | tf_op jit(solution)/shard_map/pallas_call | solution.py:343
  121.1 11.4 %shard_map.97 = (f32[5,80,256]{2,1,0:T(8,128)S(1)}, f32[5,80,256]{2,1,0:T(8,128)S(1)}, f32[6,48,256]{2,1,0:T(8,128)}, f32[2,3,256,256]{3,2,1,0:T(8,128)}) custom-call(s32[17]{0:T(128)S(1)} %fusion.1.s0, f32[904,128]{1,0:T(8,128)S(1)} %collective-permute-done.2.l0, s32[17]{0:T(128)S(1)} %fusion.s1, ...), custom_call_target="tpu_custom_call", output_to_operand_aliasing={{3}: (8, {})} | custom-call | flops 8000000000 | bytes 4000000 | tf_op jit(solution)/shard_map/pallas_call | solution.py:343
  132.5 0.1 collective-permute-start.7
  132.6 5.3 %collective-permute-start.11 = (f32[5,80,256]{2,1,0:T(8,128)S(1)}, f32[5,80,256]{2,1,0:T(8,128)S(1)}, u32[]{:S(2)}, u32[]{:S(2)}) collective-permute-start(f32[5,80,256]{2,1,0:T(8,128)S(1)} %get-tuple-element.76), channel_id=1, source_target_pairs={{0,31},{1,0},{2,1},{3,2},{4,3},{5,4},{6,5},{7,6},{8,7},{9,8},{10,9... | collective-permute-start | bytes 1228808 | tf_op jit(solution)/shard_map/ppermute | solution.py:41
  137.9 0.0 collective-permute-start.9
  137.9 2.0 %collective-permute-start.6 = (f32[5,64,256]{2,1,0:T(8,128)S(1)}, f32[5,64,256]{2,1,0:T(8,128)S(1)}, u32[]{:S(2)}, u32[]{:S(2)}) collective-permute-start(f32[5,64,256]{2,1,0:T(8,128)S(1)} %get-tuple-element.71), channel_id=1, source_target_pairs={{0,1},{1,2},{2,3},{3,4},{4,5},{5,6},{6,7},{7,8},{8,9},{9,10},{10,1... | collective-permute-start | bytes 983048 | tf_op jit(solution)/shard_map/ppermute | solution.py:41
  139.9 3.4 %collective-permute-start.10 = (f32[5,64,256]{2,1,0:T(8,128)S(1)}, f32[5,64,256]{2,1,0:T(8,128)S(1)}, u32[]{:S(2)}, u32[]{:S(2)}) collective-permute-start(f32[5,64,256]{2,1,0:T(8,128)S(1)} %get-tuple-element.75), channel_id=1, source_target_pairs={{0,31},{1,0},{2,1},{3,2},{4,3},{5,4},{6,5},{7,6},{8,7},{9,8},{10,9... | collective-permute-start | bytes 983048 | tf_op jit(solution)/shard_map/ppermute | solution.py:41
  143.3 1.4 copy-done
  144.7 10.2 %interior.1.refs_0_ = f32[2,19,256,256]{3,2,1,0:T(8,128)} custom-call(f32[2,19,256,256]{3,2,1,0:T(8,128)S(1)} %bitcast.43, f32[2,3,256,256]{3,2,1,0:T(8,128)S(1)} %copy-done), custom_call_target="tpu_custom_call" | custom-call | bytes 25000000 | tf_op jit(solution)/shard_map/interior/pallas_call | solution.py:464
  154.9 4.0 %collective-permute-done.9.refs_6_ = f32[5,64,256]{2,1,0:T(8,128)S(1)} collective-permute-done((f32[5,64,256]{2,1,0:T(8,128)S(1)}, f32[5,64,256]{2,1,0:T(8,128)S(1)}, u32[]{:S(2)}, u32[]{:S(2)}) %collective-permute-start.9) | collective-permute-done | bytes 327712 | tf_op jit(solution)/shard_map/ppermute | solution.py:41
  158.8 1.2 collective-permute-done.6.refs_3_
  160.1 2.3 %collective-permute-done.10.refs_7_ = f32[5,64,256]{2,1,0:T(8,128)S(1)} collective-permute-done((f32[5,64,256]{2,1,0:T(8,128)S(1)}, f32[5,64,256]{2,1,0:T(8,128)S(1)}, u32[]{:S(2)}, u32[]{:S(2)}) %collective-permute-start.10) | collective-permute-done | bytes 327712 | tf_op jit(solution)/shard_map/ppermute | solution.py:41
  162.3 1.5 arrivals.1
  (34 shorter events, 0.2 us)
Async XLA Ops:
  1.4 7.9 %collective-permute-start.1 = (f32[3,2,2,128]{3,2,1,0:T(2,128)S(1)}, f32[3,2,2,128]{3,2,1,0:T(2,128)S(1)}, u32[]{:S(2)}, u32[]{:S(2)}) collective-permute-start(f32[3,2,2,128]{3,2,1,0:T(2,128)S(1)} %get-tuple-element.86), channel_id=1, source_target_pairs={{1,0},{2,1},{3,2},{4,3},{5,4},{6,5},{7,6},{9,8},{10,9},{11,10},{12... | collective-permute-start | bytes 18440 | tf_op jit(solution)/shard_map/ppermute | solution.py:50
  2.7 6.9 %collective-permute-start = (f32[3,2,2,128]{3,2,1,0:T(2,128)S(1)}, f32[3,2,2,128]{3,2,1,0:T(2,128)S(1)}, u32[]{:S(2)}, u32[]{:S(2)}) collective-permute-start(f32[3,2,2,128]{3,2,1,0:T(2,128)S(1)} %get-tuple-element.87), channel_id=1, source_target_pairs={{0,1},{1,2},{2,3},{3,4},{4,5},{5,6},{6,7},{8,9},{9,10},{10,11},{11... | collective-permute-start | bytes 18440 | tf_op jit(solution)/shard_map/ppermute | solution.py:50
  9.5 0.8 copy-start.1
  10.3 0.9 copy-start.2
  11.2 0.9 copy-start.3
  12.1 0.8 copy-start.4
  12.8 0.7 copy-start.5
  13.5 0.7 copy-start.6
  25.7 22.8 %all-to-all-start = ((f32[32,4,7,128]{3,1,2,0:T(4,128)}), f32[32,4,7,128]{3,1,2,0:T(4,128)S(1)}, u32[]{:S(2)}, u32[]{:S(2)}) async-start(f32[32,4,7,128]{3,1,2,0:T(4,128)} %copy.15), calls=%async_computation | async-start | bytes 917504 | tf_op jit(solution)/shard_map/all_to_all | solution.py:631
  62.3 22.6 %slice-start = ((s8[9961472]{0:T(1024)(128)(4,1)}), s8[4194304]{0:T(1024)(128)(4,1)S(1)}, s32[]{:S(2)}) async-start(s8[9961472]{0:T(1024)(128)(4,1)} %bitcast.42), calls=%async_computation.1 | async-start | bytes 8388608
  62.3 22.6 %slice-start.1 = ((s8[9961472]{0:T(1024)(128)(4,1)}), s8[4194304]{0:T(1024)(128)(4,1)S(1)}, s32[]{:S(2)}) async-start(s8[9961472]{0:T(1024)(128)(4,1)} %bitcast.42), calls=%async_computation.2 | async-start | bytes 8388608
  62.3 22.6 %slice-start.2 = ((s8[9961472]{0:T(1024)(128)(4,1)}), s8[1572864]{0:T(1024)(128)(4,1)S(1)}, s32[]{:S(2)}) async-start(s8[9961472]{0:T(1024)(128)(4,1)} %bitcast.42), calls=%async_computation.3 | async-start | bytes 3145728
  62.3 22.5 %collective-permute-start.3 = (f32[904,128]{1,0:T(8,128)S(1)}, f32[904,128]{1,0:T(8,128)S(1)}, u32[]{:S(2)}, u32[]{:S(2)}) collective-permute-start(f32[904,128]{1,0:T(8,128)S(1)} %constant_dynamic-update-slice_fusion.list_ref), channel_id=1, source_target_pairs={{0,31},{1,0},{2,1},{3,2},{4,3},{5,4},{6,5},{7,6},{8,7},{9,8},{10,9... | collective-permute-start | bytes 1388552 | tf_op jit(solution)/shard_map/ppermute | solution.py:41
  63.6 21.2 %collective-permute-start.2 = (f32[904,128]{1,0:T(8,128)S(1)}, f32[904,128]{1,0:T(8,128)S(1)}, u32[]{:S(2)}, u32[]{:S(2)}) collective-permute-start(f32[904,128]{1,0:T(8,128)S(1)} %constant_dynamic-update-slice_fusion.list_ref), channel_id=1, source_target_pairs={{0,1},{1,2},{2,3},{3,4},{4,5},{5,6},{6,7},{7,8},{8,9},{9,10},{10,1... | collective-permute-start | bytes 1388552 | tf_op jit(solution)/shard_map/ppermute | solution.py:41
  94.6 43.2 %collective-permute-start.4 = (f32[5,48,256]{2,1,0:T(8,128)S(1)}, f32[5,48,256]{2,1,0:T(8,128)S(1)}, u32[]{:S(2)}, u32[]{:S(2)}) collective-permute-start(f32[5,48,256]{2,1,0:T(8,128)S(1)} %get-tuple-element.69), channel_id=1, source_target_pairs={{0,1},{1,2},{2,3},{3,4},{4,5},{5,6},{6,7},{7,8},{8,9},{9,10},{10,1... | collective-permute-start | bytes 737288 | tf_op jit(solution)/shard_map/ppermute | solution.py:41
  94.7 43.2 %collective-permute-start.8 = (f32[5,48,256]{2,1,0:T(8,128)S(1)}, f32[5,48,256]{2,1,0:T(8,128)S(1)}, u32[]{:S(2)}, u32[]{:S(2)}) collective-permute-start(f32[5,48,256]{2,1,0:T(8,128)S(1)} %get-tuple-element.73), channel_id=1, source_target_pairs={{0,31},{1,0},{2,1},{3,2},{4,3},{5,4},{6,5},{7,6},{8,7},{9,8},{10,9... | collective-permute-start | bytes 737288 | tf_op jit(solution)/shard_map/ppermute | solution.py:41
  110.7 29.2 %collective-permute-start.5 = (f32[5,64,256]{2,1,0:T(8,128)S(1)}, f32[5,64,256]{2,1,0:T(8,128)S(1)}, u32[]{:S(2)}, u32[]{:S(2)}) collective-permute-start(f32[5,64,256]{2,1,0:T(8,128)S(1)} %get-tuple-element.70), channel_id=1, source_target_pairs={{0,1},{1,2},{2,3},{3,4},{4,5},{5,6},{6,7},{7,8},{8,9},{9,10},{10,1... | collective-permute-start | bytes 983048 | tf_op jit(solution)/shard_map/ppermute | solution.py:41
  132.5 29.9 %collective-permute-start.7 = (f32[5,80,256]{2,1,0:T(8,128)S(1)}, f32[5,80,256]{2,1,0:T(8,128)S(1)}, u32[]{:S(2)}, u32[]{:S(2)}) collective-permute-start(f32[5,80,256]{2,1,0:T(8,128)S(1)} %get-tuple-element.72), channel_id=1, source_target_pairs={{0,1},{1,2},{2,3},{3,4},{4,5},{5,6},{6,7},{7,8},{8,9},{9,10},{10,1... | collective-permute-start | bytes 1228808 | tf_op jit(solution)/shard_map/ppermute | solution.py:41
  132.6 29.8 %collective-permute-start.11 = (f32[5,80,256]{2,1,0:T(8,128)S(1)}, f32[5,80,256]{2,1,0:T(8,128)S(1)}, u32[]{:S(2)}, u32[]{:S(2)}) collective-permute-start(f32[5,80,256]{2,1,0:T(8,128)S(1)} %get-tuple-element.76), channel_id=1, source_target_pairs={{0,31},{1,0},{2,1},{3,2},{4,3},{5,4},{6,5},{7,6},{8,7},{9,8},{10,9... | collective-permute-start | bytes 1228808 | tf_op jit(solution)/shard_map/ppermute | solution.py:41
  137.9 20.9 %collective-permute-start.9 = (f32[5,64,256]{2,1,0:T(8,128)S(1)}, f32[5,64,256]{2,1,0:T(8,128)S(1)}, u32[]{:S(2)}, u32[]{:S(2)}) collective-permute-start(f32[5,64,256]{2,1,0:T(8,128)S(1)} %get-tuple-element.74), channel_id=1, source_target_pairs={{0,31},{1,0},{2,1},{3,2},{4,3},{5,4},{6,5},{7,6},{8,7},{9,8},{10,9... | collective-permute-start | bytes 983048 | tf_op jit(solution)/shard_map/ppermute | solution.py:41
  137.9 22.2 %collective-permute-start.6 = (f32[5,64,256]{2,1,0:T(8,128)S(1)}, f32[5,64,256]{2,1,0:T(8,128)S(1)}, u32[]{:S(2)}, u32[]{:S(2)}) collective-permute-start(f32[5,64,256]{2,1,0:T(8,128)S(1)} %get-tuple-element.71), channel_id=1, source_target_pairs={{0,1},{1,2},{2,3},{3,4},{4,5},{5,6},{6,7},{7,8},{8,9},{9,10},{10,1... | collective-permute-start | bytes 983048 | tf_op jit(solution)/shard_map/ppermute | solution.py:41
  139.9 22.4 %collective-permute-start.10 = (f32[5,64,256]{2,1,0:T(8,128)S(1)}, f32[5,64,256]{2,1,0:T(8,128)S(1)}, u32[]{:S(2)}, u32[]{:S(2)}) collective-permute-start(f32[5,64,256]{2,1,0:T(8,128)S(1)} %get-tuple-element.75), channel_id=1, source_target_pairs={{0,31},{1,0},{2,1},{3,2},{4,3},{5,4},{6,5},{7,6},{8,7},{9,8},{10,9... | collective-permute-start | bytes 983048 | tf_op jit(solution)/shard_map/ppermute | solution.py:41
  143.3 1.4 copy-start

commit v3 on v2

--- a/solution.py
+++ b/solution.py
@@ -575,7 +575,6 @@
         in_specs=[SMEM] * 3 + [VMEM] * 6,
         out_specs=(VMEM,) * 8,
         scratch_shapes=[pltpu.VMEM((rows + 16, lanes), jnp.float32)] * 2,
-        compiler_params=pltpu.CompilerParams(vmem_limit_bytes=8 * MIB),
         name="prepared",
     )(outside, tension, bending, displacement, before, after, offset, owner, cell)
     return out[0], out[1], out[2:]
@@ -595,7 +594,7 @@
         for r in range(tiles + 1):
             table[count + r] = jnp.where(field == 0, float(device_count * cells), 0.0)
 
-        @pl.loop(0, device_count)
+        @pl.loop(0, device_count, unroll=4)
         def _(d):
             row, shift = (start_ref[d] // LANES, start_ref[d] % LANES)
             turned = [
@@ -605,11 +604,11 @@
             for j in range(tiles):
                 value = jnp.where(lane < LANES - shift, turned[j], turned[j + 1])
                 tag = jnp.minimum(value - before, float(cells))
-                out[d, j] = jnp.where(field == 0, tag, value)[:, :lanes]
+                out[d, :, j, :] = jnp.where(field == 0, tag, value)[:, :lanes]
 
     return pl.pallas_call(
         kernel,
-        out_shape=jax.ShapeDtypeStruct((device_count, tiles, 7, lanes), jnp.float32),
+        out_shape=jax.ShapeDtypeStruct((device_count, 7, tiles, lanes), jnp.float32),
         in_specs=[SMEM] + [VMEM] * 7,
         out_specs=VMEM,
         scratch_shapes=[pltpu.VMEM((count + tiles + 1, 7, LANES), jnp.float32)],
@@ -631,7 +630,7 @@
     return lax.all_to_all(send, ("ves", "shard"), split_axis=0, concat_axis=0, tiled=True)
 
 
-CUTS = (0, 4, 8, 12, 16)
+CUTS = (0, 3, 6, 11, 16)
 
 
 def one_step(displacement, tension, bending, offset, owner, cell, populations):
@@ -644,7 +643,7 @@
         displacement, tension, bending, offset, owner, cell, cells, width
     )
     got = dispatched(key, values, owner, device_count, cells)
-    got = [got[:, :, i, :].reshape(-1) for i in range(7)]
+    got = [got[:, i].reshape(-1) for i in range(7)]
     key = got[0].astype(jnp.int32)
     bounds = jnp.arange(windows + 1, dtype=jnp.int32) * (WINDOW << x_bit)
     starts = jnp.sum((key[None, :] < bounds[:, None]).astype(jnp.float32), 1)

time: 165 us -> 166 us (level)
  waiting for transfers between devices: 35.5 us -> 40.5 us
  local copies, waits for them, and re-layouts: 7.8 us -> 3.47 us
    ppermute x10, waiting for transfers between devices: 20.6 us -> 25.9 us  [passed_along(): return lax.ppermute(value, axis, pairs)]
    unnamed x26 -> x18, local copies, waits for them, and re-layouts: 6.08 us -> 2.64 us
  transfers between devices with their start and end apart: 13 -> 13, of which waited for: 6 -> 3; matrix products, arithmetic and copies ran while one was open for 1% -> 1% of each run, Pallas kernels for 30% -> 31%
where the time goes in v3:
time: 166 us; the launch traced here: 165 us
  Pallas kernels  65.2 us (39%)
  waiting for transfers between devices  40.5 us (24%)
  starting transfers between devices  32.6 us (20%)
  other arithmetic  22.2 us (13%)
  local copies, waits for them, and re-layouts  3.47 us (2%)
    pallas_call x4, Pallas kernels, spread_chunk(): pl.pallas_call(kernel, out_shape=(shape((5, n, width), jnp.float32), shap...  42.1 us
    ppermute x10, waiting for transfers between devices, passed_along(): return lax.ppermute(value, axis, pairs)  25.9 us
    ppermute x10, starting transfers between devices, passed_along(): return lax.ppermute(value, axis, pairs)  18.5 us
    all_to_all x1, waiting for transfers between devices, dispatched(): lax.all_to_all(send, ('ves', 'shard'), split_axis=0, concat_axis=0, tiled...  14.6 us
    sort x1, other arithmetic, one_step(): ordered = lax.sort((key,) + tuple(got[1:]), num_keys=1, is_stable=False)  13.1 us
    pallas_call x1, Pallas kernels, interior(): pl.pallas_call(kernel, out_shape=jax.ShapeDtypeStruct(populations.shape,...  10.2 us
    all_to_all x1, starting transfers between devices, dispatched(): lax.all_to_all(send, ('ves', 'shard'), split_axis=0, concat_axis=0, tiled...  7.23 us
    pallas_call x1, Pallas kernels, spread_own(): pl.pallas_call(kernel, out_shape=jax.ShapeDtypeStruct((slab * 3, width +...  7.04 us
  transfers between devices with their start and end apart: 13, of which 3 were waited for; matrix products, arithmetic and copies ran while one was open for 1% of the time, Pallas kernels for 31%

profile of v3, /device:TPU:0, one launch (start us, length us, event | category | flops | bytes accessed | tf_op | source)
XLA Modules:
  0.0 165.1 jit_solution(17466755872032453125)
XLA Ops:
  0.6 0.8 fusion.4
  1.4 1.3 collective-permute-start.1
  2.7 5.5 %collective-permute-start = (f32[3,2,2,128]{3,2,1,0:T(2,128)S(1)}, f32[3,2,2,128]{3,2,1,0:T(2,128)S(1)}, u32[]{:S(2)}, u32[]{:S(2)}) collective-permute-start(f32[3,2,2,128]{3,2,1,0:T(2,128)S(1)} %get-tuple-element.87), channel_id=1, source_target_pairs={{0,1},{1,2},{2,3},{3,4},{4,5},{5,6},{6,7},{8,9},{9,10},{10,11},{11... | collective-permute-start | bytes 18440 | tf_op jit(solution)/shard_map/ppermute | solution.py:50
  8.2 1.0 convert_reduce_fusion.1.start_ref
  9.2 0.6 pad_add_fusion.edge
  9.9 0.0 collective-permute-done.1.after_ref
  9.9 0.0 collective-permute-done.before_ref
  9.9 0.6 copy-done.1
  10.4 0.6 copy-done.2
  11.0 1.9 %prepared.1 = (f32[3,2,32,128]{3,2,1,0:T(8,128)}, s32[64,128]{1,0:T(8,128)}, f32[64,128]{1,0:T(8,128)}, f32[64,128]{1,0:T(8,128)}, f32[64,128]{1,0:T(8,128)}, /*...) custom-call(s32[2]{0:T(128)} %pad_add_fusion.edge, f32[2]{0:T(128)} %t_ref.1, f32[2]{0:T(128)} %b_ref.1, ...), custom_call_target="tpu_custom_call" | custom-call | tf_op jit(solution)/shard_map/prepared/pallas_call | solution.py:571
  12.9 6.9 %sort.90 = (s32[8192]{0:T(1024)S(1)}, f32[8192]{0:T(1024)S(1)}, f32[8192]{0:T(1024)S(1)}, f32[8192]{0:T(1024)S(1)}, f32[8192]{0:T(1024)S(1)}, /*index=5*/f32[8192]{0:T(1024)S(1)}, f32[8192]{0:T(1024)S(1)}) sort(s32[8192]{0:T(1024)} %bitcast.60, f32[8192]{0:T(1024)} %bitcast.61, f32[8192]{0:T(1024)} %bitcast.62, f32[8192]{0:T(1024)} %bitcast.63, ...), dimensions={0}, to_apply=%region_1.2 | sort | flops 106496 | bytes 458752 | tf_op jit(solution)/shard_map/sort | solution.py:624
  19.8 2.5 %packed.1 = f32[32,7,4,128]{3,2,1,0:T(4,128)} custom-call(s32[32]{0:T(128)S(1)} %convert_reduce_fusion.1.start_ref, s32[64,128]{1,0:T(8,128)S(1)} %bitcast.44, f32[64,128]{1,0:T(8,128)S(1)} %bitcast.45, f32[64,128]{1,0:T(8,128)S(1)} %bitcast.46, f32[64,128]{1,0:T(8,128)S(1)} %bitcast.47, f32[64,128]{1,0:T(8,128)S(1)} %bitcast.48, f32[64,128]{1,0:T(8,128)S(1)} %bitcast.49, ...), custom_call_target="tpu_custom_call" | custom-call | tf_op jit(solution)/shard_map/packed/pallas_call | solution.py:609
  22.3 7.2 %all-to-all-start = ((f32[32,7,4,128]{3,2,1,0:T(4,128)}), f32[32,7,4,128]{3,2,1,0:T(4,128)S(1)}, u32[]{:S(2)}, u32[]{:S(2)}) async-start(f32[32,7,4,128]{3,2,1,0:T(4,128)} %packed.1), calls=%async_computation | async-start | bytes 917504 | tf_op jit(solution)/shard_map/all_to_all | solution.py:630
  29.5 14.6 %all-to-all-done = f32[32,7,4,128]{3,2,1,0:T(4,128)S(1)} async-done(((f32[32,7,4,128]{3,2,1,0:T(4,128)}), f32[32,7,4,128]{3,2,1,0:T(4,128)S(1)}, u32[]{:S(2)}, u32[]{:S(2)}) %all-to-all-start) | async-done | bytes 458784 | tf_op jit(solution)/shard_map/all_to_all | solution.py:630
  44.2 0.1 fusion.2
  44.3 0.4 convert_reduce_fusion
  44.7 13.1 %sort.91 = (s32[16384]{0:T(1024)S(1)}, f32[16384]{0:T(1024)S(1)}, f32[16384]{0:T(1024)S(1)}, f32[16384]{0:T(1024)S(1)}, f32[16384]{0:T(1024)S(1)}, /*index=5*/f32[16384]{0:T(1024)S(1)}, f32[16384]{0:T(1024)S(1)}) sort(s32[16384]{0:T(1024)S(1)} %bitcast.52, f32[16384]{0:T(1024)S(1)} %bitcast.58, f32[16384]{0:T(1024)S(1)} %bitcast.57, f32[16384]{0:T(1024)S(1)} %bitcast.56, ...), dimensions={0}, to_apply=%region_2.3 | sort | flops 229376 | bytes 917504 | tf_op jit(solution)/shard_map/sort | solution.py:650
  57.9 0.0 slice-start
  57.9 0.0 slice-start.1
  57.9 0.0 slice-start.2
  58.0 1.3 collective-permute-start.3
  59.3 1.0 collective-permute-start.2
  60.3 7.0 %spread_own.1.total_ref = f32[6,264,256]{2,1,0:T(8,128)S(1)} custom-call(s32[17]{0:T(128)S(1)} %convert_element_type.49.starts, f32[904,128]{1,0:T(8,128)S(1)} %constant_dynamic-update-slice_fusion.list_ref), custom_call_target="tpu_custom_call" | custom-call | flops 20000000000 | bytes 4000000 | tf_op jit(solution)/shard_map/spread_own/pallas_call | solution.py:188
  67.3 13.1 %collective-permute-done.3.l1 = f32[904,128]{1,0:T(8,128)S(1)} collective-permute-done((f32[904,128]{1,0:T(8,128)S(1)}, f32[904,128]{1,0:T(8,128)S(1)}, u32[]{:S(2)}, u32[]{:S(2)}) %collective-permute-start.3) | collective-permute-done | bytes 462880 | tf_op jit(solution)/shard_map/ppermute | solution.py:41
  80.4 0.0 collective-permute-done.2.l0
  80.5 7.8 %shard_map.94 = (f32[5,32,256]{2,1,0:T(8,128)S(1)}, f32[5,32,256]{2,1,0:T(8,128)S(1)}, f32[6,48,256]{2,1,0:T(8,128)S(1)}, f32[2,3,256,256]{3,2,1,0:T(8,128)}) custom-call(s32[17]{0:T(128)S(1)} %fusion.1.s0, f32[904,128]{1,0:T(8,128)S(1)} %collective-permute-done.2.l0, s32[17]{0:T(128)S(1)} %fusion.s1, f32[904,128]{1,0:T(8,128)S(1)} %collective-permute-done.3.l1, ...), custom_call_target="tpu_custom_call" | custom-call | flops 8000000000 | bytes 4000000 | tf_op jit(solution)/shard_map/pallas_call | solution.py:343
  88.3 0.1 collective-permute-start.4
  88.4 5.3 %collective-permute-start.8 = (f32[5,32,256]{2,1,0:T(8,128)S(1)}, f32[5,32,256]{2,1,0:T(8,128)S(1)}, u32[]{:S(2)}, u32[]{:S(2)}) collective-permute-start(f32[5,32,256]{2,1,0:T(8,128)S(1)} %get-tuple-element.73), channel_id=1, source_target_pairs={{0,31},{1,0},{2,1},{3,2},{4,3},{5,4},{6,5},{7,6},{8,7},{9,8},{10,9... | collective-permute-start | bytes 491528 | tf_op jit(solution)/shard_map/ppermute | solution.py:41
  93.7 8.0 %shard_map.95 = (f32[5,48,256]{2,1,0:T(8,128)S(1)}, f32[5,48,256]{2,1,0:T(8,128)S(1)}, f32[6,48,256]{2,1,0:T(8,128)S(1)}, f32[2,3,256,256]{3,2,1,0:T(8,128)}) custom-call(s32[17]{0:T(128)S(1)} %fusion.1.s0, f32[904,128]{1,0:T(8,128)S(1)} %collective-permute-done.2.l0, s32[17]{0:T(128)S(1)} %fusion.s1, ...), custom_call_target="tpu_custom_call", output_to_operand_aliasing={{3}: (8, {})} | custom-call | flops 8000000000 | bytes 4000000 | tf_op jit(solution)/shard_map/pallas_call | solution.py:343
  101.8 0.1 collective-permute-start.5
  101.8 12.7 %shard_map.96 = (f32[5,80,256]{2,1,0:T(8,128)S(1)}, f32[5,80,256]{2,1,0:T(8,128)S(1)}, f32[6,48,256]{2,1,0:T(8,128)S(1)}, f32[2,3,256,256]{3,2,1,0:T(8,128)}) custom-call(s32[17]{0:T(128)S(1)} %fusion.1.s0, f32[904,128]{1,0:T(8,128)S(1)} %collective-permute-done.2.l0, s32[17]{0:T(128)S(1)} %fusion.s1, ...), custom_call_target="tpu_custom_call", output_to_operand_aliasing={{3}: (8, {})} | custom-call | flops 8000000000 | bytes 4000000 | tf_op jit(solution)/shard_map/pallas_call | solution.py:343
  114.6 13.6 %shard_map.97 = (f32[5,96,256]{2,1,0:T(8,128)S(1)}, f32[5,96,256]{2,1,0:T(8,128)S(1)}, f32[6,48,256]{2,1,0:T(8,128)}, f32[2,3,256,256]{3,2,1,0:T(8,128)}) custom-call(s32[17]{0:T(128)S(1)} %fusion.1.s0, f32[904,128]{1,0:T(8,128)S(1)} %collective-permute-done.2.l0, s32[17]{0:T(128)S(1)} %fusion.s1, ...), custom_call_target="tpu_custom_call", output_to_operand_aliasing={{3}: (8, {})} | custom-call | flops 8000000000 | bytes 4000000 | tf_op jit(solution)/shard_map/pallas_call | solution.py:343
  128.2 0.1 collective-permute-start.7
  128.3 5.3 %collective-permute-start.11 = (f32[5,96,256]{2,1,0:T(8,128)S(1)}, f32[5,96,256]{2,1,0:T(8,128)S(1)}, u32[]{:S(2)}, u32[]{:S(2)}) collective-permute-start(f32[5,96,256]{2,1,0:T(8,128)S(1)} %get-tuple-element.76), channel_id=1, source_target_pairs={{0,31},{1,0},{2,1},{3,2},{4,3},{5,4},{6,5},{7,6},{8,7},{9,8},{10,9... | collective-permute-start | bytes 1474568 | tf_op jit(solution)/shard_map/ppermute | solution.py:41
  133.6 0.0 collective-permute-done.4.refs_1_
  133.6 0.0 collective-permute-start.6
  133.6 0.0 collective-permute-done.8.refs_5_
  133.6 5.3 %collective-permute-start.10 = (f32[5,80,256]{2,1,0:T(8,128)S(1)}, f32[5,80,256]{2,1,0:T(8,128)S(1)}, u32[]{:S(2)}, u32[]{:S(2)}) collective-permute-start(f32[5,80,256]{2,1,0:T(8,128)S(1)} %get-tuple-element.75), channel_id=1, source_target_pairs={{0,31},{1,0},{2,1},{3,2},{4,3},{5,4},{6,5},{7,6},{8,7},{9,8},{10,9... | collective-permute-start | bytes 1228808 | tf_op jit(solution)/shard_map/ppermute | solution.py:41
  138.9 0.0 collective-permute-done.5.refs_2_
  138.9 0.1 collective-permute-start.9
  139.0 1.4 copy-done
  140.4 10.2 %interior.1.refs_0_ = f32[2,19,256,256]{3,2,1,0:T(8,128)} custom-call(f32[2,19,256,256]{3,2,1,0:T(8,128)S(1)} %bitcast.43, f32[2,3,256,256]{3,2,1,0:T(8,128)S(1)} %copy-done), custom_call_target="tpu_custom_call" | custom-call | bytes 25000000 | tf_op jit(solution)/shard_map/interior/pallas_call | solution.py:464
  150.6 12.7 %collective-permute-done.9.refs_6_ = f32[5,48,256]{2,1,0:T(8,128)S(1)} collective-permute-done((f32[5,48,256]{2,1,0:T(8,128)S(1)}, f32[5,48,256]{2,1,0:T(8,128)S(1)}, u32[]{:S(2)}, u32[]{:S(2)}) %collective-permute-start.9) | collective-permute-done | bytes 245792 | tf_op jit(solution)/shard_map/ppermute | solution.py:41
  163.3 0.0 collective-permute-done.6.refs_3_
  163.3 0.0 collective-permute-done.10.refs_7_
  163.3 0.0 collective-permute-done.7.refs_4_
  163.3 0.0 collective-permute-done.11.refs_8_
  163.3 1.6 arrivals.1
  (25 shorter events, 0.1 us)
Async XLA Ops:
  1.4 8.5 %collective-permute-start.1 = (f32[3,2,2,128]{3,2,1,0:T(2,128)S(1)}, f32[3,2,2,128]{3,2,1,0:T(2,128)S(1)}, u32[]{:S(2)}, u32[]{:S(2)}) collective-permute-start(f32[3,2,2,128]{3,2,1,0:T(2,128)S(1)} %get-tuple-element.86), channel_id=1, source_target_pairs={{1,0},{2,1},{3,2},{4,3},{5,4},{6,5},{7,6},{9,8},{10,9},{11,10},{12... | collective-permute-start | bytes 18440 | tf_op jit(solution)/shard_map/ppermute | solution.py:50
  2.7 7.2 %collective-permute-start = (f32[3,2,2,128]{3,2,1,0:T(2,128)S(1)}, f32[3,2,2,128]{3,2,1,0:T(2,128)S(1)}, u32[]{:S(2)}, u32[]{:S(2)}) collective-permute-start(f32[3,2,2,128]{3,2,1,0:T(2,128)S(1)} %get-tuple-element.87), channel_id=1, source_target_pairs={{0,1},{1,2},{2,3},{3,4},{4,5},{5,6},{6,7},{8,9},{9,10},{10,11},{11... | collective-permute-start | bytes 18440 | tf_op jit(solution)/shard_map/ppermute | solution.py:50
  9.9 0.6 copy-start.1
  10.4 0.6 copy-start.2
  22.3 21.9 %all-to-all-start = ((f32[32,7,4,128]{3,2,1,0:T(4,128)}), f32[32,7,4,128]{3,2,1,0:T(4,128)S(1)}, u32[]{:S(2)}, u32[]{:S(2)}) async-start(f32[32,7,4,128]{3,2,1,0:T(4,128)} %packed.1), calls=%async_computation | async-start | bytes 917504 | tf_op jit(solution)/shard_map/all_to_all | solution.py:630
  57.9 22.6 %slice-start = ((s8[9961472]{0:T(1024)(128)(4,1)}), s8[4194304]{0:T(1024)(128)(4,1)S(1)}, s32[]{:S(2)}) async-start(s8[9961472]{0:T(1024)(128)(4,1)} %bitcast.42), calls=%async_computation.1 | async-start | bytes 8388608
  57.9 22.6 %slice-start.1 = ((s8[9961472]{0:T(1024)(128)(4,1)}), s8[4194304]{0:T(1024)(128)(4,1)S(1)}, s32[]{:S(2)}) async-start(s8[9961472]{0:T(1024)(128)(4,1)} %bitcast.42), calls=%async_computation.2 | async-start | bytes 8388608
  57.9 22.6 %slice-start.2 = ((s8[9961472]{0:T(1024)(128)(4,1)}), s8[1572864]{0:T(1024)(128)(4,1)S(1)}, s32[]{:S(2)}) async-start(s8[9961472]{0:T(1024)(128)(4,1)} %bitcast.42), calls=%async_computation.3 | async-start | bytes 3145728
  58.0 22.5 %collective-permute-start.3 = (f32[904,128]{1,0:T(8,128)S(1)}, f32[904,128]{1,0:T(8,128)S(1)}, u32[]{:S(2)}, u32[]{:S(2)}) collective-permute-start(f32[904,128]{1,0:T(8,128)S(1)} %constant_dynamic-update-slice_fusion.list_ref), channel_id=1, source_target_pairs={{0,31},{1,0},{2,1},{3,2},{4,3},{5,4},{6,5},{7,6},{8,7},{9,8},{10,9... | collective-permute-start | bytes 1388552 | tf_op jit(solution)/shard_map/ppermute | solution.py:41
  59.3 21.2 %collective-permute-start.2 = (f32[904,128]{1,0:T(8,128)S(1)}, f32[904,128]{1,0:T(8,128)S(1)}, u32[]{:S(2)}, u32[]{:S(2)}) collective-permute-start(f32[904,128]{1,0:T(8,128)S(1)} %constant_dynamic-update-slice_fusion.list_ref), channel_id=1, source_target_pairs={{0,1},{1,2},{2,3},{3,4},{4,5},{5,6},{6,7},{7,8},{8,9},{9,10},{10,1... | collective-permute-start | bytes 1388552 | tf_op jit(solution)/shard_map/ppermute | solution.py:41
  88.3 45.3 %collective-permute-start.4 = (f32[5,32,256]{2,1,0:T(8,128)S(1)}, f32[5,32,256]{2,1,0:T(8,128)S(1)}, u32[]{:S(2)}, u32[]{:S(2)}) collective-permute-start(f32[5,32,256]{2,1,0:T(8,128)S(1)} %get-tuple-element.69), channel_id=1, source_target_pairs={{0,1},{1,2},{2,3},{3,4},{4,5},{5,6},{6,7},{7,8},{8,9},{9,10},{10,1... | collective-permute-start | bytes 491528 | tf_op jit(solution)/shard_map/ppermute | solution.py:41
  88.4 45.2 %collective-permute-start.8 = (f32[5,32,256]{2,1,0:T(8,128)S(1)}, f32[5,32,256]{2,1,0:T(8,128)S(1)}, u32[]{:S(2)}, u32[]{:S(2)}) collective-permute-start(f32[5,32,256]{2,1,0:T(8,128)S(1)} %get-tuple-element.73), channel_id=1, source_target_pairs={{0,31},{1,0},{2,1},{3,2},{4,3},{5,4},{6,5},{7,6},{8,7},{9,8},{10,9... | collective-permute-start | bytes 491528 | tf_op jit(solution)/shard_map/ppermute | solution.py:41
  101.8 37.2 %collective-permute-start.5 = (f32[5,48,256]{2,1,0:T(8,128)S(1)}, f32[5,48,256]{2,1,0:T(8,128)S(1)}, u32[]{:S(2)}, u32[]{:S(2)}) collective-permute-start(f32[5,48,256]{2,1,0:T(8,128)S(1)} %get-tuple-element.70), channel_id=1, source_target_pairs={{0,1},{1,2},{2,3},{3,4},{4,5},{5,6},{6,7},{7,8},{8,9},{9,10},{10,1... | collective-permute-start | bytes 737288 | tf_op jit(solution)/shard_map/ppermute | solution.py:41
  128.2 35.1 %collective-permute-start.7 = (f32[5,96,256]{2,1,0:T(8,128)S(1)}, f32[5,96,256]{2,1,0:T(8,128)S(1)}, u32[]{:S(2)}, u32[]{:S(2)}) collective-permute-start(f32[5,96,256]{2,1,0:T(8,128)S(1)} %get-tuple-element.72), channel_id=1, source_target_pairs={{0,1},{1,2},{2,3},{3,4},{4,5},{5,6},{6,7},{7,8},{8,9},{9,10},{10,1... | collective-permute-start | bytes 1474568 | tf_op jit(solution)/shard_map/ppermute | solution.py:41
  128.3 35.1 %collective-permute-start.11 = (f32[5,96,256]{2,1,0:T(8,128)S(1)}, f32[5,96,256]{2,1,0:T(8,128)S(1)}, u32[]{:S(2)}, u32[]{:S(2)}) collective-permute-start(f32[5,96,256]{2,1,0:T(8,128)S(1)} %get-tuple-element.76), channel_id=1, source_target_pairs={{0,31},{1,0},{2,1},{3,2},{4,3},{5,4},{6,5},{7,6},{8,7},{9,8},{10,9... | collective-permute-start | bytes 1474568 | tf_op jit(solution)/shard_map/ppermute | solution.py:41
  133.6 29.7 %collective-permute-start.6 = (f32[5,80,256]{2,1,0:T(8,128)S(1)}, f32[5,80,256]{2,1,0:T(8,128)S(1)}, u32[]{:S(2)}, u32[]{:S(2)}) collective-permute-start(f32[5,80,256]{2,1,0:T(8,128)S(1)} %get-tuple-element.71), channel_id=1, source_target_pairs={{0,1},{1,2},{2,3},{3,4},{4,5},{5,6},{6,7},{7,8},{8,9},{9,10},{10,1... | collective-permute-start | bytes 1228808 | tf_op jit(solution)/shard_map/ppermute | solution.py:41
  133.6 29.7 %collective-permute-start.10 = (f32[5,80,256]{2,1,0:T(8,128)S(1)}, f32[5,80,256]{2,1,0:T(8,128)S(1)}, u32[]{:S(2)}, u32[]{:S(2)}) collective-permute-start(f32[5,80,256]{2,1,0:T(8,128)S(1)} %get-tuple-element.75), channel_id=1, source_target_pairs={{0,31},{1,0},{2,1},{3,2},{4,3},{5,4},{6,5},{7,6},{8,7},{9,8},{10,9... | collective-permute-start | bytes 1228808 | tf_op jit(solution)/shard_map/ppermute | solution.py:41
  138.9 24.4 %collective-permute-start.9 = (f32[5,48,256]{2,1,0:T(8,128)S(1)}, f32[5,48,256]{2,1,0:T(8,128)S(1)}, u32[]{:S(2)}, u32[]{:S(2)}) collective-permute-start(f32[5,48,256]{2,1,0:T(8,128)S(1)} %get-tuple-element.74), channel_id=1, source_target_pairs={{0,31},{1,0},{2,1},{3,2},{4,3},{5,4},{6,5},{7,6},{8,7},{9,8},{10,9... | collective-permute-start | bytes 737288 | tf_op jit(solution)/shard_map/ppermute | solution.py:41
  139.0 1.4 copy-start

commit v4 on v3

--- a/solution.py
+++ b/solution.py
@@ -617,6 +617,70 @@
     )(starts, *columns)
 
 
+def exchanged(send):
+    groups, members = (lax.axis_size("ves"), lax.axis_size("shard"))
+    count = groups * members
+
+    def kernel(send_ref, got_ref, own_sem, send_sems, got_sems):
+        group, member = (lax.axis_index("ves"), lax.axis_index("shard"))
+        me = group * members + member
+        barrier = pltpu.get_barrier_semaphore()
+
+        def other(k):
+            peer = lax.rem(me + k, count)
+            return peer, (peer // members, lax.rem(peer, members))
+
+        def greet(k, carry):
+            pl.semaphore_signal(
+                barrier, inc=1, device_id=other(k)[1], device_id_type=pl.DeviceIdType.MESH
+            )
+            return carry
+
+        lax.fori_loop(1, count, greet, 0)
+        own = pltpu.make_async_copy(send_ref.at[me], got_ref.at[me], own_sem)
+        own.start()
+        pl.semaphore_wait(barrier, count - 1)
+
+        def copy(k):
+            peer, place = other(k)
+            return pltpu.make_async_remote_copy(
+                src_ref=send_ref.at[peer],
+                dst_ref=got_ref.at[me],
+                send_sem=send_sems.at[k],
+                recv_sem=got_sems.at[k],
+                device_id=place,
+                device_id_type=pl.DeviceIdType.MESH,
+            )
+
+        def begin(k, carry):
+            copy(k).start()
+            return carry
+
+        def finish(k, carry):
+            copy(k).wait()
+            return carry
+
+        lax.fori_loop(1, count, begin, 0)
+        own.wait()
+        lax.fori_loop(1, count, finish, 0)
+
+    return pl.pallas_call(
+        kernel,
+        out_shape=jax.ShapeDtypeStruct(send.shape, send.dtype),
+        in_specs=[ANY],
+        out_specs=ANY,
+        scratch_shapes=[
+            pltpu.SemaphoreType.DMA,
+            pltpu.SemaphoreType.DMA((count,)),
+            pltpu.SemaphoreType.DMA((count,)),
+        ],
+        compiler_params=pltpu.CompilerParams(
+            collective_id=0, has_side_effects=True, vmem_limit_bytes=4 * MIB
+        ),
+        name="exchanged",
+    )(send)
+
+
 def dispatched(key, values, owner, device_count, cells):
     capacity = 2 * owner.size // device_count
     devices = jnp.arange(device_count, dtype=jnp.int32)
@@ -627,7 +691,7 @@
     send = packed(
         starts, [v.reshape(-1, LANES) for v in ordered], device_count, capacity, cells
     )
-    return lax.all_to_all(send, ("ves", "shard"), split_axis=0, concat_axis=0, tiled=True)
+    return exchanged(send)
 
 
 CUTS = (0, 3, 6, 11, 16)

time: 166 us -> 162 us (0.976)
  Pallas kernels: 65.2 us -> 83.7 us
  waiting for transfers between devices: 40.5 us -> 24.2 us
  starting transfers between devices: 32.6 us -> 26.5 us
    pallas_call x0 -> x1, Pallas kernels: none -> 19.3 us  [exchanged(): pl.pallas_call(kernel, out_shape=jax.ShapeDtypeStruct(send.shape, send.dt...]
    all_to_all x1 -> x0, waiting for transfers between devices: 14.6 us -> none  [dispatched(): lax.all_to_all(send, ('ves', 'shard'), split_axis=0, concat_axis=0, tiled...]
    all_to_all x1 -> x0, starting transfers between devices: 7.23 us -> none  [dispatched(): lax.all_to_all(send, ('ves', 'shard'), split_axis=0, concat_axis=0, tiled...]
    ppermute x10, waiting for transfers between devices: 25.9 us -> 24.2 us  [passed_along(): return lax.ppermute(value, axis, pairs)]
  transfers between devices with their start and end apart: 13 -> 12, of which waited for: 3 -> 2; matrix products, arithmetic and copies ran while one was open for 1% -> 1% of each run, Pallas kernels for 31% -> 32%
where the time goes in v4:
time: 162 us; the launch traced here: 161 us
  Pallas kernels  83.7 us (52%)
  starting transfers between devices  26.5 us (16%)
  waiting for transfers between devices  24.2 us (15%)
  other arithmetic  22.4 us (14%)
  local copies, waits for them, and re-layouts  3.47 us (2%)
    pallas_call x4, Pallas kernels, spread_chunk(): pl.pallas_call(kernel, out_shape=(shape((5, n, width), jnp.float32), shap...  42.1 us
    ppermute x10, waiting for transfers between devices, passed_along(): return lax.ppermute(value, axis, pairs)  24.2 us
    ppermute x10, starting transfers between devices, passed_along(): return lax.ppermute(value, axis, pairs)  19.7 us
    pallas_call x1, Pallas kernels, exchanged(): pl.pallas_call(kernel, out_shape=jax.ShapeDtypeStruct(send.shape, send.dt...  19.3 us
    sort x1, other arithmetic, one_step(): ordered = lax.sort((key,) + tuple(got[1:]), num_keys=1, is_stable=False)  13.3 us
    pallas_call x1, Pallas kernels, interior(): pl.pallas_call(kernel, out_shape=jax.ShapeDtypeStruct(populations.shape,...  10.2 us
    pallas_call x1, Pallas kernels, spread_own(): pl.pallas_call(kernel, out_shape=jax.ShapeDtypeStruct((slab * 3, width +...  7.05 us
    sort x1, other arithmetic, dispatched(): lax.sort((key.reshape(-1),) + tuple((v.reshape(-1) for v in values)), num...  6.91 us
  transfers between devices with their start and end apart: 12, of which 2 were waited for; matrix products, arithmetic and copies ran while one was open for 1% of the time, Pallas kernels for 32%

profile of v4, /device:TPU:0, one launch (start us, length us, event | category | flops | bytes accessed | tf_op | source)
XLA Modules:
  0.0 161.4 jit_solution(2030278528302503200)
XLA Ops:
  0.6 0.8 fusion.4
  1.4 1.3 collective-permute-start.1
  2.7 5.5 %collective-permute-start = (f32[3,2,2,128]{3,2,1,0:T(2,128)S(1)}, f32[3,2,2,128]{3,2,1,0:T(2,128)S(1)}, u32[]{:S(2)}, u32[]{:S(2)}) collective-permute-start(f32[3,2,2,128]{3,2,1,0:T(2,128)S(1)} %get-tuple-element.87), channel_id=1, source_target_pairs={{0,1},{1,2},{2,3},{3,4},{4,5},{5,6},{6,7},{8,9},{9,10},{10,11},{11... | collective-permute-start | bytes 18440 | tf_op jit(solution)/shard_map/ppermute | solution.py:50
  8.2 1.0 convert_reduce_fusion.1.start_ref
  9.2 0.6 pad_add_fusion.edge
  9.9 0.0 collective-permute-done.1.after_ref
  9.9 0.0 collective-permute-done.before_ref
  9.9 0.6 copy-done.1
  10.5 0.6 copy-done.2
  11.1 1.9 %prepared.1 = (f32[3,2,32,128]{3,2,1,0:T(8,128)}, s32[64,128]{1,0:T(8,128)}, f32[64,128]{1,0:T(8,128)}, f32[64,128]{1,0:T(8,128)}, f32[64,128]{1,0:T(8,128)}, /*...) custom-call(s32[2]{0:T(128)} %pad_add_fusion.edge, f32[2]{0:T(128)} %t_ref.1, f32[2]{0:T(128)} %b_ref.1, ...), custom_call_target="tpu_custom_call" | custom-call | tf_op jit(solution)/shard_map/prepared/pallas_call | solution.py:571
  12.9 6.9 %sort.90 = (s32[8192]{0:T(1024)S(1)}, f32[8192]{0:T(1024)S(1)}, f32[8192]{0:T(1024)S(1)}, f32[8192]{0:T(1024)S(1)}, f32[8192]{0:T(1024)S(1)}, /*index=5*/f32[8192]{0:T(1024)S(1)}, f32[8192]{0:T(1024)S(1)}) sort(s32[8192]{0:T(1024)} %bitcast.60, f32[8192]{0:T(1024)} %bitcast.61, f32[8192]{0:T(1024)} %bitcast.62, f32[8192]{0:T(1024)} %bitcast.63, ...), dimensions={0}, to_apply=%region_1.2 | sort | flops 106496 | bytes 458752 | tf_op jit(solution)/shard_map/sort | solution.py:688
  19.8 1.7 %packed.1.send_ref = f32[32,7,4,128]{3,2,1,0:T(4,128)S(1)} custom-call(s32[32]{0:T(128)S(1)} %convert_reduce_fusion.1.start_ref, s32[64,128]{1,0:T(8,128)S(1)} %bitcast.44, f32[64,128]{1,0:T(8,128)S(1)} %bitcast.45, f32[64,128]{1,0:T(8,128)S(1)} %bitcast.46, f32[64,128]{1,0:T(8,128)S(1)} %bitcast.47, f32[64,128]{1,0:T(8,128)S(1)} %bitcast.48, ...), custom_call_target="tpu_custom_call" | custom-call | tf_op jit(solution)/shard_map/packed/pallas_call | solution.py:609
  21.5 19.3 %exchanged.1 = f32[32,7,4,128]{3,2,1,0:T(4,128)S(1)} custom-call(f32[32,7,4,128]{3,2,1,0:T(4,128)S(1)} %packed.1.send_ref), custom_call_target="tpu_custom_call" | custom-call | tf_op jit(solution)/shard_map/exchanged/pallas_call | solution.py:667
  40.8 0.1 fusion.2
  40.9 0.4 convert_reduce_fusion
  41.3 13.3 %sort.91 = (s32[16384]{0:T(1024)S(1)}, f32[16384]{0:T(1024)S(1)}, f32[16384]{0:T(1024)S(1)}, f32[16384]{0:T(1024)S(1)}, f32[16384]{0:T(1024)S(1)}, /*index=5*/f32[16384]{0:T(1024)S(1)}, f32[16384]{0:T(1024)S(1)}) sort(s32[16384]{0:T(1024)S(1)} %bitcast.52, f32[16384]{0:T(1024)S(1)} %bitcast.58, f32[16384]{0:T(1024)S(1)} %bitcast.57, f32[16384]{0:T(1024)S(1)} %bitcast.56, ...), dimensions={0}, to_apply=%region_2.3 | sort | flops 229376 | bytes 917504 | tf_op jit(solution)/shard_map/sort | solution.py:714
  54.8 0.0 slice-start
  54.8 0.0 slice-start.1
  54.8 0.0 slice-start.2
  54.8 3.5 %collective-permute-start.3 = (f32[904,128]{1,0:T(8,128)S(1)}, f32[904,128]{1,0:T(8,128)S(1)}, u32[]{:S(2)}, u32[]{:S(2)}) collective-permute-start(f32[904,128]{1,0:T(8,128)S(1)} %constant_dynamic-update-slice_fusion.list_ref), channel_id=1, source_target_pairs={{0,31},{1,0},{2,1},{3,2},{4,3},{5,4},{6,5},{7,6},{8,7},{9,8},{10,9... | collective-permute-start | bytes 1388552 | tf_op jit(solution)/shard_map/ppermute | solution.py:41
  58.3 0.0 collective-permute-start.2
  58.3 7.0 %spread_own.1.total_ref = f32[6,264,256]{2,1,0:T(8,128)S(1)} custom-call(s32[17]{0:T(128)S(1)} %convert_element_type.49.starts, f32[904,128]{1,0:T(8,128)S(1)} %constant_dynamic-update-slice_fusion.list_ref), custom_call_target="tpu_custom_call" | custom-call | flops 20000000000 | bytes 4000000 | tf_op jit(solution)/shard_map/spread_own/pallas_call | solution.py:188
  65.4 11.8 %collective-permute-done.3.l1 = f32[904,128]{1,0:T(8,128)S(1)} collective-permute-done((f32[904,128]{1,0:T(8,128)S(1)}, f32[904,128]{1,0:T(8,128)S(1)}, u32[]{:S(2)}, u32[]{:S(2)}) %collective-permute-start.3) | collective-permute-done | bytes 462880 | tf_op jit(solution)/shard_map/ppermute | solution.py:41
  77.2 0.0 collective-permute-done.2.l0
  77.2 0.0 slice-done
  77.2 7.7 %shard_map.94 = (f32[5,32,256]{2,1,0:T(8,128)S(1)}, f32[5,32,256]{2,1,0:T(8,128)S(1)}, f32[6,48,256]{2,1,0:T(8,128)S(1)}, f32[2,3,256,256]{3,2,1,0:T(8,128)}) custom-call(s32[17]{0:T(128)S(1)} %fusion.1.s0, f32[904,128]{1,0:T(8,128)S(1)} %collective-permute-done.2.l0, s32[17]{0:T(128)S(1)} %fusion.s1, f32[904,128]{1,0:T(8,128)S(1)} %collective-permute-done.3.l1, ...), custom_call_target="tpu_custom_call" | custom-call | flops 8000000000 | bytes 4000000 | tf_op jit(solution)/shard_map/pallas_call | solution.py:343
  85.0 0.1 collective-permute-start.4
  85.1 5.3 %collective-permute-start.8 = (f32[5,32,256]{2,1,0:T(8,128)S(1)}, f32[5,32,256]{2,1,0:T(8,128)S(1)}, u32[]{:S(2)}, u32[]{:S(2)}) collective-permute-start(f32[5,32,256]{2,1,0:T(8,128)S(1)} %get-tuple-element.73), channel_id=1, source_target_pairs={{0,31},{1,0},{2,1},{3,2},{4,3},{5,4},{6,5},{7,6},{8,7},{9,8},{10,9... | collective-permute-start | bytes 491528 | tf_op jit(solution)/shard_map/ppermute | solution.py:41
  90.4 8.0 %shard_map.95 = (f32[5,48,256]{2,1,0:T(8,128)S(1)}, f32[5,48,256]{2,1,0:T(8,128)S(1)}, f32[6,48,256]{2,1,0:T(8,128)S(1)}, f32[2,3,256,256]{3,2,1,0:T(8,128)}) custom-call(s32[17]{0:T(128)S(1)} %fusion.1.s0, f32[904,128]{1,0:T(8,128)S(1)} %collective-permute-done.2.l0, s32[17]{0:T(128)S(1)} %fusion.s1, ...), custom_call_target="tpu_custom_call", output_to_operand_aliasing={{3}: (8, {})} | custom-call | flops 8000000000 | bytes 4000000 | tf_op jit(solution)/shard_map/pallas_call | solution.py:343
  98.5 0.1 collective-permute-start.5
  98.5 12.7 %shard_map.96 = (f32[5,80,256]{2,1,0:T(8,128)S(1)}, f32[5,80,256]{2,1,0:T(8,128)S(1)}, f32[6,48,256]{2,1,0:T(8,128)S(1)}, f32[2,3,256,256]{3,2,1,0:T(8,128)}) custom-call(s32[17]{0:T(128)S(1)} %fusion.1.s0, f32[904,128]{1,0:T(8,128)S(1)} %collective-permute-done.2.l0, s32[17]{0:T(128)S(1)} %fusion.s1, ...), custom_call_target="tpu_custom_call", output_to_operand_aliasing={{3}: (8, {})} | custom-call | flops 8000000000 | bytes 4000000 | tf_op jit(solution)/shard_map/pallas_call | solution.py:343
  111.3 13.6 %shard_map.97 = (f32[5,96,256]{2,1,0:T(8,128)S(1)}, f32[5,96,256]{2,1,0:T(8,128)S(1)}, f32[6,48,256]{2,1,0:T(8,128)}, f32[2,3,256,256]{3,2,1,0:T(8,128)}) custom-call(s32[17]{0:T(128)S(1)} %fusion.1.s0, f32[904,128]{1,0:T(8,128)S(1)} %collective-permute-done.2.l0, s32[17]{0:T(128)S(1)} %fusion.s1, ...), custom_call_target="tpu_custom_call", output_to_operand_aliasing={{3}: (8, {})} | custom-call | flops 8000000000 | bytes 4000000 | tf_op jit(solution)/shard_map/pallas_call | solution.py:343
  124.9 0.1 collective-permute-start.7
  125.0 5.3 %collective-permute-start.11 = (f32[5,96,256]{2,1,0:T(8,128)S(1)}, f32[5,96,256]{2,1,0:T(8,128)S(1)}, u32[]{:S(2)}, u32[]{:S(2)}) collective-permute-start(f32[5,96,256]{2,1,0:T(8,128)S(1)} %get-tuple-element.76), channel_id=1, source_target_pairs={{0,31},{1,0},{2,1},{3,2},{4,3},{5,4},{6,5},{7,6},{8,7},{9,8},{10,9... | collective-permute-start | bytes 1474568 | tf_op jit(solution)/shard_map/ppermute | solution.py:41
  130.3 0.0 collective-permute-done.4.refs_1_
  130.3 0.0 collective-permute-start.6
  130.3 0.0 collective-permute-done.8.refs_5_
  130.3 5.3 %collective-permute-start.10 = (f32[5,80,256]{2,1,0:T(8,128)S(1)}, f32[5,80,256]{2,1,0:T(8,128)S(1)}, u32[]{:S(2)}, u32[]{:S(2)}) collective-permute-start(f32[5,80,256]{2,1,0:T(8,128)S(1)} %get-tuple-element.75), channel_id=1, source_target_pairs={{0,31},{1,0},{2,1},{3,2},{4,3},{5,4},{6,5},{7,6},{8,7},{9,8},{10,9... | collective-permute-start | bytes 1228808 | tf_op jit(solution)/shard_map/ppermute | solution.py:41
  135.6 0.0 collective-permute-done.5.refs_2_
  135.6 0.1 collective-permute-start.9
  135.7 1.4 copy-done
  137.1 10.2 %interior.1.refs_0_ = f32[2,19,256,256]{3,2,1,0:T(8,128)} custom-call(f32[2,19,256,256]{3,2,1,0:T(8,128)S(1)} %bitcast.43, f32[2,3,256,256]{3,2,1,0:T(8,128)S(1)} %copy-done), custom_call_target="tpu_custom_call" | custom-call | bytes 25000000 | tf_op jit(solution)/shard_map/interior/pallas_call | solution.py:464
  147.3 12.3 %collective-permute-done.9.refs_6_ = f32[5,48,256]{2,1,0:T(8,128)S(1)} collective-permute-done((f32[5,48,256]{2,1,0:T(8,128)S(1)}, f32[5,48,256]{2,1,0:T(8,128)S(1)}, u32[]{:S(2)}, u32[]{:S(2)}) %collective-permute-start.9) | collective-permute-done | bytes 245792 | tf_op jit(solution)/shard_map/ppermute | solution.py:41
  159.6 0.0 collective-permute-done.6.refs_3_
  159.6 0.0 collective-permute-done.10.refs_7_
  159.6 0.0 collective-permute-done.7.refs_4_
  159.6 0.0 collective-permute-done.11.refs_8_
  159.6 1.6 arrivals.1
  (24 shorter events, 0.1 us)
Async XLA Ops:
  1.4 8.5 %collective-permute-start.1 = (f32[3,2,2,128]{3,2,1,0:T(2,128)S(1)}, f32[3,2,2,128]{3,2,1,0:T(2,128)S(1)}, u32[]{:S(2)}, u32[]{:S(2)}) collective-permute-start(f32[3,2,2,128]{3,2,1,0:T(2,128)S(1)} %get-tuple-element.86), channel_id=1, source_target_pairs={{1,0},{2,1},{3,2},{4,3},{5,4},{6,5},{7,6},{9,8},{10,9},{11,10},{12... | collective-permute-start | bytes 18440 | tf_op jit(solution)/shard_map/ppermute | solution.py:50
  2.7 7.2 %collective-permute-start = (f32[3,2,2,128]{3,2,1,0:T(2,128)S(1)}, f32[3,2,2,128]{3,2,1,0:T(2,128)S(1)}, u32[]{:S(2)}, u32[]{:S(2)}) collective-permute-start(f32[3,2,2,128]{3,2,1,0:T(2,128)S(1)} %get-tuple-element.87), channel_id=1, source_target_pairs={{0,1},{1,2},{2,3},{3,4},{4,5},{5,6},{6,7},{8,9},{9,10},{10,11},{11... | collective-permute-start | bytes 18440 | tf_op jit(solution)/shard_map/ppermute | solution.py:50
  9.9 0.6 copy-start.1
  10.5 0.6 copy-start.2
  54.8 22.4 %slice-start = ((s8[9961472]{0:T(1024)(128)(4,1)}), s8[4194304]{0:T(1024)(128)(4,1)S(1)}, s32[]{:S(2)}) async-start(s8[9961472]{0:T(1024)(128)(4,1)} %bitcast.42), calls=%async_computation | async-start | bytes 8388608
  54.8 22.4 %slice-start.1 = ((s8[9961472]{0:T(1024)(128)(4,1)}), s8[4194304]{0:T(1024)(128)(4,1)S(1)}, s32[]{:S(2)}) async-start(s8[9961472]{0:T(1024)(128)(4,1)} %bitcast.42), calls=%async_computation.1 | async-start | bytes 8388608
  54.8 22.4 %slice-start.2 = ((s8[9961472]{0:T(1024)(128)(4,1)}), s8[1572864]{0:T(1024)(128)(4,1)S(1)}, s32[]{:S(2)}) async-start(s8[9961472]{0:T(1024)(128)(4,1)} %bitcast.42), calls=%async_computation.2 | async-start | bytes 3145728
  54.8 22.3 %collective-permute-start.3 = (f32[904,128]{1,0:T(8,128)S(1)}, f32[904,128]{1,0:T(8,128)S(1)}, u32[]{:S(2)}, u32[]{:S(2)}) collective-permute-start(f32[904,128]{1,0:T(8,128)S(1)} %constant_dynamic-update-slice_fusion.list_ref), channel_id=1, source_target_pairs={{0,31},{1,0},{2,1},{3,2},{4,3},{5,4},{6,5},{7,6},{8,7},{9,8},{10,9... | collective-permute-start | bytes 1388552 | tf_op jit(solution)/shard_map/ppermute | solution.py:41
  58.3 18.9 %collective-permute-start.2 = (f32[904,128]{1,0:T(8,128)S(1)}, f32[904,128]{1,0:T(8,128)S(1)}, u32[]{:S(2)}, u32[]{:S(2)}) collective-permute-start(f32[904,128]{1,0:T(8,128)S(1)} %constant_dynamic-update-slice_fusion.list_ref), channel_id=1, source_target_pairs={{0,1},{1,2},{2,3},{3,4},{4,5},{5,6},{6,7},{7,8},{8,9},{9,10},{10,1... | collective-permute-start | bytes 1388552 | tf_op jit(solution)/shard_map/ppermute | solution.py:41
  85.0 45.3 %collective-permute-start.4 = (f32[5,32,256]{2,1,0:T(8,128)S(1)}, f32[5,32,256]{2,1,0:T(8,128)S(1)}, u32[]{:S(2)}, u32[]{:S(2)}) collective-permute-start(f32[5,32,256]{2,1,0:T(8,128)S(1)} %get-tuple-element.69), channel_id=1, source_target_pairs={{0,1},{1,2},{2,3},{3,4},{4,5},{5,6},{6,7},{7,8},{8,9},{9,10},{10,1... | collective-permute-start | bytes 491528 | tf_op jit(solution)/shard_map/ppermute | solution.py:41
  85.1 45.2 %collective-permute-start.8 = (f32[5,32,256]{2,1,0:T(8,128)S(1)}, f32[5,32,256]{2,1,0:T(8,128)S(1)}, u32[]{:S(2)}, u32[]{:S(2)}) collective-permute-start(f32[5,32,256]{2,1,0:T(8,128)S(1)} %get-tuple-element.73), channel_id=1, source_target_pairs={{0,31},{1,0},{2,1},{3,2},{4,3},{5,4},{6,5},{7,6},{8,7},{9,8},{10,9... | collective-permute-start | bytes 491528 | tf_op jit(solution)/shard_map/ppermute | solution.py:41
  98.5 37.2 %collective-permute-start.5 = (f32[5,48,256]{2,1,0:T(8,128)S(1)}, f32[5,48,256]{2,1,0:T(8,128)S(1)}, u32[]{:S(2)}, u32[]{:S(2)}) collective-permute-start(f32[5,48,256]{2,1,0:T(8,128)S(1)} %get-tuple-element.70), channel_id=1, source_target_pairs={{0,1},{1,2},{2,3},{3,4},{4,5},{5,6},{6,7},{7,8},{8,9},{9,10},{10,1... | collective-permute-start | bytes 737288 | tf_op jit(solution)/shard_map/ppermute | solution.py:41
  124.9 34.7 %collective-permute-start.7 = (f32[5,96,256]{2,1,0:T(8,128)S(1)}, f32[5,96,256]{2,1,0:T(8,128)S(1)}, u32[]{:S(2)}, u32[]{:S(2)}) collective-permute-start(f32[5,96,256]{2,1,0:T(8,128)S(1)} %get-tuple-element.72), channel_id=1, source_target_pairs={{0,1},{1,2},{2,3},{3,4},{4,5},{5,6},{6,7},{7,8},{8,9},{9,10},{10,1... | collective-permute-start | bytes 1474568 | tf_op jit(solution)/shard_map/ppermute | solution.py:41
  125.0 34.7 %collective-permute-start.11 = (f32[5,96,256]{2,1,0:T(8,128)S(1)}, f32[5,96,256]{2,1,0:T(8,128)S(1)}, u32[]{:S(2)}, u32[]{:S(2)}) collective-permute-start(f32[5,96,256]{2,1,0:T(8,128)S(1)} %get-tuple-element.76), channel_id=1, source_target_pairs={{0,31},{1,0},{2,1},{3,2},{4,3},{5,4},{6,5},{7,6},{8,7},{9,8},{10,9... | collective-permute-start | bytes 1474568 | tf_op jit(solution)/shard_map/ppermute | solution.py:41
  130.3 29.3 %collective-permute-start.6 = (f32[5,80,256]{2,1,0:T(8,128)S(1)}, f32[5,80,256]{2,1,0:T(8,128)S(1)}, u32[]{:S(2)}, u32[]{:S(2)}) collective-permute-start(f32[5,80,256]{2,1,0:T(8,128)S(1)} %get-tuple-element.71), channel_id=1, source_target_pairs={{0,1},{1,2},{2,3},{3,4},{4,5},{5,6},{6,7},{7,8},{8,9},{9,10},{10,1... | collective-permute-start | bytes 1228808 | tf_op jit(solution)/shard_map/ppermute | solution.py:41
  130.3 29.3 %collective-permute-start.10 = (f32[5,80,256]{2,1,0:T(8,128)S(1)}, f32[5,80,256]{2,1,0:T(8,128)S(1)}, u32[]{:S(2)}, u32[]{:S(2)}) collective-permute-start(f32[5,80,256]{2,1,0:T(8,128)S(1)} %get-tuple-element.75), channel_id=1, source_target_pairs={{0,31},{1,0},{2,1},{3,2},{4,3},{5,4},{6,5},{7,6},{8,7},{9,8},{10,9... | collective-permute-start | bytes 1228808 | tf_op jit(solution)/shard_map/ppermute | solution.py:41
  135.6 24.0 %collective-permute-start.9 = (f32[5,48,256]{2,1,0:T(8,128)S(1)}, f32[5,48,256]{2,1,0:T(8,128)S(1)}, u32[]{:S(2)}, u32[]{:S(2)}) collective-permute-start(f32[5,48,256]{2,1,0:T(8,128)S(1)} %get-tuple-element.74), channel_id=1, source_target_pairs={{0,31},{1,0},{2,1},{3,2},{4,3},{5,4},{6,5},{7,6},{8,7},{9,8},{10,9... | collective-permute-start | bytes 737288 | tf_op jit(solution)/shard_map/ppermute | solution.py:41
  135.7 1.4 copy-start

commit v5 on v4

--- a/solution.py
+++ b/solution.py
@@ -134,9 +134,17 @@
         base = (w * WINDOW).astype(jnp.float32)
         at_row = (w + offset) * WINDOW
 
-        @pl.loop(begin, end)
-        def _(b):
-            parts = [half(b * (BLOCK // LANES) + h, base) for h in range(BLOCK // LANES)]
+        @pl.loop(0, (end - begin + 1) // 2)
+        def _(pair):
+            b = begin + 2 * pair
+            more = b + 1 < end
+            parts = []
+            for block, shifted in (
+                (b, base),
+                (jnp.where(more, b + 1, b), jnp.where(more, base, -4.0 * ROWS * WINDOW * LANES)),
+            ):
+                for h in range(BLOCK // LANES):
+                    parts.append(half(block * (BLOCK // LANES) + h, shifted))
             product = lax.dot_general(
                 jnp.concatenate([p[0] for p in parts], 1),
                 jnp.concatenate([p[1] for p in parts], 1),
@@ -694,7 +702,7 @@
     return exchanged(send)
 
 
-CUTS = (0, 3, 6, 11, 16)
+CUTS = (0, 4, 9, 13, 16)
 
 
 def one_step(displacement, tension, bending, offset, owner, cell, populations):

time: 162 us -> 166 us (1.025)
  waiting for transfers between devices: 24.2 us -> 39.8 us
  Pallas kernels: 83.7 us -> 72.5 us
    ppermute x10, waiting for transfers between devices: 24.2 us -> 39.7 us  [passed_along(): return lax.ppermute(value, axis, pairs)]
    pallas_call x4, Pallas kernels: 42.1 us -> 32.6 us  [spread_chunk(): pl.pallas_call(kernel, out_shape=(shape((5, n, width), jnp.float32), shap...]
    pallas_call x1, Pallas kernels: 7.05 us -> 5.36 us  [spread_own(): pl.pallas_call(kernel, out_shape=jax.ShapeDtypeStruct((slab * 3, width +...]
  transfers between devices with their start and end apart: 12 -> 12, of which waited for: 2 -> 5; matrix products, arithmetic and copies ran while one was open for 1% -> 1% of each run, Pallas kernels for 32% -> 9%
where the time goes in v5:
time: 166 us
  Pallas kernels  72.5 us (44%)
  waiting for transfers between devices  39.8 us (24%)
  starting transfers between devices  26.4 us (16%)
  other arithmetic  22.4 us (13%)
  local copies, waits for them, and re-layouts  3.47 us (2%)
    ppermute x10, waiting for transfers between devices, passed_along(): return lax.ppermute(value, axis, pairs)  39.7 us
    pallas_call x4, Pallas kernels, spread_chunk(): pl.pallas_call(kernel, out_shape=(shape((5, n, width), jnp.float32), shap...  32.6 us
    ppermute x10, starting transfers between devices, passed_along(): return lax.ppermute(value, axis, pairs)  19.6 us
    pallas_call x1, Pallas kernels, exchanged(): pl.pallas_call(kernel, out_shape=jax.ShapeDtypeStruct(send.shape, send.dt...  19.3 us
    sort x1, other arithmetic, one_step(): ordered = lax.sort((key,) + tuple(got[1:]), num_keys=1, is_stable=False)  13.3 us
    pallas_call x1, Pallas kernels, interior(): pl.pallas_call(kernel, out_shape=jax.ShapeDtypeStruct(populations.shape,...  10.2 us
    sort x1, other arithmetic, dispatched(): lax.sort((key.reshape(-1),) + tuple((v.reshape(-1) for v in values)), num...  6.91 us
    ppermute x2, starting transfers between devices, halos(): return (lax.ppermute(last, axis, up), lax.ppermute(initial, axis, down))  6.81 us
  transfers between devices with their start and end apart: 12, of which 5 were waited for; matrix products, arithmetic and copies ran while one was open for 1% of the time, Pallas kernels for 9%

profile of v5, /device:TPU:0, one launch (start us, length us, event | category | flops | bytes accessed | tf_op | source)
XLA Modules:
  0.0 165.7 jit_solution(8747598911439663344)
XLA Ops:
  0.6 0.8 fusion.4
  1.4 1.3 collective-permute-start.1
  2.7 5.5 %collective-permute-start = (f32[3,2,2,128]{3,2,1,0:T(2,128)S(1)}, f32[3,2,2,128]{3,2,1,0:T(2,128)S(1)}, u32[]{:S(2)}, u32[]{:S(2)}) collective-permute-start(f32[3,2,2,128]{3,2,1,0:T(2,128)S(1)} %get-tuple-element.87), channel_id=1, source_target_pairs={{0,1},{1,2},{2,3},{3,4},{4,5},{5,6},{6,7},{8,9},{9,10},{10,11},{11... | collective-permute-start | bytes 18440 | tf_op jit(solution)/shard_map/ppermute | solution.py:50
  8.2 1.0 convert_reduce_fusion.1.start_ref
  9.2 0.6 pad_add_fusion.edge
  9.9 0.0 collective-permute-done.1.after_ref
  9.9 0.0 collective-permute-done.before_ref
  9.9 0.6 copy-done.1
  10.5 0.6 copy-done.2
  11.1 1.9 %prepared.1 = (f32[3,2,32,128]{3,2,1,0:T(8,128)}, s32[64,128]{1,0:T(8,128)}, f32[64,128]{1,0:T(8,128)}, f32[64,128]{1,0:T(8,128)}, f32[64,128]{1,0:T(8,128)}, /*...) custom-call(s32[2]{0:T(128)} %pad_add_fusion.edge, f32[2]{0:T(128)} %t_ref.1, f32[2]{0:T(128)} %b_ref.1, ...), custom_call_target="tpu_custom_call" | custom-call | tf_op jit(solution)/shard_map/prepared/pallas_call | solution.py:579
  12.9 6.9 %sort.90 = (s32[8192]{0:T(1024)S(1)}, f32[8192]{0:T(1024)S(1)}, f32[8192]{0:T(1024)S(1)}, f32[8192]{0:T(1024)S(1)}, f32[8192]{0:T(1024)S(1)}, /*index=5*/f32[8192]{0:T(1024)S(1)}, f32[8192]{0:T(1024)S(1)}) sort(s32[8192]{0:T(1024)} %bitcast.60, f32[8192]{0:T(1024)} %bitcast.61, f32[8192]{0:T(1024)} %bitcast.62, f32[8192]{0:T(1024)} %bitcast.63, ...), dimensions={0}, to_apply=%region_1.2 | sort | flops 106496 | bytes 458752 | tf_op jit(solution)/shard_map/sort | solution.py:696
  19.8 1.7 %packed.1.send_ref = f32[32,7,4,128]{3,2,1,0:T(4,128)S(1)} custom-call(s32[32]{0:T(128)S(1)} %convert_reduce_fusion.1.start_ref, s32[64,128]{1,0:T(8,128)S(1)} %bitcast.44, f32[64,128]{1,0:T(8,128)S(1)} %bitcast.45, f32[64,128]{1,0:T(8,128)S(1)} %bitcast.46, f32[64,128]{1,0:T(8,128)S(1)} %bitcast.47, f32[64,128]{1,0:T(8,128)S(1)} %bitcast.48, ...), custom_call_target="tpu_custom_call" | custom-call | tf_op jit(solution)/shard_map/packed/pallas_call | solution.py:617
  21.5 19.3 %exchanged.1 = f32[32,7,4,128]{3,2,1,0:T(4,128)S(1)} custom-call(f32[32,7,4,128]{3,2,1,0:T(4,128)S(1)} %packed.1.send_ref), custom_call_target="tpu_custom_call" | custom-call | tf_op jit(solution)/shard_map/exchanged/pallas_call | solution.py:675
  40.8 0.1 fusion.2
  40.9 0.4 convert_reduce_fusion
  41.3 13.3 %sort.91 = (s32[16384]{0:T(1024)S(1)}, f32[16384]{0:T(1024)S(1)}, f32[16384]{0:T(1024)S(1)}, f32[16384]{0:T(1024)S(1)}, f32[16384]{0:T(1024)S(1)}, /*index=5*/f32[16384]{0:T(1024)S(1)}, f32[16384]{0:T(1024)S(1)}) sort(s32[16384]{0:T(1024)S(1)} %bitcast.52, f32[16384]{0:T(1024)S(1)} %bitcast.58, f32[16384]{0:T(1024)S(1)} %bitcast.57, f32[16384]{0:T(1024)S(1)} %bitcast.56, ...), dimensions={0}, to_apply=%region_2.3 | sort | flops 229376 | bytes 917504 | tf_op jit(solution)/shard_map/sort | solution.py:722
  54.8 0.0 slice-start
  54.8 0.0 slice-start.1
  54.8 0.0 slice-start.2
  54.8 3.5 %collective-permute-start.3 = (f32[904,128]{1,0:T(8,128)S(1)}, f32[904,128]{1,0:T(8,128)S(1)}, u32[]{:S(2)}, u32[]{:S(2)}) collective-permute-start(f32[904,128]{1,0:T(8,128)S(1)} %constant_dynamic-update-slice_fusion.list_ref), channel_id=1, source_target_pairs={{0,31},{1,0},{2,1},{3,2},{4,3},{5,4},{6,5},{7,6},{8,7},{9,8},{10,9... | collective-permute-start | bytes 1388552 | tf_op jit(solution)/shard_map/ppermute | solution.py:41
  58.3 0.0 collective-permute-start.2
  58.3 5.4 %spread_own.1.total_ref = f32[6,264,256]{2,1,0:T(8,128)S(1)} custom-call(s32[17]{0:T(128)S(1)} %convert_element_type.49.starts, f32[904,128]{1,0:T(8,128)S(1)} %constant_dynamic-update-slice_fusion.list_ref), custom_call_target="tpu_custom_call" | custom-call | flops 20000000000 | bytes 4000000 | tf_op jit(solution)/shard_map/spread_own/pallas_call | solution.py:196
  63.7 13.5 %collective-permute-done.3.l1 = f32[904,128]{1,0:T(8,128)S(1)} collective-permute-done((f32[904,128]{1,0:T(8,128)S(1)}, f32[904,128]{1,0:T(8,128)S(1)}, u32[]{:S(2)}, u32[]{:S(2)}) %collective-permute-start.3) | collective-permute-done | bytes 462880 | tf_op jit(solution)/shard_map/ppermute | solution.py:41
  77.2 0.0 collective-permute-done.2.l0
  77.2 0.0 slice-done
  77.2 7.3 %shard_map.94 = (f32[5,48,256]{2,1,0:T(8,128)S(1)}, f32[5,48,256]{2,1,0:T(8,128)S(1)}, f32[6,48,256]{2,1,0:T(8,128)S(1)}, f32[2,3,256,256]{3,2,1,0:T(8,128)}) custom-call(s32[17]{0:T(128)S(1)} %fusion.1.s0, f32[904,128]{1,0:T(8,128)S(1)} %collective-permute-done.2.l0, s32[17]{0:T(128)S(1)} %fusion.s1, f32[904,128]{1,0:T(8,128)S(1)} %collective-permute-done.3.l1, ...), custom_call_target="tpu_custom_call" | custom-call | flops 8000000000 | bytes 4000000 | tf_op jit(solution)/shard_map/pallas_call | solution.py:351
  84.6 10.0 %shard_map.95 = (f32[5,80,256]{2,1,0:T(8,128)S(1)}, f32[5,80,256]{2,1,0:T(8,128)S(1)}, f32[6,48,256]{2,1,0:T(8,128)S(1)}, f32[2,3,256,256]{3,2,1,0:T(8,128)}) custom-call(s32[17]{0:T(128)S(1)} %fusion.1.s0, f32[904,128]{1,0:T(8,128)S(1)} %collective-permute-done.2.l0, s32[17]{0:T(128)S(1)} %fusion.s1, ...), custom_call_target="tpu_custom_call", output_to_operand_aliasing={{3}: (8, {})} | custom-call | flops 8000000000 | bytes 4000000 | tf_op jit(solution)/shard_map/pallas_call | solution.py:351
  94.6 8.1 %shard_map.96 = (f32[5,64,256]{2,1,0:T(8,128)S(1)}, f32[5,64,256]{2,1,0:T(8,128)S(1)}, f32[6,48,256]{2,1,0:T(8,128)S(1)}, f32[2,3,256,256]{3,2,1,0:T(8,128)}) custom-call(s32[17]{0:T(128)S(1)} %fusion.1.s0, f32[904,128]{1,0:T(8,128)S(1)} %collective-permute-done.2.l0, s32[17]{0:T(128)S(1)} %fusion.s1, ...), custom_call_target="tpu_custom_call", output_to_operand_aliasing={{3}: (8, {})} | custom-call | flops 8000000000 | bytes 4000000 | tf_op jit(solution)/shard_map/pallas_call | solution.py:351
  102.8 7.2 %shard_map.97 = (f32[5,64,256]{2,1,0:T(8,128)S(1)}, f32[5,64,256]{2,1,0:T(8,128)S(1)}, f32[6,48,256]{2,1,0:T(8,128)}, f32[2,3,256,256]{3,2,1,0:T(8,128)}) custom-call(s32[17]{0:T(128)S(1)} %fusion.1.s0, f32[904,128]{1,0:T(8,128)S(1)} %collective-permute-done.2.l0, s32[17]{0:T(128)S(1)} %fusion.s1, ...), custom_call_target="tpu_custom_call", output_to_operand_aliasing={{3}: (8, {})} | custom-call | flops 8000000000 | bytes 4000000 | tf_op jit(solution)/shard_map/pallas_call | solution.py:351
  109.9 0.1 collective-permute-start.7
  110.0 0.1 collective-permute-start.4
  110.1 5.3 %collective-permute-start.8 = (f32[5,48,256]{2,1,0:T(8,128)S(1)}, f32[5,48,256]{2,1,0:T(8,128)S(1)}, u32[]{:S(2)}, u32[]{:S(2)}) collective-permute-start(f32[5,48,256]{2,1,0:T(8,128)S(1)} %get-tuple-element.73), channel_id=1, source_target_pairs={{0,31},{1,0},{2,1},{3,2},{4,3},{5,4},{6,5},{7,6},{8,7},{9,8},{10,9... | collective-permute-start | bytes 737288 | tf_op jit(solution)/shard_map/ppermute | solution.py:41
  115.4 0.0 collective-permute-start.5
  115.4 5.3 %collective-permute-start.9 = (f32[5,80,256]{2,1,0:T(8,128)S(1)}, f32[5,80,256]{2,1,0:T(8,128)S(1)}, u32[]{:S(2)}, u32[]{:S(2)}) collective-permute-start(f32[5,80,256]{2,1,0:T(8,128)S(1)} %get-tuple-element.74), channel_id=1, source_target_pairs={{0,31},{1,0},{2,1},{3,2},{4,3},{5,4},{6,5},{7,6},{8,7},{9,8},{10,9... | collective-permute-start | bytes 1228808 | tf_op jit(solution)/shard_map/ppermute | solution.py:41
  120.7 20.6 %collective-permute-done.4.refs_1_ = f32[5,48,256]{2,1,0:T(8,128)S(1)} collective-permute-done((f32[5,48,256]{2,1,0:T(8,128)S(1)}, f32[5,48,256]{2,1,0:T(8,128)S(1)}, u32[]{:S(2)}, u32[]{:S(2)}) %collective-permute-start.4) | collective-permute-done | bytes 245792 | tf_op jit(solution)/shard_map/ppermute | solution.py:41
  141.4 0.0 collective-permute-start.11
  141.4 0.0 collective-permute-done.8.refs_5_
  141.4 2.5 %collective-permute-start.6 = (f32[5,64,256]{2,1,0:T(8,128)S(1)}, f32[5,64,256]{2,1,0:T(8,128)S(1)}, u32[]{:S(2)}, u32[]{:S(2)}) collective-permute-start(f32[5,64,256]{2,1,0:T(8,128)S(1)} %get-tuple-element.71), channel_id=1, source_target_pairs={{0,1},{1,2},{2,3},{3,4},{4,5},{5,6},{6,7},{7,8},{8,9},{9,10},{10,1... | collective-permute-start | bytes 983048 | tf_op jit(solution)/shard_map/ppermute | solution.py:41
  143.9 0.0 collective-permute-done.7.refs_4_
  143.9 2.9 %collective-permute-start.10 = (f32[5,64,256]{2,1,0:T(8,128)S(1)}, f32[5,64,256]{2,1,0:T(8,128)S(1)}, u32[]{:S(2)}, u32[]{:S(2)}) collective-permute-start(f32[5,64,256]{2,1,0:T(8,128)S(1)} %get-tuple-element.75), channel_id=1, source_target_pairs={{0,31},{1,0},{2,1},{3,2},{4,3},{5,4},{6,5},{7,6},{8,7},{9,8},{10,9... | collective-permute-start | bytes 983048 | tf_op jit(solution)/shard_map/ppermute | solution.py:41
  146.7 1.4 copy-done
  148.1 10.2 %interior.1.refs_0_ = f32[2,19,256,256]{3,2,1,0:T(8,128)} custom-call(f32[2,19,256,256]{3,2,1,0:T(8,128)S(1)} %bitcast.43, f32[2,3,256,256]{3,2,1,0:T(8,128)S(1)} %copy-done), custom_call_target="tpu_custom_call" | custom-call | bytes 25000000 | tf_op jit(solution)/shard_map/interior/pallas_call | solution.py:472
  158.3 1.3 collective-permute-done.11.refs_8_
  159.6 0.9 collective-permute-done.6.refs_3_
  160.5 3.4 %collective-permute-done.10.refs_7_ = f32[5,64,256]{2,1,0:T(8,128)S(1)} collective-permute-done((f32[5,64,256]{2,1,0:T(8,128)S(1)}, f32[5,64,256]{2,1,0:T(8,128)S(1)}, u32[]{:S(2)}, u32[]{:S(2)}) %collective-permute-start.10) | collective-permute-done | bytes 327712 | tf_op jit(solution)/shard_map/ppermute | solution.py:41
  163.9 0.0 collective-permute-done.5.refs_2_
  163.9 0.0 collective-permute-done.9.refs_6_
  163.9 1.5 arrivals.1
  (24 shorter events, 0.1 us)
Async XLA Ops:
  1.4 8.5 %collective-permute-start.1 = (f32[3,2,2,128]{3,2,1,0:T(2,128)S(1)}, f32[3,2,2,128]{3,2,1,0:T(2,128)S(1)}, u32[]{:S(2)}, u32[]{:S(2)}) collective-permute-start(f32[3,2,2,128]{3,2,1,0:T(2,128)S(1)} %get-tuple-element.86), channel_id=1, source_target_pairs={{1,0},{2,1},{3,2},{4,3},{5,4},{6,5},{7,6},{9,8},{10,9},{11,10},{12... | collective-permute-start | bytes 18440 | tf_op jit(solution)/shard_map/ppermute | solution.py:50
  2.7 7.2 %collective-permute-start = (f32[3,2,2,128]{3,2,1,0:T(2,128)S(1)}, f32[3,2,2,128]{3,2,1,0:T(2,128)S(1)}, u32[]{:S(2)}, u32[]{:S(2)}) collective-permute-start(f32[3,2,2,128]{3,2,1,0:T(2,128)S(1)} %get-tuple-element.87), channel_id=1, source_target_pairs={{0,1},{1,2},{2,3},{3,4},{4,5},{5,6},{6,7},{8,9},{9,10},{10,11},{11... | collective-permute-start | bytes 18440 | tf_op jit(solution)/shard_map/ppermute | solution.py:50
  9.9 0.6 copy-start.1
  10.5 0.6 copy-start.2
  54.8 22.4 %slice-start = ((s8[9961472]{0:T(1024)(128)(4,1)}), s8[4194304]{0:T(1024)(128)(4,1)S(1)}, s32[]{:S(2)}) async-start(s8[9961472]{0:T(1024)(128)(4,1)} %bitcast.42), calls=%async_computation | async-start | bytes 8388608
  54.8 22.4 %slice-start.1 = ((s8[9961472]{0:T(1024)(128)(4,1)}), s8[4194304]{0:T(1024)(128)(4,1)S(1)}, s32[]{:S(2)}) async-start(s8[9961472]{0:T(1024)(128)(4,1)} %bitcast.42), calls=%async_computation.1 | async-start | bytes 8388608
  54.8 22.4 %slice-start.2 = ((s8[9961472]{0:T(1024)(128)(4,1)}), s8[1572864]{0:T(1024)(128)(4,1)S(1)}, s32[]{:S(2)}) async-start(s8[9961472]{0:T(1024)(128)(4,1)} %bitcast.42), calls=%async_computation.2 | async-start | bytes 3145728
  54.8 22.3 %collective-permute-start.3 = (f32[904,128]{1,0:T(8,128)S(1)}, f32[904,128]{1,0:T(8,128)S(1)}, u32[]{:S(2)}, u32[]{:S(2)}) collective-permute-start(f32[904,128]{1,0:T(8,128)S(1)} %constant_dynamic-update-slice_fusion.list_ref), channel_id=1, source_target_pairs={{0,31},{1,0},{2,1},{3,2},{4,3},{5,4},{6,5},{7,6},{8,7},{9,8},{10,9... | collective-permute-start | bytes 1388552 | tf_op jit(solution)/shard_map/ppermute | solution.py:41
  58.3 18.9 %collective-permute-start.2 = (f32[904,128]{1,0:T(8,128)S(1)}, f32[904,128]{1,0:T(8,128)S(1)}, u32[]{:S(2)}, u32[]{:S(2)}) collective-permute-start(f32[904,128]{1,0:T(8,128)S(1)} %constant_dynamic-update-slice_fusion.list_ref), channel_id=1, source_target_pairs={{0,1},{1,2},{2,3},{3,4},{4,5},{5,6},{6,7},{7,8},{8,9},{9,10},{10,1... | collective-permute-start | bytes 1388552 | tf_op jit(solution)/shard_map/ppermute | solution.py:41
  109.9 33.9 %collective-permute-start.7 = (f32[5,64,256]{2,1,0:T(8,128)S(1)}, f32[5,64,256]{2,1,0:T(8,128)S(1)}, u32[]{:S(2)}, u32[]{:S(2)}) collective-permute-start(f32[5,64,256]{2,1,0:T(8,128)S(1)} %get-tuple-element.72), channel_id=1, source_target_pairs={{0,1},{1,2},{2,3},{3,4},{4,5},{5,6},{6,7},{7,8},{8,9},{9,10},{10,1... | collective-permute-start | bytes 983048 | tf_op jit(solution)/shard_map/ppermute | solution.py:41
  110.0 31.4 %collective-permute-start.4 = (f32[5,48,256]{2,1,0:T(8,128)S(1)}, f32[5,48,256]{2,1,0:T(8,128)S(1)}, u32[]{:S(2)}, u32[]{:S(2)}) collective-permute-start(f32[5,48,256]{2,1,0:T(8,128)S(1)} %get-tuple-element.69), channel_id=1, source_target_pairs={{0,1},{1,2},{2,3},{3,4},{4,5},{5,6},{6,7},{7,8},{8,9},{9,10},{10,1... | collective-permute-start | bytes 737288 | tf_op jit(solution)/shard_map/ppermute | solution.py:41
  110.1 31.3 %collective-permute-start.8 = (f32[5,48,256]{2,1,0:T(8,128)S(1)}, f32[5,48,256]{2,1,0:T(8,128)S(1)}, u32[]{:S(2)}, u32[]{:S(2)}) collective-permute-start(f32[5,48,256]{2,1,0:T(8,128)S(1)} %get-tuple-element.73), channel_id=1, source_target_pairs={{0,31},{1,0},{2,1},{3,2},{4,3},{5,4},{6,5},{7,6},{8,7},{9,8},{10,9... | collective-permute-start | bytes 737288 | tf_op jit(solution)/shard_map/ppermute | solution.py:41
  115.4 48.5 %collective-permute-start.5 = (f32[5,80,256]{2,1,0:T(8,128)S(1)}, f32[5,80,256]{2,1,0:T(8,128)S(1)}, u32[]{:S(2)}, u32[]{:S(2)}) collective-permute-start(f32[5,80,256]{2,1,0:T(8,128)S(1)} %get-tuple-element.70), channel_id=1, source_target_pairs={{0,1},{1,2},{2,3},{3,4},{4,5},{5,6},{6,7},{7,8},{8,9},{9,10},{10,1... | collective-permute-start | bytes 1228808 | tf_op jit(solution)/shard_map/ppermute | solution.py:41
  115.4 48.5 %collective-permute-start.9 = (f32[5,80,256]{2,1,0:T(8,128)S(1)}, f32[5,80,256]{2,1,0:T(8,128)S(1)}, u32[]{:S(2)}, u32[]{:S(2)}) collective-permute-start(f32[5,80,256]{2,1,0:T(8,128)S(1)} %get-tuple-element.74), channel_id=1, source_target_pairs={{0,31},{1,0},{2,1},{3,2},{4,3},{5,4},{6,5},{7,6},{8,7},{9,8},{10,9... | collective-permute-start | bytes 1228808 | tf_op jit(solution)/shard_map/ppermute | solution.py:41
  141.4 18.2 %collective-permute-start.11 = (f32[5,64,256]{2,1,0:T(8,128)S(1)}, f32[5,64,256]{2,1,0:T(8,128)S(1)}, u32[]{:S(2)}, u32[]{:S(2)}) collective-permute-start(f32[5,64,256]{2,1,0:T(8,128)S(1)} %get-tuple-element.76), channel_id=1, source_target_pairs={{0,31},{1,0},{2,1},{3,2},{4,3},{5,4},{6,5},{7,6},{8,7},{9,8},{10,9... | collective-permute-start | bytes 983048 | tf_op jit(solution)/shard_map/ppermute | solution.py:41
  141.4 19.1 %collective-permute-start.6 = (f32[5,64,256]{2,1,0:T(8,128)S(1)}, f32[5,64,256]{2,1,0:T(8,128)S(1)}, u32[]{:S(2)}, u32[]{:S(2)}) collective-permute-start(f32[5,64,256]{2,1,0:T(8,128)S(1)} %get-tuple-element.71), channel_id=1, source_target_pairs={{0,1},{1,2},{2,3},{3,4},{4,5},{5,6},{6,7},{7,8},{8,9},{9,10},{10,1... | collective-permute-start | bytes 983048 | tf_op jit(solution)/shard_map/ppermute | solution.py:41
  143.9 20.1 %collective-permute-start.10 = (f32[5,64,256]{2,1,0:T(8,128)S(1)}, f32[5,64,256]{2,1,0:T(8,128)S(1)}, u32[]{:S(2)}, u32[]{:S(2)}) collective-permute-start(f32[5,64,256]{2,1,0:T(8,128)S(1)} %get-tuple-element.75), channel_id=1, source_target_pairs={{0,31},{1,0},{2,1},{3,2},{4,3},{5,4},{6,5},{7,6},{8,7},{9,8},{10,9... | collective-permute-start | bytes 983048 | tf_op jit(solution)/shard_map/ppermute | solution.py:41
  146.7 1.4 copy-start

commit v6 on v5

--- a/solution.py
+++ b/solution.py
@@ -703,6 +703,7 @@
 
 
 CUTS = (0, 4, 9, 13, 16)
+OFFSET_BITS = (16, 16, 14)
 
 
 def one_step(displacement, tension, bending, offset, owner, cell, populations):
@@ -719,10 +720,31 @@
     key = got[0].astype(jnp.int32)
     bounds = jnp.arange(windows + 1, dtype=jnp.int32) * (WINDOW << x_bit)
     starts = jnp.sum((key[None, :] < bounds[:, None]).astype(jnp.float32), 1)
+    fixed = [
+        jnp.floor(v * (2.0**n - 1.0) + 0.5).astype(jnp.int32)
+        for v, n in zip(got[4:], OFFSET_BITS)
+    ]
+    top = width << x_bit
     ordered = lax.sort(
-        (key,) + tuple(got[1:]), num_keys=1, is_stable=False
+        (
+            ((key - top) << OFFSET_BITS[2]) + fixed[2],
+            ((fixed[0] - (1 << 15)) << OFFSET_BITS[1]) + fixed[1],
+        )
+        + tuple(got[1:4]),
+        num_keys=1,
+        is_stable=False,
     )
-    columns = list(ordered[1:]) + [ordered[0].astype(jnp.float32)]
+    code = (ordered[0] >> OFFSET_BITS[2]) + top
+    fixed = [
+        (ordered[1] >> OFFSET_BITS[1]) + (1 << 15),
+        ordered[1] & ((1 << OFFSET_BITS[1]) - 1),
+        ordered[0] & ((1 << OFFSET_BITS[2]) - 1),
+    ]
+    columns = (
+        list(ordered[2:])
+        + [v.astype(jnp.float32) * (1.0 / (2.0**n - 1.0)) for v, n in zip(fixed, OFFSET_BITS)]
+        + [code.astype(jnp.float32)]
+    )
     starts = jnp.pad(starts, (0, LANES - windows - 1))
     listed = jnp.concatenate(
         [v.reshape(-1, LANES) for v in columns]

time: 166 us -> 163 us (0.982)
  other arithmetic: 22.4 us -> 19.2 us
    sort x1, other arithmetic: 13.3 us -> 10 us  [one_step(): lax.sort(((key - top << OFFSET_BITS[2]) + fixed[2], (fixed[0] - (1 << 15)...]
  transfers between devices with their start and end apart: 12 -> 12, of which waited for: 5 -> 5; matrix products, arithmetic and copies ran while one was open for 1% -> 1% of each run, Pallas kernels for 9% -> 10%
where the time goes in v6:
time: 163 us
  Pallas kernels  72.9 us (45%)
  waiting for transfers between devices  39.7 us (24%)
  starting transfers between devices  26.4 us (16%)
  other arithmetic  19.2 us (12%)
  local copies, waits for them, and re-layouts  3.45 us (2%)
    ppermute x10, waiting for transfers between devices, passed_along(): return lax.ppermute(value, axis, pairs)  39.7 us
    pallas_call x4, Pallas kernels, spread_chunk(): pl.pallas_call(kernel, out_shape=(shape((5, n, width), jnp.float32), shap...  32.8 us
    ppermute x10, starting transfers between devices, passed_along(): return lax.ppermute(value, axis, pairs)  19.6 us
    pallas_call x1, Pallas kernels, exchanged(): pl.pallas_call(kernel, out_shape=jax.ShapeDtypeStruct(send.shape, send.dt...  19.3 us
    pallas_call x1, Pallas kernels, interior(): pl.pallas_call(kernel, out_shape=jax.ShapeDtypeStruct(populations.shape,...  10.2 us
    sort x1, other arithmetic, one_step(): lax.sort(((key - top << OFFSET_BITS[2]) + fixed[2], (fixed[0] - (1 << 15)...  10 us
    sort x1, other arithmetic, dispatched(): lax.sort((key.reshape(-1),) + tuple((v.reshape(-1) for v in values)), num...  6.91 us
    ppermute x2, starting transfers between devices, halos(): return (lax.ppermute(last, axis, up), lax.ppermute(initial, axis, down))  6.81 us
  transfers between devices with their start and end apart: 12, of which 5 were waited for; matrix products, arithmetic and copies ran while one was open for 1% of the time, Pallas kernels for 10%

profile of v6, /device:TPU:0, one launch (start us, length us, event | category | flops | bytes accessed | tf_op | source)
XLA Modules:
  0.0 162.8 jit_solution(570372134900951826)
XLA Ops:
  0.6 0.8 fusion.4
  1.4 1.3 collective-permute-start.1
  2.7 5.5 %collective-permute-start = (f32[3,2,2,128]{3,2,1,0:T(2,128)S(1)}, f32[3,2,2,128]{3,2,1,0:T(2,128)S(1)}, u32[]{:S(2)}, u32[]{:S(2)}) collective-permute-start(f32[3,2,2,128]{3,2,1,0:T(2,128)S(1)} %get-tuple-element.81), channel_id=1, source_target_pairs={{0,1},{1,2},{2,3},{3,4},{4,5},{5,6},{6,7},{8,9},{9,10},{10,11},{11... | collective-permute-start | bytes 18440 | tf_op jit(solution)/shard_map/ppermute | solution.py:50
  8.2 1.0 convert_reduce_fusion.1.start_ref
  9.2 0.6 pad_add_fusion.edge
  9.9 0.0 collective-permute-done.1.after_ref
  9.9 0.0 collective-permute-done.before_ref
  9.9 0.6 copy-done.1
  10.5 0.6 copy-done.2
  11.1 1.9 %prepared.1 = (f32[3,2,32,128]{3,2,1,0:T(8,128)}, s32[64,128]{1,0:T(8,128)}, f32[64,128]{1,0:T(8,128)}, f32[64,128]{1,0:T(8,128)}, f32[64,128]{1,0:T(8,128)}, /*...) custom-call(s32[2]{0:T(128)} %pad_add_fusion.edge, f32[2]{0:T(128)} %t_ref.1, f32[2]{0:T(128)} %b_ref.1, ...), custom_call_target="tpu_custom_call" | custom-call | tf_op jit(solution)/shard_map/prepared/pallas_call | solution.py:579
  12.9 6.9 %sort.78 = (s32[8192]{0:T(1024)S(1)}, f32[8192]{0:T(1024)S(1)}, f32[8192]{0:T(1024)S(1)}, f32[8192]{0:T(1024)S(1)}, f32[8192]{0:T(1024)S(1)}, /*index=5*/f32[8192]{0:T(1024)S(1)}, f32[8192]{0:T(1024)S(1)}) sort(s32[8192]{0:T(1024)} %bitcast.58, f32[8192]{0:T(1024)} %bitcast.59, f32[8192]{0:T(1024)} %bitcast.60, f32[8192]{0:T(1024)} %bitcast.61, ...), dimensions={0}, to_apply=%region_1.2 | sort | flops 106496 | bytes 458752 | tf_op jit(solution)/shard_map/sort | solution.py:696
  19.8 1.9 %packed.1.send_ref = f32[32,7,4,128]{3,2,1,0:T(4,128)S(1)} custom-call(s32[32]{0:T(128)S(1)} %convert_reduce_fusion.1.start_ref, s32[64,128]{1,0:T(8,128)S(1)} %bitcast.43, f32[64,128]{1,0:T(8,128)S(1)} %bitcast.44, f32[64,128]{1,0:T(8,128)S(1)} %bitcast.45, f32[64,128]{1,0:T(8,128)S(1)} %bitcast.46, f32[64,128]{1,0:T(8,128)S(1)} %bitcast.47, ...), custom_call_target="tpu_custom_call" | custom-call | tf_op jit(solution)/shard_map/packed/pallas_call | solution.py:617
  21.7 19.3 %exchanged.1 = f32[32,7,4,128]{3,2,1,0:T(4,128)S(1)} custom-call(f32[32,7,4,128]{3,2,1,0:T(4,128)S(1)} %packed.1.send_ref), custom_call_target="tpu_custom_call" | custom-call | tf_op jit(solution)/shard_map/exchanged/pallas_call | solution.py:675
  41.0 0.1 shift-left_add_fusion
  41.1 0.1 fusion.2
  41.1 0.4 convert_reduce_fusion
  41.6 10.0 %sort.79 = (s32[16384]{0:T(1024)S(1)}, s32[16384]{0:T(1024)S(1)}, f32[16384]{0:T(1024)S(1)}, f32[16384]{0:T(1024)S(1)}, f32[16384]{0:T(1024)S(1)}) sort(s32[16384]{0:T(1024)S(1)} %shift-left_add_fusion.1, s32[16384]{0:T(1024)S(1)} %bitcast.52, f32[16384]{0:T(1024)S(1)} %bitcast.55, f32[16384]{0:T(1024)S(1)} %bitcast.54, f32[16384]{0:T(1024)S(1)} %bitcast.53), dimensions={0}, to_apply=%region_2.3 | sort | flops 229376 | bytes 655360 | tf_op jit(solution)/shard_map/sort | solution.py:728
  51.7 0.0 slice-start
  51.8 0.0 slice-start.1
  51.8 0.0 slice-start.2
  51.8 3.5 %collective-permute-start.3 = (f32[904,128]{1,0:T(8,128)S(1)}, f32[904,128]{1,0:T(8,128)S(1)}, u32[]{:S(2)}, u32[]{:S(2)}) collective-permute-start(f32[904,128]{1,0:T(8,128)S(1)} %constant_dynamic-update-slice_fusion.list_ref), channel_id=1, source_target_pairs={{0,31},{1,0},{2,1},{3,2},{4,3},{5,4},{6,5},{7,6},{8,7},{9,8},{10,9... | collective-permute-start | bytes 1388552 | tf_op jit(solution)/shard_map/ppermute | solution.py:41
  55.3 0.0 collective-permute-start.2
  55.3 5.4 %spread_own.1.total_ref = f32[6,264,256]{2,1,0:T(8,128)S(1)} custom-call(s32[17]{0:T(128)S(1)} %convert_element_type.85.starts, f32[904,128]{1,0:T(8,128)S(1)} %constant_dynamic-update-slice_fusion.list_ref), custom_call_target="tpu_custom_call" | custom-call | flops 20000000000 | bytes 4000000 | tf_op jit(solution)/shard_map/spread_own/pallas_call | solution.py:196
  60.6 13.5 %collective-permute-done.3.l1 = f32[904,128]{1,0:T(8,128)S(1)} collective-permute-done((f32[904,128]{1,0:T(8,128)S(1)}, f32[904,128]{1,0:T(8,128)S(1)}, u32[]{:S(2)}, u32[]{:S(2)}) %collective-permute-start.3) | collective-permute-done | bytes 462880 | tf_op jit(solution)/shard_map/ppermute | solution.py:41
  74.1 0.0 collective-permute-done.2.l0
  74.2 7.3 %shard_map.94 = (f32[5,48,256]{2,1,0:T(8,128)S(1)}, f32[5,48,256]{2,1,0:T(8,128)S(1)}, f32[6,48,256]{2,1,0:T(8,128)S(1)}, f32[2,3,256,256]{3,2,1,0:T(8,128)}) custom-call(s32[17]{0:T(128)S(1)} %fusion.1.s0, f32[904,128]{1,0:T(8,128)S(1)} %collective-permute-done.2.l0, s32[17]{0:T(128)S(1)} %fusion.s1, f32[904,128]{1,0:T(8,128)S(1)} %collective-permute-done.3.l1, ...), custom_call_target="tpu_custom_call" | custom-call | flops 8000000000 | bytes 4000000 | tf_op jit(solution)/shard_map/pallas_call | solution.py:351
  81.6 10.0 %shard_map.95 = (f32[5,80,256]{2,1,0:T(8,128)S(1)}, f32[5,80,256]{2,1,0:T(8,128)S(1)}, f32[6,48,256]{2,1,0:T(8,128)S(1)}, f32[2,3,256,256]{3,2,1,0:T(8,128)}) custom-call(s32[17]{0:T(128)S(1)} %fusion.1.s0, f32[904,128]{1,0:T(8,128)S(1)} %collective-permute-done.2.l0, s32[17]{0:T(128)S(1)} %fusion.s1, ...), custom_call_target="tpu_custom_call", output_to_operand_aliasing={{3}: (8, {})} | custom-call | flops 8000000000 | bytes 4000000 | tf_op jit(solution)/shard_map/pallas_call | solution.py:351
  91.6 8.4 %shard_map.96 = (f32[5,64,256]{2,1,0:T(8,128)S(1)}, f32[5,64,256]{2,1,0:T(8,128)S(1)}, f32[6,48,256]{2,1,0:T(8,128)S(1)}, f32[2,3,256,256]{3,2,1,0:T(8,128)}) custom-call(s32[17]{0:T(128)S(1)} %fusion.1.s0, f32[904,128]{1,0:T(8,128)S(1)} %collective-permute-done.2.l0, s32[17]{0:T(128)S(1)} %fusion.s1, ...), custom_call_target="tpu_custom_call", output_to_operand_aliasing={{3}: (8, {})} | custom-call | flops 8000000000 | bytes 4000000 | tf_op jit(solution)/shard_map/pallas_call | solution.py:351
  100.0 7.2 %shard_map.97 = (f32[5,64,256]{2,1,0:T(8,128)S(1)}, f32[5,64,256]{2,1,0:T(8,128)S(1)}, f32[6,48,256]{2,1,0:T(8,128)}, f32[2,3,256,256]{3,2,1,0:T(8,128)}) custom-call(s32[17]{0:T(128)S(1)} %fusion.1.s0, f32[904,128]{1,0:T(8,128)S(1)} %collective-permute-done.2.l0, s32[17]{0:T(128)S(1)} %fusion.s1, ...), custom_call_target="tpu_custom_call", output_to_operand_aliasing={{3}: (8, {})} | custom-call | flops 8000000000 | bytes 4000000 | tf_op jit(solution)/shard_map/pallas_call | solution.py:351
  107.1 0.1 collective-permute-start.7
  107.2 0.1 collective-permute-start.4
  107.3 5.3 %collective-permute-start.8 = (f32[5,48,256]{2,1,0:T(8,128)S(1)}, f32[5,48,256]{2,1,0:T(8,128)S(1)}, u32[]{:S(2)}, u32[]{:S(2)}) collective-permute-start(f32[5,48,256]{2,1,0:T(8,128)S(1)} %get-tuple-element.69), channel_id=1, source_target_pairs={{0,31},{1,0},{2,1},{3,2},{4,3},{5,4},{6,5},{7,6},{8,7},{9,8},{10,9... | collective-permute-start | bytes 737288 | tf_op jit(solution)/shard_map/ppermute | solution.py:41
  112.6 0.0 collective-permute-start.5
  112.6 5.3 %collective-permute-start.9 = (f32[5,80,256]{2,1,0:T(8,128)S(1)}, f32[5,80,256]{2,1,0:T(8,128)S(1)}, u32[]{:S(2)}, u32[]{:S(2)}) collective-permute-start(f32[5,80,256]{2,1,0:T(8,128)S(1)} %get-tuple-element.70), channel_id=1, source_target_pairs={{0,31},{1,0},{2,1},{3,2},{4,3},{5,4},{6,5},{7,6},{8,7},{9,8},{10,9... | collective-permute-start | bytes 1228808 | tf_op jit(solution)/shard_map/ppermute | solution.py:41
  117.9 20.6 %collective-permute-done.4.refs_1_ = f32[5,48,256]{2,1,0:T(8,128)S(1)} collective-permute-done((f32[5,48,256]{2,1,0:T(8,128)S(1)}, f32[5,48,256]{2,1,0:T(8,128)S(1)}, u32[]{:S(2)}, u32[]{:S(2)}) %collective-permute-start.4) | collective-permute-done | bytes 245792 | tf_op jit(solution)/shard_map/ppermute | solution.py:41
  138.5 0.0 collective-permute-start.11
  138.5 0.0 collective-permute-done.8.refs_5_
  138.5 2.5 %collective-permute-start.6 = (f32[5,64,256]{2,1,0:T(8,128)S(1)}, f32[5,64,256]{2,1,0:T(8,128)S(1)}, u32[]{:S(2)}, u32[]{:S(2)}) collective-permute-start(f32[5,64,256]{2,1,0:T(8,128)S(1)} %get-tuple-element.67), channel_id=1, source_target_pairs={{0,1},{1,2},{2,3},{3,4},{4,5},{5,6},{6,7},{7,8},{8,9},{9,10},{10,1... | collective-permute-start | bytes 983048 | tf_op jit(solution)/shard_map/ppermute | solution.py:41
  141.0 0.0 collective-permute-done.7.refs_4_
  141.0 2.9 %collective-permute-start.10 = (f32[5,64,256]{2,1,0:T(8,128)S(1)}, f32[5,64,256]{2,1,0:T(8,128)S(1)}, u32[]{:S(2)}, u32[]{:S(2)}) collective-permute-start(f32[5,64,256]{2,1,0:T(8,128)S(1)} %get-tuple-element.71), channel_id=1, source_target_pairs={{0,31},{1,0},{2,1},{3,2},{4,3},{5,4},{6,5},{7,6},{8,7},{9,8},{10,9... | collective-permute-start | bytes 983048 | tf_op jit(solution)/shard_map/ppermute | solution.py:41
  143.9 1.4 copy-done
  145.3 10.2 %interior.1.refs_0_ = f32[2,19,256,256]{3,2,1,0:T(8,128)} custom-call(f32[2,19,256,256]{3,2,1,0:T(8,128)S(1)} %bitcast.42, f32[2,3,256,256]{3,2,1,0:T(8,128)S(1)} %copy-done), custom_call_target="tpu_custom_call" | custom-call | bytes 25000000 | tf_op jit(solution)/shard_map/interior/pallas_call | solution.py:472
  155.5 1.3 collective-permute-done.11.refs_8_
  156.8 0.9 collective-permute-done.6.refs_3_
  157.7 3.4 %collective-permute-done.10.refs_7_ = f32[5,64,256]{2,1,0:T(8,128)S(1)} collective-permute-done((f32[5,64,256]{2,1,0:T(8,128)S(1)}, f32[5,64,256]{2,1,0:T(8,128)S(1)}, u32[]{:S(2)}, u32[]{:S(2)}) %collective-permute-start.10) | collective-permute-done | bytes 327712 | tf_op jit(solution)/shard_map/ppermute | solution.py:41
  161.1 0.0 collective-permute-done.5.refs_2_
  161.1 0.0 collective-permute-done.9.refs_6_
  161.1 1.5 arrivals.1
  (26 shorter events, 0.2 us)
Async XLA Ops:
  1.4 8.5 %collective-permute-start.1 = (f32[3,2,2,128]{3,2,1,0:T(2,128)S(1)}, f32[3,2,2,128]{3,2,1,0:T(2,128)S(1)}, u32[]{:S(2)}, u32[]{:S(2)}) collective-permute-start(f32[3,2,2,128]{3,2,1,0:T(2,128)S(1)} %get-tuple-element.80), channel_id=1, source_target_pairs={{1,0},{2,1},{3,2},{4,3},{5,4},{6,5},{7,6},{9,8},{10,9},{11,10},{12... | collective-permute-start | bytes 18440 | tf_op jit(solution)/shard_map/ppermute | solution.py:50
  2.7 7.2 %collective-permute-start = (f32[3,2,2,128]{3,2,1,0:T(2,128)S(1)}, f32[3,2,2,128]{3,2,1,0:T(2,128)S(1)}, u32[]{:S(2)}, u32[]{:S(2)}) collective-permute-start(f32[3,2,2,128]{3,2,1,0:T(2,128)S(1)} %get-tuple-element.81), channel_id=1, source_target_pairs={{0,1},{1,2},{2,3},{3,4},{4,5},{5,6},{6,7},{8,9},{9,10},{10,11},{11... | collective-permute-start | bytes 18440 | tf_op jit(solution)/shard_map/ppermute | solution.py:50
  9.9 0.6 copy-start.1
  10.5 0.6 copy-start.2
  51.7 22.4 %slice-start = ((s8[9961472]{0:T(1024)(128)(4,1)}), s8[4194304]{0:T(1024)(128)(4,1)S(1)}, s32[]{:S(2)}) async-start(s8[9961472]{0:T(1024)(128)(4,1)} %bitcast.41), calls=%async_computation | async-start | bytes 8388608
  51.8 22.4 %slice-start.1 = ((s8[9961472]{0:T(1024)(128)(4,1)}), s8[4194304]{0:T(1024)(128)(4,1)S(1)}, s32[]{:S(2)}) async-start(s8[9961472]{0:T(1024)(128)(4,1)} %bitcast.41), calls=%async_computation.1 | async-start | bytes 8388608
  51.8 22.4 %slice-start.2 = ((s8[9961472]{0:T(1024)(128)(4,1)}), s8[1572864]{0:T(1024)(128)(4,1)S(1)}, s32[]{:S(2)}) async-start(s8[9961472]{0:T(1024)(128)(4,1)} %bitcast.41), calls=%async_computation.2 | async-start | bytes 3145728
  51.8 22.3 %collective-permute-start.3 = (f32[904,128]{1,0:T(8,128)S(1)}, f32[904,128]{1,0:T(8,128)S(1)}, u32[]{:S(2)}, u32[]{:S(2)}) collective-permute-start(f32[904,128]{1,0:T(8,128)S(1)} %constant_dynamic-update-slice_fusion.list_ref), channel_id=1, source_target_pairs={{0,31},{1,0},{2,1},{3,2},{4,3},{5,4},{6,5},{7,6},{8,7},{9,8},{10,9... | collective-permute-start | bytes 1388552 | tf_op jit(solution)/shard_map/ppermute | solution.py:41
  55.3 18.9 %collective-permute-start.2 = (f32[904,128]{1,0:T(8,128)S(1)}, f32[904,128]{1,0:T(8,128)S(1)}, u32[]{:S(2)}, u32[]{:S(2)}) collective-permute-start(f32[904,128]{1,0:T(8,128)S(1)} %constant_dynamic-update-slice_fusion.list_ref), channel_id=1, source_target_pairs={{0,1},{1,2},{2,3},{3,4},{4,5},{5,6},{6,7},{7,8},{8,9},{9,10},{10,1... | collective-permute-start | bytes 1388552 | tf_op jit(solution)/shard_map/ppermute | solution.py:41
  107.1 33.9 %collective-permute-start.7 = (f32[5,64,256]{2,1,0:T(8,128)S(1)}, f32[5,64,256]{2,1,0:T(8,128)S(1)}, u32[]{:S(2)}, u32[]{:S(2)}) collective-permute-start(f32[5,64,256]{2,1,0:T(8,128)S(1)} %get-tuple-element.68), channel_id=1, source_target_pairs={{0,1},{1,2},{2,3},{3,4},{4,5},{5,6},{6,7},{7,8},{8,9},{9,10},{10,1... | collective-permute-start | bytes 983048 | tf_op jit(solution)/shard_map/ppermute | solution.py:41
  107.2 31.3 %collective-permute-start.4 = (f32[5,48,256]{2,1,0:T(8,128)S(1)}, f32[5,48,256]{2,1,0:T(8,128)S(1)}, u32[]{:S(2)}, u32[]{:S(2)}) collective-permute-start(f32[5,48,256]{2,1,0:T(8,128)S(1)} %get-tuple-element.65), channel_id=1, source_target_pairs={{0,1},{1,2},{2,3},{3,4},{4,5},{5,6},{6,7},{7,8},{8,9},{9,10},{10,1... | collective-permute-start | bytes 737288 | tf_op jit(solution)/shard_map/ppermute | solution.py:41
  107.3 31.3 %collective-permute-start.8 = (f32[5,48,256]{2,1,0:T(8,128)S(1)}, f32[5,48,256]{2,1,0:T(8,128)S(1)}, u32[]{:S(2)}, u32[]{:S(2)}) collective-permute-start(f32[5,48,256]{2,1,0:T(8,128)S(1)} %get-tuple-element.69), channel_id=1, source_target_pairs={{0,31},{1,0},{2,1},{3,2},{4,3},{5,4},{6,5},{7,6},{8,7},{9,8},{10,9... | collective-permute-start | bytes 737288 | tf_op jit(solution)/shard_map/ppermute | solution.py:41
  112.6 48.5 %collective-permute-start.5 = (f32[5,80,256]{2,1,0:T(8,128)S(1)}, f32[5,80,256]{2,1,0:T(8,128)S(1)}, u32[]{:S(2)}, u32[]{:S(2)}) collective-permute-start(f32[5,80,256]{2,1,0:T(8,128)S(1)} %get-tuple-element.66), channel_id=1, source_target_pairs={{0,1},{1,2},{2,3},{3,4},{4,5},{5,6},{6,7},{7,8},{8,9},{9,10},{10,1... | collective-permute-start | bytes 1228808 | tf_op jit(solution)/shard_map/ppermute | solution.py:41
  112.6 48.5 %collective-permute-start.9 = (f32[5,80,256]{2,1,0:T(8,128)S(1)}, f32[5,80,256]{2,1,0:T(8,128)S(1)}, u32[]{:S(2)}, u32[]{:S(2)}) collective-permute-start(f32[5,80,256]{2,1,0:T(8,128)S(1)} %get-tuple-element.70), channel_id=1, source_target_pairs={{0,31},{1,0},{2,1},{3,2},{4,3},{5,4},{6,5},{7,6},{8,7},{9,8},{10,9... | collective-permute-start | bytes 1228808 | tf_op jit(solution)/shard_map/ppermute | solution.py:41
  138.5 18.2 %collective-permute-start.11 = (f32[5,64,256]{2,1,0:T(8,128)S(1)}, f32[5,64,256]{2,1,0:T(8,128)S(1)}, u32[]{:S(2)}, u32[]{:S(2)}) collective-permute-start(f32[5,64,256]{2,1,0:T(8,128)S(1)} %get-tuple-element.72), channel_id=1, source_target_pairs={{0,31},{1,0},{2,1},{3,2},{4,3},{5,4},{6,5},{7,6},{8,7},{9,8},{10,9... | collective-permute-start | bytes 983048 | tf_op jit(solution)/shard_map/ppermute | solution.py:41
  138.5 19.1 %collective-permute-start.6 = (f32[5,64,256]{2,1,0:T(8,128)S(1)}, f32[5,64,256]{2,1,0:T(8,128)S(1)}, u32[]{:S(2)}, u32[]{:S(2)}) collective-permute-start(f32[5,64,256]{2,1,0:T(8,128)S(1)} %get-tuple-element.67), channel_id=1, source_target_pairs={{0,1},{1,2},{2,3},{3,4},{4,5},{5,6},{6,7},{7,8},{8,9},{9,10},{10,1... | collective-permute-start | bytes 983048 | tf_op jit(solution)/shard_map/ppermute | solution.py:41
  141.0 20.1 %collective-permute-start.10 = (f32[5,64,256]{2,1,0:T(8,128)S(1)}, f32[5,64,256]{2,1,0:T(8,128)S(1)}, u32[]{:S(2)}, u32[]{:S(2)}) collective-permute-start(f32[5,64,256]{2,1,0:T(8,128)S(1)} %get-tuple-element.71), channel_id=1, source_target_pairs={{0,31},{1,0},{2,1},{3,2},{4,3},{5,4},{6,5},{7,6},{8,7},{9,8},{10,9... | collective-permute-start | bytes 983048 | tf_op jit(solution)/shard_map/ppermute | solution.py:41
  143.9 1.4 copy-start
